TPU v7x, 256 devices: a whole 4x4x8 slice. The times are simulated.
256 devices in a mesh: seq: 128 (over z, x_hi, y, core), head: 2 (over x_lo).
Axes of the slice: x: 4 (x_hi: 2, x_lo: 2; x = x_hi * 2 + x_lo), y: 4, z: 8, core: 2. Of those that a mesh axis runs over, the one named last changes fastest.
Arguments:
- query: bfloat16 [32768, 8, 4, 128], P('seq', None, 'head'), may hold values from -40 to 40
- key_in: bfloat16 [32768, 8, 128], P('seq', 'head'), may hold values from -16 to 16
- value: bfloat16 [32768, 8, 128], P('seq', 'head'), may hold values from -6 to 6
- grad_out: bfloat16 [32768, 8, 4, 128], P('seq', None, 'head'), may hold values from -6 to 6
- band_width: int32 [8, 4], P(None, 'head'), may hold values from 1 to 2, as said below
- stride_bits: int32 [7], replicated, may hold values from 0 to 6, each once
- partner_table: int32 [256, 7], P('seq'), may hold values from 0 to 1
Outputs:
- attn_out: bfloat16 [32768, 8, 4, 128], P('seq', None, 'head')
- grad_query: bfloat16 [32768, 8, 4, 128], P('seq', None, 'head')
- grad_key: bfloat16 [32768, 8, 128], P('seq', 'head')
- grad_value: bfloat16 [32768, 8, 128], P('seq', 'head')
Inputs may be any that keep to these rules, and one draw needn't show every extreme that they name: `band_width`: some query head has band width 1 and some has 2. `stride_bits`: each section flips a different bit.
All inputs are finite; a program needn't handle non-finite values.
Results may differ from a plain program's by a relative error of at most 0.023.
Values may be sent and summed in bfloat16 or wider, within the bound.
No kernel may reach another device: no remote copies, remote signals or barrier semaphores. Data moves between devices by JAX's collectives and lax.ppermute only.
A program may use at most 192 MiB of HBM per device.

v0:
```python
import jax
import jax.numpy as jnp
from jax import lax
from jax.sharding import PartitionSpec as P

BLOCK = 128
BANDMAX = 2


def from_behind(value, axis, steps):
    count = lax.axis_size(axis)
    initial, last = (max(0, -steps), min(count, count - steps))
    return lax.ppermute(value, axis, [(source, source + steps) for source in range(initial, last)])


def extended_2(block, sides, width):
    for axis, dim in sides:
        count = lax.axis_size(axis)
        forward = [(i, i + 1) for i in range(count - 1)]
        backward = [(target, source) for source, target in forward]
        low = lax.ppermute(
            lax.slice_in_dim(block, block.shape[dim] - width, None, axis=dim), axis, forward
        )
        high = lax.ppermute(lax.slice_in_dim(block, 0, width, axis=dim), axis, backward)
        block = jnp.concatenate([low, block, high], axis=dim)
    return block


def swapped(value, axis, distance):
    return lax.ppermute(value, axis, [(i, i ^ 1 << distance) for i in range(lax.axis_size(axis))])


def attend(query_block, grad_block, key_block, value_block, valid_keys, score_scale):
    scores = (
        jnp.einsum("qhgd,khd->hgqk", query_block, key_block, preferred_element_type=jnp.float32)
        * score_scale
    )
    scores = jnp.where(valid_keys[:, :, None, :], scores, -jnp.inf)
    row_max = jnp.max(scores, axis=-1, keepdims=True)
    log_total = row_max + jnp.log(jnp.sum(jnp.exp(scores - row_max), axis=-1, keepdims=True))
    probability = jnp.exp(scores - log_total)
    weights = probability.astype(jnp.bfloat16)
    output = jnp.einsum(
        "hgqk,khd->qhgd", weights, value_block, preferred_element_type=jnp.float32
    ).astype(jnp.bfloat16)
    row_delta = jnp.sum(grad_block.astype(jnp.float32) * output.astype(jnp.float32), axis=-1)
    grad_prob = jnp.einsum(
        "qhgd,khd->hgqk", grad_block, value_block, preferred_element_type=jnp.float32
    )
    grad_score = (
        probability * (grad_prob - jnp.transpose(row_delta, (1, 2, 0))[..., None])
    ).astype(jnp.bfloat16)
    grad_q = (
        jnp.einsum("hgqk,khd->qhgd", grad_score, key_block, preferred_element_type=jnp.float32)
        * score_scale
    ).astype(jnp.bfloat16)
    grad_k = (
        jnp.einsum("hgqk,qhgd->khd", grad_score, query_block, preferred_element_type=jnp.float32)
        * score_scale
    )
    grad_v = jnp.einsum("hgqk,qhgd->khd", weights, grad_block, preferred_element_type=jnp.float32)
    return (output, grad_q, grad_k, grad_v)


def fold_rims(extended, rim_rows):
    rows_dev = extended.shape[1] - 2 * rim_rows
    inner = extended[:, rim_rows : rim_rows + rows_dev]
    from_right = from_behind(extended[:, :rim_rows].astype(jnp.bfloat16), "seq", -1).astype(
        jnp.float32
    )
    from_left = from_behind(
        extended[:, rim_rows + rows_dev :].astype(jnp.bfloat16), "seq", 1
    ).astype(jnp.float32)
    inner = inner.at[:, rows_dev - rim_rows :].add(from_right)
    inner = inner.at[:, :rim_rows].add(from_left)
    return inner


def shards(query, key_in, value, grad_out, band_width, stride_bits, partner_table):
    rows_dev = key_in.shape[0]
    head_dim = key_in.shape[2]
    groups_local = query.shape[2]
    local_blocks = rows_dev // BLOCK
    half_band = BANDMAX - 1
    rim_rows = half_band * BLOCK
    span_blocks = 2 * half_band + 1
    levels = lax.axis_size("seq").bit_length() - 1
    all_blocks = local_blocks * lax.axis_size("seq")
    score_scale = head_dim ** (-0.5)
    device = lax.axis_index("seq")
    stacked = jnp.stack([key_in, value])
    all_heads = lax.all_gather(stacked, "head", axis=2, tiled=True)
    extended = extended_2(all_heads, (("seq", 1),), rim_rows)
    received = [swapped(all_heads, "seq", level_bit) for level_bit in range(levels)]
    kv_heads = extended.shape[2]
    band_keys = jnp.stack(
        [
            extended[:, block_num * BLOCK : block_num * BLOCK + span_blocks * BLOCK]
            for block_num in range(local_blocks)
        ],
        axis=0,
    )
    chosen_list = []
    partner_list = []
    for level_bit in range(levels):
        section_match = (stride_bits == level_bit).astype(jnp.int32)
        chosen = jnp.sum(partner_table * section_match[None, :], axis=1)
        chosen_list.append(chosen)
        arriving = received[level_bit].reshape(2, local_blocks, BLOCK, kv_heads, head_dim)
        partner_list.append(jnp.take(arriving, chosen, axis=1))
    partner_keys = jnp.stack(partner_list, axis=2)
    partner_keys = jnp.swapaxes(partner_keys, 0, 1).reshape(
        local_blocks, 2, levels * BLOCK, kv_heads, head_dim
    )
    key_pairs = jnp.concatenate([band_keys, partner_keys], axis=2)
    offsets = jnp.arange(-half_band, half_band + 1, dtype=jnp.int32)
    global_blocks = device * local_blocks + jnp.arange(local_blocks, dtype=jnp.int32)
    nearby = global_blocks[:, None] + offsets[None, :]
    edge_valid = (nearby >= 0) & (nearby < all_blocks)
    width_valid = jnp.abs(offsets)[None, None, :] < band_width[:, :, None]
    band_valid = edge_valid[:, None, None, :] & width_valid[None]
    valid_all = jnp.concatenate(
        [band_valid, jnp.ones((local_blocks, kv_heads, groups_local, levels), jnp.bool_)], axis=-1
    )
    valid_all = jnp.repeat(valid_all, BLOCK, axis=-1)
    query_blocks = query.reshape(local_blocks, BLOCK, kv_heads, groups_local, head_dim)
    grad_blocks = grad_out.reshape(local_blocks, BLOCK, kv_heads, groups_local, head_dim)
    head_step = min(kv_heads, 4)

    def one_block(block_items):
        query_block, grad_block, key_pair, valid_keys = block_items
        results = [
            attend(
                query_block[:, head_start : head_start + head_step],
                grad_block[:, head_start : head_start + head_step],
                key_pair[0][:, head_start : head_start + head_step],
                key_pair[1][:, head_start : head_start + head_step],
                valid_keys[head_start : head_start + head_step],
                score_scale,
            )
            for head_start in range(0, kv_heads, head_step)
        ]
        return tuple(
            (jnp.concatenate([result[member] for result in results], axis=1) for member in range(4))
        )

    outputs, grad_queries, key_terms, value_terms = lax.map(
        one_block, (query_blocks, grad_blocks, key_pairs, valid_all)
    )
    band_total = jnp.zeros((2, rows_dev + 2 * rim_rows, kv_heads, head_dim), jnp.float32)
    for block_num in range(local_blocks):
        band_piece = jnp.stack(
            [
                key_terms[block_num, : span_blocks * BLOCK],
                value_terms[block_num, : span_blocks * BLOCK],
            ]
        )
        band_total = band_total.at[
            :, block_num * BLOCK : block_num * BLOCK + span_blocks * BLOCK
        ].add(band_piece)
    targets = jnp.arange(local_blocks, dtype=jnp.int32)
    partner_terms = []
    for level_bit in range(levels):
        first = (span_blocks + level_bit) * BLOCK
        level_part = jnp.stack(
            [key_terms[:, first : first + BLOCK], value_terms[:, first : first + BLOCK]], axis=1
        )
        routing = (chosen_list[level_bit][:, None] == targets[None, :]).astype(jnp.float32)
        routed = jnp.einsum("jt,jcbhd->ctbhd", routing, level_part, precision=lax.Precision.HIGHEST)
        partner_terms.append(routed.reshape(2, rows_dev, kv_heads, head_dim))
    total = fold_rims(band_total, rim_rows)
    for level_bit in range(levels):
        total = total + swapped(partner_terms[level_bit], "seq", level_bit)
    total = lax.psum_scatter(total, "head", scatter_dimension=2, tiled=True)
    return (
        outputs.reshape(query.shape),
        grad_queries.reshape(query.shape),
        total[0].astype(jnp.bfloat16),
        total[1].astype(jnp.bfloat16),
    )


def solution(mesh):
    placed = (
        P("seq", None, "head", None),
        P("seq", "head", None),
        P("seq", "head", None),
        P("seq", None, "head", None),
        P(None, "head"),
        P(),
        P("seq", None),
    )
    return jax.shard_map(
        shards,
        mesh=mesh,
        in_specs=placed,
        out_specs=(
            P("seq", None, "head", None),
            P("seq", None, "head", None),
            P("seq", "head", None),
            P("seq", "head", None),
        ),
        check_vma=False,
    )
```

profile of v0, /device:TPU:1, one launch (start us, length us, event | category | flops | bytes accessed | tf_op | source)
XLA Modules:
  0.0 666.9 jit_solution(8617291111567787883)
XLA Ops:
  10.2 29.8 %all-gather.2.cloned.1.call-done = bf16[2,256,8,128]{3,1,2,0:T(8,128)(2,1)} async-done(((bf16[2,256,4,128]{3,1,2,0:T(8,128)(2,1)}), bf16[2,256,8,128]{3,1,2,0:T(8,128)(2,1)}) %all-gather.2.cloned.1.call-update) | async-done | bytes 1048592 | tf_op jit(solution)/shard_map/all_gather | solution.py:92
  56.6 8.6 %collective-permute-done.1 = bf16[2,128,8,128]{3,1,2,0:T(8,128)(2,1)S(1)} collective-permute-done((bf16[2,128,8,128]{3,1,2,0:T(8,128)(2,1)S(1)}, bf16[2,128,8,128]{3,1,2,0:T(8,128)(2,1)S(1)}, u32[]{:S(2)}, u32[]{:S(2)}) %collective-permute-start.1) | collective-permute-done | bytes 524320 | tf_op jit(solution)/shard_map/ppermute | solution.py:24
  65.2 4.9 collective-permute-start.8
  70.1 4.5 collective-permute-done.5
  86.1 19.5 %collective-permute-done.3 = bf16[2,256,8,128]{3,1,2,0:T(8,128)(2,1)} collective-permute-done((bf16[2,256,8,128]{3,1,2,0:T(8,128)(2,1)}, bf16[2,256,8,128]{3,1,2,0:T(8,128)(2,1)}, u32[]{:S(2)}, u32[]{:S(2)}) %collective-permute-start.3) | collective-permute-done | bytes 1048608 | tf_op jit(solution)/shard_map/ppermute | solution.py:30
  114.3 22.6 %collective-permute-done.7 = bf16[2,256,8,128]{3,1,2,0:T(8,128)(2,1)} collective-permute-done((bf16[2,256,8,128]{3,1,2,0:T(8,128)(2,1)}, bf16[2,256,8,128]{3,1,2,0:T(8,128)(2,1)}, u32[]{:S(2)}, u32[]{:S(2)}) %collective-permute-start.7) | collective-permute-done | bytes 1048608 | tf_op jit(solution)/shard_map/ppermute | solution.py:30
  145.0 7.3 %pad_maximum_fusion = bf16[2,2,1280,8,128]{4,2,3,1,0:T(8,128)(2,1)} fusion(bf16[2,2,896,8,128]{4,2,3,1,0:T(8,128)(2,1)S(1)} %bitcast.369, bf16[1,2,384,8,128]{4,2,3,1,0:T(8,128)(2,1)S(1)} %get-tuple-element.188, bf16[1,2,384,8,128]{4,2,3,1,0:T(8,128)(2,1)S(1)} %get-tuple-element.187), kind=kLoop, calls=%fused_computation.70 | loop fusion | flops 31457280 | bytes 20971520 | tf_op jit(solution)/shard_map/concatenate | solution.py:115
  152.4 86.7 %while.20 = (s32[]{:T(128)}, bf16[2,128,8,2,128]{4,3,2,1,0:T(2,128)(2,1)}, bf16[2,128,8,2,128]{4,3,2,1,0:T(2,128)(2,1)}, f32[2,1280,8,128]{1,3,2,0:T(8,128)}, f3...) while((s32[]{:T(128)}, ...), condition=%wide.region_14.16_spmd, body=%wide.region_7.15_spmd.sunk | while | flops 4066897920 | bytes 144654640 | solution.py:147
  189.0 6.6 fusion.133
  232.1 6.6 fusion.133
  239.1 12.0 %copy.126 = f32[2,1280,8,128]{3,2,1,0:T(8,128)} copy(f32[2,1280,8,128]{1,3,2,0:T(8,128)} %get-tuple-element.106) | data formatting | bytes 20971520 | tf_op jit(solution)/shard_map/while | solution.py:147
  251.1 16.4 %copy.130 = f32[2,1280,8,128]{3,0,2,1:T(2,128)} copy(f32[2,1280,8,128]{1,3,2,0:T(8,128)} %get-tuple-element.106) | data formatting | bytes 20971520 | tf_op jit(solution)/shard_map/while | solution.py:147
  269.6 5.8 slice_bitcast_fusion.24
  275.4 16.4 %copy.129 = f32[2,1280,8,128]{3,0,2,1:T(2,128)} copy(f32[2,1280,8,128]{1,3,2,0:T(8,128)} %get-tuple-element.105) | data formatting | bytes 20971520 | tf_op jit(solution)/shard_map/while | solution.py:147
  291.8 5.6 slice_bitcast_fusion.25
  297.4 5.7 fusion.38
  304.7 5.6 fusion.37
  311.9 26.1 %collective-permute-start.12 = (f32[2,256,8,128]{3,2,1,0:T(8,128)}, f32[2,256,8,128]{3,2,1,0:T(8,128)}, u32[]{:S(2)}, u32[]{:S(2)}) collective-permute-start(f32[2,256,8,128]{3,2,1,0:T(8,128)} %bitcast.86), channel_id=1, source_target_pairs={{0,4},{2,6},{4,0},{6,2},{8,12},{10,14},{12,8},{14,10},{16,20},{18,... | collective-permute-start | bytes 6291464 | tf_op jit(solution)/shard_map/ppermute | solution.py:30
  338.0 14.8 %collective-permute-start.13 = (f32[2,256,8,128]{3,2,1,0:T(8,128)}, f32[2,256,8,128]{3,2,1,0:T(8,128)}, u32[]{:S(2)}, u32[]{:S(2)}) collective-permute-start(f32[2,256,8,128]{3,2,1,0:T(8,128)} %bitcast.92), channel_id=1, source_target_pairs={{0,8},{2,10},{4,12},{6,14},{8,0},{10,2},{12,4},{14,6},{16,24},{18,... | collective-permute-start | bytes 6291464 | tf_op jit(solution)/shard_map/ppermute | solution.py:30
  352.8 6.8 %fusion.36 = f32[2,2,128,8,128]{4,1,3,2,0:T(2,128)} fusion(f32[2,1,128,8,128]{4,0,3,2,1:T(2,128)S(1)} %copy-done.19, f32[2,1,128,8,128]{4,0,3,2,1:T(2,128)S(1)} %get-tuple-element.169, s32[2]{0:T(128)S(1)} %copy-done.35), kind=kOutput, calls=%fused_computation.91 | convolution fusion | flops 13107204 | bytes 4194312 | tf_op jit(solution)/shard_map/jt,jcbhd->ctbhd/dot_general | solution.py:169
  359.6 12.0 %copy.125 = f32[2,1280,8,128]{3,2,1,0:T(8,128)} copy(f32[2,1280,8,128]{1,3,2,0:T(8,128)} %get-tuple-element.105) | data formatting | bytes 20971520 | tf_op jit(solution)/shard_map/while | solution.py:147
  380.7 5.7 fusion.42
  387.9 5.6 fusion.41
  395.1 5.6 fusion.40
  402.3 5.8 fusion.39
  412.5 21.4 %collective-permute-done.10 = bf16[2,128,8,128]{3,2,1,0:T(8,128)(2,1)S(1)} collective-permute-done((bf16[2,128,8,128]{3,2,1,0:T(8,128)(2,1)S(1)}, bf16[2,128,8,128]{3,2,1,0:T(8,128)(2,1)S(1)}, u32[]{:S(2)}, u32[]{:S(2)}) %collective-permute-start.10) | collective-permute-done | bytes 524320 | tf_op jit(solution)/shard_map/ppermute | solution.py:13
  433.8 5.6 collective-permute-start.15
  446.0 7.1 %collective-permute-done.14 = f32[2,256,8,128]{3,2,1,0:T(8,128)S(1)} collective-permute-done((f32[2,256,8,128]{3,2,1,0:T(8,128)S(1)}, f32[2,256,8,128]{3,2,1,0:T(8,128)S(1)}, u32[]{:S(2)}, u32[]{:S(2)}) %collective-permute-start.14) | collective-permute-done | bytes 2097184 | tf_op jit(solution)/shard_map/ppermute | solution.py:30
  453.1 76.4 %collective-permute-done.15 = f32[2,256,8,128]{3,2,1,0:T(8,128)S(1)} collective-permute-done((f32[2,256,8,128]{3,2,1,0:T(8,128)S(1)}, f32[2,256,8,128]{3,2,1,0:T(8,128)S(1)}, u32[]{:S(2)}, u32[]{:S(2)}) %collective-permute-start.15) | collective-permute-done | bytes 2097184 | tf_op jit(solution)/shard_map/ppermute | solution.py:30
  529.4 55.7 %collective-permute-done.16 = f32[2,256,8,128]{3,2,1,0:T(8,128)S(1)} collective-permute-done((f32[2,256,8,128]{3,2,1,0:T(8,128)S(1)}, f32[2,256,8,128]{3,2,1,0:T(8,128)S(1)}, u32[]{:S(2)}, u32[]{:S(2)}) %collective-permute-start.16) | collective-permute-done | bytes 2097184 | tf_op jit(solution)/shard_map/ppermute | solution.py:30
  585.1 16.3 %collective-permute-done.17 = f32[2,256,8,128]{3,2,1,0:T(8,128)S(1)} collective-permute-done((f32[2,256,8,128]{3,2,1,0:T(8,128)S(1)}, f32[2,256,8,128]{3,2,1,0:T(8,128)S(1)}, u32[]{:S(2)}, u32[]{:S(2)}) %collective-permute-start.17) | collective-permute-done | bytes 2097184 | tf_op jit(solution)/shard_map/ppermute | solution.py:30
  606.4 50.3 %reduce-scatter.2.cloned.1.call-done = f32[2,256,4,128]{3,1,0,2:T(8,128)} async-done(((f32[2,256,8,128]{3,1,0,2:T(8,128)}), f32[2,256,4,128]{3,1,0,2:T(8,128)}) %reduce-scatter.2.cloned.1.call-update) | async-done | bytes 1048592 | tf_op jit(solution)/shard_map/reduce_scatter | solution.py:174
  (251 shorter events, 157.8 us)
Async XLA Ops:
  7.2 32.8 %all-gather.2.cloned.1.call-start = ((), (), s32[]{:S(2)}) async-start(), calls=%async_computation.1 | async-start | bytes 1572864 | tf_op jit(solution)/shard_map/all_gather | solution.py:92
  9.2 647.5 %reduce-scatter.2.cloned.1.call-start = ((), (), s32[]{:S(2)}) async-start(), calls=%async_computation.2 | async-start | bytes 3145728 | tf_op jit(solution)/shard_map/reduce_scatter | solution.py:174
  9.6 39.7 %copy-start.32 = (s32[2]{0:T(128)}, s32[2]{0:T(128)S(1)}, u32[]{:S(2)}) copy-start(s32[2]{0:T(128)S(1)} %get-tuple-element.131) | copy-start | bytes 28
  9.6 41.6 %copy-start.28 = (s32[2]{0:T(128)}, s32[2]{0:T(128)S(1)}, u32[]{:S(2)}) copy-start(s32[2]{0:T(128)S(1)} %get-tuple-element.132) | copy-start | bytes 28
  9.6 67.2 %copy-start.38 = (s32[2]{0:T(128)}, s32[2]{0:T(128)S(1)}, u32[]{:S(2)}) copy-start(s32[2]{0:T(128)S(1)} %get-tuple-element.134) | copy-start | bytes 28
  9.6 67.2 %copy-start.36 = (s32[2]{0:T(128)}, s32[2]{0:T(128)S(1)}, u32[]{:S(2)}) copy-start(s32[2]{0:T(128)S(1)} %get-tuple-element.135) | copy-start | bytes 28
  9.6 67.2 %copy-start.26 = (s32[2]{0:T(128)}, s32[2]{0:T(128)S(1)}, u32[]{:S(2)}) copy-start(s32[2]{0:T(128)S(1)} %get-tuple-element.133) | copy-start | bytes 28
  9.6 67.5 %copy-start.30 = (s32[2]{0:T(128)}, s32[2]{0:T(128)S(1)}, u32[]{:S(2)}) copy-start(s32[2]{0:T(128)S(1)} %get-tuple-element.137) | copy-start | bytes 28
  9.6 67.5 %copy-start.34 = (s32[2]{0:T(128)}, s32[2]{0:T(128)S(1)}, u32[]{:S(2)}) copy-start(s32[2]{0:T(128)S(1)} %get-tuple-element.136) | copy-start | bytes 28
  40.0 36.8 %copy-start.4 = (bf16[2,256,8,128]{3,1,2,0:T(8,128)(2,1)S(1)}, bf16[2,256,8,128]{3,1,2,0:T(8,128)(2,1)}, u32[]{:S(2)}) copy-start(bf16[2,256,8,128]{3,1,2,0:T(8,128)(2,1)} %all-gather.2.cloned.1.call-done) | copy-start | bytes 3145732
  40.0 25.1 %collective-permute-start.6 = (bf16[2,256,8,128]{3,1,2,0:T(8,128)(2,1)}, bf16[2,256,8,128]{3,1,2,0:T(8,128)(2,1)S(1)}, u32[]{:S(2)}, u32[]{:S(2)}) collective-permute-start(bf16[2,256,8,128]{3,1,2,0:T(8,128)(2,1)} %all-gather.2.cloned.1.call-done), channel_id=1, source_target_pairs={{0,32},{2,34},{4,36},{6,38},{8,40},{10,42},{12,44},{14,46},{16,48}... | collective-permute-start | bytes 3145736 | tf_op jit(solution)/shard_map/ppermute | solution.py:30
  41.3 33.2 %collective-permute-start.5 = (bf16[2,256,8,128]{3,1,2,0:T(8,128)(2,1)}, bf16[2,256,8,128]{3,1,2,0:T(8,128)(2,1)S(1)}, u32[]{:S(2)}, u32[]{:S(2)}) collective-permute-start(bf16[2,256,8,128]{3,1,2,0:T(8,128)(2,1)} %all-gather.2.cloned.1.call-done), channel_id=1, source_target_pairs={{0,16},{2,18},{4,20},{6,22},{8,24},{10,26},{12,28},{14,30},{16,0},... | collective-permute-start | bytes 3145736 | tf_op jit(solution)/shard_map/ppermute | solution.py:30
  45.0 10.3 %collective-permute-start = (bf16[2,128,8,128]{3,1,2,0:T(8,128)(2,1)S(1)}, bf16[2,128,8,128]{3,1,2,0:T(8,128)(2,1)S(1)}, u32[]{:S(2)}, u32[]{:S(2)}) collective-permute-start(bf16[2,128,8,128]{3,1,2,0:T(8,128)(2,1)S(1)} %get-tuple-element.189), channel_id=1, source_target_pairs={{0,2},{2,4},{4,6},{6,8},{8,10},{10,12},{12,14},{14,16},{16,18},{18... | collective-permute-start | bytes 1572872 | tf_op jit(solution)/shard_map/ppermute | solution.py:21
  49.3 15.9 %collective-permute-start.1 = (bf16[2,128,8,128]{3,1,2,0:T(8,128)(2,1)S(1)}, bf16[2,128,8,128]{3,1,2,0:T(8,128)(2,1)S(1)}, u32[]{:S(2)}, u32[]{:S(2)}) collective-permute-start(bf16[2,128,8,128]{3,1,2,0:T(8,128)(2,1)S(1)} %get-tuple-element.190), channel_id=1, source_target_pairs={{2,0},{4,2},{6,4},{8,6},{10,8},{12,10},{14,12},{16,14},{18,16},{20... | collective-permute-start | bytes 1572872 | tf_op jit(solution)/shard_map/ppermute | solution.py:24
  51.2 32.0 %collective-permute-start.4 = (bf16[2,256,8,128]{3,1,2,0:T(8,128)(2,1)}, bf16[2,256,8,128]{3,1,2,0:T(8,128)(2,1)}, u32[]{:S(2)}, u32[]{:S(2)}) collective-permute-start(bf16[2,256,8,128]{3,1,2,0:T(8,128)(2,1)} %all-gather.2.cloned.1.call-done), channel_id=1, source_target_pairs={{0,8},{2,10},{4,12},{6,14},{8,0},{10,2},{12,4},{14,6},{16,24},{18,... | collective-permute-start | bytes 3145736 | tf_op jit(solution)/shard_map/ppermute | solution.py:30
  55.3 50.3 %collective-permute-start.3 = (bf16[2,256,8,128]{3,1,2,0:T(8,128)(2,1)}, bf16[2,256,8,128]{3,1,2,0:T(8,128)(2,1)}, u32[]{:S(2)}, u32[]{:S(2)}) collective-permute-start(bf16[2,256,8,128]{3,1,2,0:T(8,128)(2,1)} %all-gather.2.cloned.1.call-done), channel_id=1, source_target_pairs={{0,4},{2,6},{4,0},{6,2},{8,12},{10,14},{12,8},{14,10},{16,20},{18,... | collective-permute-start | bytes 3145736 | tf_op jit(solution)/shard_map/ppermute | solution.py:30
  65.1 43.4 %collective-permute-start.2 = (bf16[2,256,8,128]{3,1,2,0:T(8,128)(2,1)}, bf16[2,256,8,128]{3,1,2,0:T(8,128)(2,1)}, u32[]{:S(2)}, u32[]{:S(2)}) collective-permute-start(bf16[2,256,8,128]{3,1,2,0:T(8,128)(2,1)} %all-gather.2.cloned.1.call-done), channel_id=1, source_target_pairs={{0,2},{2,0},{4,6},{6,4},{8,10},{10,8},{12,14},{14,12},{16,18},{18,... | collective-permute-start | bytes 3145736 | tf_op jit(solution)/shard_map/ppermute | solution.py:30
  65.2 12.0 %copy-start.22 = (bf16[2,256,8,128]{3,1,2,0:T(8,128)(2,1)}, bf16[2,256,8,128]{3,1,2,0:T(8,128)(2,1)S(1)}, u32[]{:S(2)}) copy-start(bf16[2,256,8,128]{3,1,2,0:T(8,128)(2,1)S(1)} %collective-permute-done.6) | copy-start | bytes 3145732
  65.2 46.2 %collective-permute-start.8 = (bf16[2,256,8,128]{3,1,2,0:T(8,128)(2,1)}, bf16[2,256,8,128]{3,1,2,0:T(8,128)(2,1)}, u32[]{:S(2)}, u32[]{:S(2)}) collective-permute-start(bf16[2,256,8,128]{3,1,2,0:T(8,128)(2,1)} %all-gather.2.cloned.1.call-done), channel_id=1, source_target_pairs={{0,128},{2,130},{4,132},{6,134},{8,136},{10,138},{12,140},{14,142}... | collective-permute-start | bytes 3145736 | tf_op jit(solution)/shard_map/ppermute | solution.py:30
  74.5 62.3 %collective-permute-start.7 = (bf16[2,256,8,128]{3,1,2,0:T(8,128)(2,1)}, bf16[2,256,8,128]{3,1,2,0:T(8,128)(2,1)}, u32[]{:S(2)}, u32[]{:S(2)}) collective-permute-start(bf16[2,256,8,128]{3,1,2,0:T(8,128)(2,1)} %all-gather.2.cloned.1.call-done), channel_id=1, source_target_pairs={{0,64},{2,66},{4,68},{6,70},{8,72},{10,74},{12,76},{14,78},{16,80}... | collective-permute-start | bytes 3145736 | tf_op jit(solution)/shard_map/ppermute | solution.py:30
  197.3 5.6 copy-start.2
  310.3 42.5 %copy-start.19 = (f32[2,1,128,8,128]{4,0,3,2,1:T(2,128)S(1)}, f32[2,1,128,8,128]{4,0,3,2,1:T(2,128)}, u32[]{:S(2)}) copy-start(f32[2,1,128,8,128]{4,0,3,2,1:T(2,128)} %get-tuple-element.176) | copy-start | bytes 3145732
  310.3 42.5 %copy-start.35 = (s32[2]{0:T(128)S(1)}, s32[2]{0:T(128)}, u32[]{:S(2)}) copy-start(s32[2]{0:T(128)} %copy-done.34) | copy-start | bytes 28
  311.9 128.4 %collective-permute-start.12 = (f32[2,256,8,128]{3,2,1,0:T(8,128)}, f32[2,256,8,128]{3,2,1,0:T(8,128)}, u32[]{:S(2)}, u32[]{:S(2)}) collective-permute-start(f32[2,256,8,128]{3,2,1,0:T(8,128)} %bitcast.86), channel_id=1, source_target_pairs={{0,4},{2,6},{4,0},{6,2},{8,12},{10,14},{12,8},{14,10},{16,20},{18,... | collective-permute-start | bytes 6291464 | tf_op jit(solution)/shard_map/ppermute | solution.py:30
  338.0 105.4 %collective-permute-start.13 = (f32[2,256,8,128]{3,2,1,0:T(8,128)}, f32[2,256,8,128]{3,2,1,0:T(8,128)}, u32[]{:S(2)}, u32[]{:S(2)}) collective-permute-start(f32[2,256,8,128]{3,2,1,0:T(8,128)} %bitcast.92), channel_id=1, source_target_pairs={{0,8},{2,10},{4,12},{6,14},{8,0},{10,2},{12,4},{14,6},{16,24},{18,... | collective-permute-start | bytes 6291464 | tf_op jit(solution)/shard_map/ppermute | solution.py:30
  376.1 57.7 %collective-permute-start.10 = (bf16[2,128,8,128]{3,2,1,0:T(8,128)(2,1)S(1)}, bf16[2,128,8,128]{3,2,1,0:T(8,128)(2,1)S(1)}, u32[]{:S(2)}, u32[]{:S(2)}) collective-permute-start(bf16[2,128,8,128]{3,2,1,0:T(8,128)(2,1)S(1)} %slice.376), channel_id=1, source_target_pairs={{0,2},{2,4},{4,6},{6,8},{8,10},{10,12},{12,14},{14,16},{16,18},{18... | collective-permute-start | bytes 1572872 | tf_op jit(solution)/shard_map/ppermute | solution.py:13
  378.3 62.0 %collective-permute-start.9 = (bf16[2,128,8,128]{3,2,1,0:T(8,128)(2,1)S(1)}, bf16[2,128,8,128]{3,2,1,0:T(8,128)(2,1)S(1)}, u32[]{:S(2)}, u32[]{:S(2)}) collective-permute-start(bf16[2,128,8,128]{3,2,1,0:T(8,128)(2,1)S(1)} %fusion.44), channel_id=1, source_target_pairs={{2,0},{4,2},{6,4},{8,6},{10,8},{12,10},{14,12},{16,14},{18,16},{20... | collective-permute-start | bytes 1572872 | tf_op jit(solution)/shard_map/ppermute | solution.py:13
  408.3 44.7 %collective-permute-start.14 = (f32[2,256,8,128]{3,2,1,0:T(8,128)S(1)}, f32[2,256,8,128]{3,2,1,0:T(8,128)S(1)}, u32[]{:S(2)}, u32[]{:S(2)}) collective-permute-start(f32[2,256,8,128]{3,2,1,0:T(8,128)S(1)} %bitcast.374), channel_id=1, source_target_pairs={{0,16},{2,18},{4,20},{6,22},{8,24},{10,26},{12,28},{14,30},{16,0},... | collective-permute-start | bytes 6291464 | tf_op jit(solution)/shard_map/ppermute | solution.py:30
  433.8 95.6 %collective-permute-start.15 = (f32[2,256,8,128]{3,2,1,0:T(8,128)S(1)}, f32[2,256,8,128]{3,2,1,0:T(8,128)S(1)}, u32[]{:S(2)}, u32[]{:S(2)}) collective-permute-start(f32[2,256,8,128]{3,2,1,0:T(8,128)S(1)} %bitcast.373), channel_id=1, source_target_pairs={{0,32},{2,34},{4,36},{6,38},{8,40},{10,42},{12,44},{14,46},{16,48}... | collective-permute-start | bytes 6291464 | tf_op jit(solution)/shard_map/ppermute | solution.py:30
  440.3 144.8 %collective-permute-start.16 = (f32[2,256,8,128]{3,2,1,0:T(8,128)S(1)}, f32[2,256,8,128]{3,2,1,0:T(8,128)S(1)}, u32[]{:S(2)}, u32[]{:S(2)}) collective-permute-start(f32[2,256,8,128]{3,2,1,0:T(8,128)S(1)} %bitcast.372), channel_id=1, source_target_pairs={{0,64},{2,66},{4,68},{6,70},{8,72},{10,74},{12,76},{14,78},{16,80}... | collective-permute-start | bytes 6291464 | tf_op jit(solution)/shard_map/ppermute | solution.py:30
  440.3 161.0 %collective-permute-start.17 = (f32[2,256,8,128]{3,2,1,0:T(8,128)S(1)}, f32[2,256,8,128]{3,2,1,0:T(8,128)S(1)}, u32[]{:S(2)}, u32[]{:S(2)}) collective-permute-start(f32[2,256,8,128]{3,2,1,0:T(8,128)S(1)} %bitcast.371), channel_id=1, source_target_pairs={{0,128},{2,130},{4,132},{6,134},{8,136},{10,138},{12,140},{14,142}... | collective-permute-start | bytes 6291464 | tf_op jit(solution)/shard_map/ppermute | solution.py:30
  443.3 158.0 %collective-permute-start.11 = (f32[2,256,8,128]{3,2,1,0:T(8,128)S(1)}, f32[2,256,8,128]{3,2,1,0:T(8,128)S(1)}, u32[]{:S(2)}, u32[]{:S(2)}) collective-permute-start(f32[2,256,8,128]{3,2,1,0:T(8,128)S(1)} %bitcast.370), channel_id=1, source_target_pairs={{0,2},{2,0},{4,6},{6,4},{8,10},{10,8},{12,14},{14,12},{16,18},{18,... | collective-permute-start | bytes 6291464 | tf_op jit(solution)/shard_map/ppermute | solution.py:30
  (33 other events, 71.0 us)
Sparse Core Ops, SparseCore 0:
  9.8 30.1 all-gather.1
  606.5 50.1 reduce-scatter.1
where the time goes:
time: 676 us; the launch traced here: 667 us
  waiting for transfers between devices  317 us (47%)
  local copies, waits for them, and re-layouts  137 us (20%)
  starting transfers between devices  79.4 us (12%)
  matrix products  77.5 us (11%)
  other arithmetic  40.3 us (6%)
  between operations  15.1 us (2%)
    ppermute x14, waiting for transfers between devices, swapped(): lax.ppermute(value, axis, [(i, i ^ 1 << distance) for i in range(lax.axis...  204 us
    ppermute x14, starting transfers between devices, swapped(): lax.ppermute(value, axis, [(i, i ^ 1 << distance) for i in range(lax.axis...  68.7 us
    while x4, local copies, waits for them, and re-layouts, shards(): lax.map(one_block, (query_blocks, grad_blocks, key_pairs, valid_all))  56.8 us
    reduce_scatter x1, waiting for transfers between devices, shards(): total = lax.psum_scatter(total, 'head', scatter_dimension=2, tiled=True)  50.3 us
    dot_general x7, matrix products, shards(): jnp.einsum('jt,jcbhd->ctbhd', routing, level_part, precision=lax.Precisio...  40.9 us
    all_gather x1, waiting for transfers between devices, shards(): all_heads = lax.all_gather(stacked, 'head', axis=2, tiled=True)  29.8 us
    ppermute x2, waiting for transfers between devices, from_behind(): lax.ppermute(value, axis, [(source, source + steps) for source in range(i...  22.3 us
    gather x7, local copies, waits for them, and re-layouts, shards(): partner_list.append(jnp.take(arriving, chosen, axis=1))  20.2 us
  transfers between devices with their start and end apart: 20, of which 15 were waited for; matrix products, arithmetic and copies ran while one was open for 10% of the time, Pallas kernels for 0%

commit v1 on v0

v1 whole, which is shorter than its diff:
```python
import math

import jax
import jax.numpy as jnp
from jax import lax
from jax.experimental import pallas as pl
from jax.experimental.pallas import tpu as pltpu
from jax.sharding import PartitionSpec as P

BLOCK = 128
HEAD_DIM = 128
CHUNKS = 1
LOCAL_HEADS = 4
LEVELS = 7
BAND_SLOTS = 3
SLOTS = BAND_SLOTS + LEVELS
ROWS = 512
NEG = -1e30
F32 = jnp.float32
BF16 = jnp.bfloat16
WHOLE = pl.BlockSpec(memory_space=pltpu.VMEM)
SCALARS = pl.BlockSpec(memory_space=pltpu.SMEM)


def vmem(mib):
    return pltpu.CompilerParams(vmem_limit_bytes=mib << 20)


def dot(lhs, rhs, lhs_dim, rhs_dim):
    return lax.dot_general(
        lhs, rhs, (((lhs_dim,), (rhs_dim,)), ((), ())), preferred_element_type=F32
    )


def query_order(place, rows_first):
    ordered = lax.broadcasted_iota(jnp.int32, (256, 256), rows_first)
    natural = lax.broadcasted_iota(jnp.int32, (256, 256), 1 - rows_first)
    source = (ordered & 15) * 16 + ((ordered >> 4) ^ (place * 8))
    return (natural == source).astype(BF16)


def key_order(rows_first):
    ordered = lax.broadcasted_iota(jnp.int32, (256, 256), rows_first)
    natural = lax.broadcasted_iota(jnp.int32, (256, 256), 1 - rows_first)
    return (natural == (ordered & 63) * 4 + (ordered >> 6)).astype(BF16)


def pack_kernel(scalars, query, grad, key, value, *outs):
    place = scalars[0]
    chunks = len(outs) // 3
    pairs, keeps, sends = outs[:chunks], outs[chunks : 2 * chunks], outs[2 * chunks :]
    per = LOCAL_HEADS // chunks
    order = key_order(0)
    for member, source in enumerate((key, value)):
        for part in range(4):
            rows = dot(order, source[part * 256 : part * 256 + 256], 1, 0).astype(BF16)
            for head in range(LOCAL_HEADS):
                pairs[head // per][head % per, member, part * 64 : part * 64 + 64] = rows[
                    head * 64 : head * 64 + 64
                ]
    order = query_order(place, 0)
    for member, source in enumerate((query, grad)):
        for part in range(16):
            rows = dot(order, source[part * 256 : part * 256 + 256], 1, 0).astype(BF16)
            block, inner = part // 8, (part % 8) * 16
            for head in range(2 * LOCAL_HEADS):
                target = (keeps, sends)[head // LOCAL_HEADS]
                local = head % LOCAL_HEADS
                for group in range(2):
                    start = (member * 2 + block) * 256 + group * 128 + inner
                    first = (head * 2 + group) * 16
                    target[local // per][local % per, start : start + 16] = rows[first : first + 16]
    sublane = lax.broadcasted_iota(jnp.int32, (16, HEAD_DIM), 0)
    for head in range(2 * LOCAL_HEADS):
        target = (keeps, sends)[head // LOCAL_HEADS]
        local = head % LOCAL_HEADS
        actual = head ^ (place * LOCAL_HEADS)
        width = jnp.where(sublane == 0, scalars[1 + actual * 2], scalars[2 + actual * 2])
        target[local // per][local % per, 1024:1040] = width.astype(F32).astype(BF16)


def attend_kernel(scalars, *refs):
    own, ext = refs[0], refs[1]
    arrived = refs[2 : 2 + LEVELS]
    keep, other = refs[2 + LEVELS : 4 + LEVELS]
    outs = refs[4 + LEVELS :]
    keep_out, other_out, own_out, ext_out = outs[:4]
    level_out = outs[4 : 4 + LEVELS]
    scores, exps, dscores, keys, values, acc = outs[4 + LEVELS :]
    heads = own.shape[0]
    device = scalars[0]
    last = scalars[1]
    even = (device & 1) == 0
    scale = HEAD_DIM**-0.5
    log_scale = scale * math.log2(math.e)

    def one_head(head, carry):
        acc[...] = jnp.zeros_like(acc)
        widths = jnp.concatenate(
            [
                ref[head, 1024:1040].astype(F32)[group : group + 1]
                for ref in (keep, other)
                for group in range(2)
            ],
            axis=1,
        )
        width_bias = jnp.where(widths > 1.5, 0.0, NEG)
        for block in range(2):
            side = 1 - block
            outer_valid = device > 0 if block == 0 else device < last
            from_ext = even if block == 0 else jnp.logical_not(even)
            side_rows = side * BLOCK
            for member, store in enumerate((keys, values)):
                store[0:BLOCK] = own[head, member, 0:BLOCK]
                store[BLOCK : 2 * BLOCK] = own[head, member, BLOCK : 2 * BLOCK]
                store[2 * BLOCK : 3 * BLOCK] = jnp.where(
                    from_ext,
                    ext[head, member],
                    arrived[0][head, member, side_rows : side_rows + BLOCK],
                )
                for level in range(LEVELS):
                    chosen = scalars[2 + block * LEVELS + level]
                    first = (BAND_SLOTS + level) * BLOCK
                    store[first : first + BLOCK] = arrived[level][
                        head, member, pl.ds(pl.multiple_of(chosen * BLOCK, BLOCK), BLOCK)
                    ]
            query_t, grad_t = (
                jnp.concatenate(
                    [
                        jnp.transpose(
                            ref[
                                head,
                                (member * 2 + block) * 256 : (member * 2 + block) * 256 + 256,
                            ]
                        )
                        for ref in (keep, other)
                    ],
                    axis=1,
                )
                for member in range(2)
            )
            outer_bias = width_bias + jnp.where(outer_valid, 0.0, NEG)
            peak = jnp.full((8, ROWS), NEG, F32)
            for slot in range(SLOTS):
                span = slice(slot * BLOCK, slot * BLOCK + BLOCK)
                part = dot(keys[span], query_t, 1, 0)
                if slot == side:
                    part = part + width_bias
                if slot == 2:
                    part = part + outer_bias
                scores[span] = part
                peak = jnp.maximum(peak, jnp.max(part.reshape(BLOCK // 8, 8, ROWS), axis=0))
            peak = jnp.max(peak, axis=0, keepdims=True) * log_scale
            total = jnp.zeros((8, ROWS), F32)
            for slot in range(SLOTS):
                span = slice(slot * BLOCK, slot * BLOCK + BLOCK)
                part = jnp.exp2(scores[span] * log_scale - peak)
                total = total + jnp.sum(part.reshape(BLOCK // 8, 8, ROWS), axis=0)
                exps[span] = part.astype(BF16)
            inverse = 1.0 / jnp.sum(total, axis=0, keepdims=True)
            out_t = (dot(values[...], exps[...], 0, 0) * inverse).astype(BF16)
            grad_t = (grad_t.astype(F32) * inverse).astype(BF16)
            delta = jnp.sum(out_t.astype(F32) * grad_t.astype(F32), axis=0, keepdims=True)
            for slot in range(SLOTS):
                span = slice(slot * BLOCK, slot * BLOCK + BLOCK)
                part = dot(values[span], grad_t, 1, 0)
                dscores[span] = (exps[span].astype(F32) * (part - delta)).astype(BF16)
            dquery_t = (dot(keys[...], dscores[...], 0, 0) * scale).astype(BF16)
            for member, rows_t in enumerate((out_t, dquery_t)):
                first = (member * 2 + block) * 256
                keep_out[head, first : first + 256] = jnp.transpose(rows_t[:, 0:256])
                other_out[head, first : first + 256] = jnp.transpose(rows_t[:, 256:512])
            outer_row = jnp.where(from_ext, 2, 3 + side)
            for member, (lhs, rhs, factor) in enumerate(
                ((dscores, query_t, scale), (exps, grad_t, None))
            ):
                terms = dot(lhs[...], rhs, 1, 1)
                if factor is not None:
                    terms = terms * factor
                acc[member, 0 : 2 * BLOCK] += terms[0 : 2 * BLOCK]
                targets = [outer_row] + [
                    3 + 2 * level + scalars[2 + block * LEVELS + level] for level in range(LEVELS)
                ]
                for slot, row in enumerate(targets):
                    at = pl.ds(pl.multiple_of(row * BLOCK, BLOCK), BLOCK)
                    first = (2 + slot) * BLOCK
                    acc[member, at] += terms[first : first + BLOCK]
        for member in range(2):
            own_out[head, member] = acc[member, 0 : 2 * BLOCK]
            ext_out[head, member] = acc[member, 2 * BLOCK : 3 * BLOCK].astype(BF16)
            for level in range(LEVELS):
                first = (3 + 2 * level) * BLOCK
                level_out[level][head, member] = acc[member, first : first + 2 * BLOCK].astype(BF16)
        return carry

    lax.fori_loop(0, heads, one_head, 0)


def finish_kernel(scalars, *refs):
    place, even = scalars[0], scalars[1]
    ins, outs = refs[:-4], refs[-4:]
    out_ref, dquery_ref, dkey_ref, dvalue_ref = outs
    per_chunk = len(ins) // CHUNKS
    per = LOCAL_HEADS // CHUNKS
    order = query_order(place, 1)
    for member, target in enumerate((out_ref, dquery_ref)):
        for part in range(16):
            block, inner = part // 8, (part % 8) * 16
            pieces = []
            for head in range(2 * LOCAL_HEADS):
                local = head % LOCAL_HEADS
                source = ins[(local // per) * per_chunk + head // LOCAL_HEADS]
                for group in range(2):
                    start = (member * 2 + block) * 256 + group * 128 + inner
                    pieces.append(source[local % per, start : start + 16])
            rows = jnp.concatenate(pieces, axis=0)
            target[part * 256 : part * 256 + 256] = dot(order, rows, 1, 0).astype(BF16)
    order = key_order(1)
    for member, target in enumerate((dkey_ref, dvalue_ref)):
        for part in range(4):
            pieces = []
            for head in range(LOCAL_HEADS):
                mine = ins[(head // per) * per_chunk : (head // per + 1) * per_chunk]
                span = slice(part * 64, part * 64 + 64)
                total = mine[2][head % per, member, span]
                for ref in mine[4:]:
                    total = total + ref[head % per, member, span].astype(F32)
                inner = (part % 2) * 64
                beyond = mine[3][head % per, member, inner : inner + 64].astype(F32)
                here = even == 1 if part < 2 else even == 0
                total = total + jnp.where(here, beyond, 0.0)
                pieces.append(total.astype(BF16))
            rows = jnp.concatenate(pieces, axis=0)
            target[part * 256 : part * 256 + 256] = dot(order, rows, 1, 0).astype(BF16)


def flipped(value, mask):
    return lax.ppermute(value, "seq", [(i, i ^ mask) for i in range(lax.axis_size("seq"))])


def past_end(value):
    pairs = []
    for i in range(1, lax.axis_size("seq") - 1, 2):
        pairs += [(i, i + 1), (i + 1, i)]
    return lax.ppermute(value, "seq", pairs)


def other_head(value):
    return lax.ppermute(value, "head", [(0, 1), (1, 0)])


def shards(query, key_in, value, grad_out, band_width, stride_bits, partner_table):
    rows = key_in.shape[0]
    per = LOCAL_HEADS // CHUNKS
    device = lax.axis_index("seq").astype(jnp.int32)
    place = lax.axis_index("head").astype(jnp.int32)
    even = (device & 1) == 0
    match = (stride_bits[None, :] == jnp.arange(LEVELS, dtype=jnp.int32)[:, None]).astype(jnp.int32)
    chosen = jnp.sum(partner_table[:, None, :] * match[None], axis=2)

    pair = jax.ShapeDtypeStruct((per, 2, rows, HEAD_DIM), BF16)
    sides = jax.ShapeDtypeStruct((per, 1040, HEAD_DIM), BF16)
    packed = pl.pallas_call(
        pack_kernel,
        out_shape=[pair] * CHUNKS + [sides] * (2 * CHUNKS),
        in_specs=[SCALARS] + [WHOLE] * 4,
        out_specs=[WHOLE] * (3 * CHUNKS),
        compiler_params=vmem(24),
        name="pack",
    )(
        jnp.concatenate([place[None], band_width.reshape(-1)]),
        query.reshape(-1, HEAD_DIM),
        grad_out.reshape(-1, HEAD_DIM),
        key_in.reshape(-1, HEAD_DIM),
        value.reshape(-1, HEAD_DIM),
    )
    pairs, keeps, sends = packed[:CHUNKS], packed[CHUNKS : 2 * CHUNKS], packed[2 * CHUNKS :]

    scalars = jnp.concatenate(
        [device[None], jnp.full((1,), lax.axis_size("seq") - 1, jnp.int32), chosen.reshape(-1)]
    )
    end = jax.ShapeDtypeStruct((per, 2, BLOCK, HEAD_DIM), BF16)
    half = jax.ShapeDtypeStruct((per, 1024, HEAD_DIM), BF16)
    parts = []
    for chunk in range(CHUNKS):
        own = pairs[chunk]
        arrived = [None] * LEVELS
        arrived[5] = flipped(own, 32)
        arrived[1] = flipped(own, 2)
        arrived[3] = flipped(own, 8)
        other = other_head(sends[chunk])
        arrived[6] = flipped(arrived[5], 96)
        arrived[4] = flipped(own, 16)
        arrived[2] = flipped(arrived[1], 6)
        ends = jnp.where(even, own[:, :, :BLOCK], own[:, :, BLOCK:])
        ext = past_end(ends)
        arrived[0] = flipped(own, 1)
        results = pl.pallas_call(
            attend_kernel,
            out_shape=[
                half,
                half,
                jax.ShapeDtypeStruct((per, 2, rows, HEAD_DIM), F32),
                end,
            ]
            + [pair] * LEVELS,
            in_specs=[SCALARS] + [WHOLE] * (4 + LEVELS),
            out_specs=[WHOLE] * (4 + LEVELS),
            scratch_shapes=[
                pltpu.VMEM((SLOTS * BLOCK, ROWS), F32),
                pltpu.VMEM((SLOTS * BLOCK, ROWS), BF16),
                pltpu.VMEM((SLOTS * BLOCK, ROWS), BF16),
                pltpu.VMEM((SLOTS * BLOCK, HEAD_DIM), BF16),
                pltpu.VMEM((SLOTS * BLOCK, HEAD_DIM), BF16),
                pltpu.VMEM((2, (3 + 2 * LEVELS) * BLOCK, HEAD_DIM), F32),
            ],
            compiler_params=vmem(40),
            name="attend",
        )(scalars, own, ext, *arrived, keeps[chunk], other)
        keep_out, other_out, own_terms, ext_terms = results[:4]
        terms = results[4:]
        far = flipped(terms[6], 96)
        near = flipped(terms[2], 6)
        swapped_out = other_head(other_out)
        back = [
            flipped(terms[4], 16),
            flipped(terms[3], 8),
            flipped((terms[5].astype(F32) + far.astype(F32)).astype(BF16), 32),
            flipped((terms[1].astype(F32) + near.astype(F32)).astype(BF16), 2),
            flipped(terms[0], 1),
        ]
        ext_back = past_end(ext_terms)
        parts += [keep_out, swapped_out, own_terms, ext_back] + back

    results = pl.pallas_call(
        finish_kernel,
        out_shape=[jax.ShapeDtypeStruct((rows * 16, HEAD_DIM), BF16)] * 2
        + [jax.ShapeDtypeStruct((rows * 4, HEAD_DIM), BF16)] * 2,
        in_specs=[SCALARS] + [WHOLE] * len(parts),
        out_specs=[WHOLE] * 4,
        compiler_params=vmem(32),
        name="finish",
    )(jnp.stack([place, even.astype(jnp.int32)]), *parts)
    return (
        results[0].reshape(query.shape),
        results[1].reshape(query.shape),
        results[2].reshape(key_in.shape),
        results[3].reshape(key_in.shape),
    )


def solution(mesh):
    placed = (
        P("seq", None, "head", None),
        P("seq", "head", None),
        P("seq", "head", None),
        P("seq", None, "head", None),
        P(None, "head"),
        P(),
        P("seq", None),
    )
    return jax.shard_map(
        shards,
        mesh=mesh,
        in_specs=placed,
        out_specs=(
            P("seq", None, "head", None),
            P("seq", None, "head", None),
            P("seq", "head", None),
            P("seq", "head", None),
        ),
        check_vma=False,
    )
```

time: 676 us -> 163 us (0.24); the launches traced: 667 us -> 162 us
  waiting for transfers between devices: 317 us -> 72.4 us
  local copies, waits for them, and re-layouts: 137 us -> 7.83 us
  matrix products: 77.5 us -> 0 us
  other arithmetic: 40.3 us -> 2.37 us
  starting transfers between devices: 79.4 us -> 46.9 us
  Pallas kernels: 0 us -> 31.9 us
  between operations: 15.1 us -> 0.71 us
    ppermute x18, waiting for transfers between devices: 236 us -> 72.4 us  [the longest x14 60.7 us: flipped(): lax.ppermute(value, 'seq', [(i, i ^ mask) for i in range(lax.axis_size('s...]
    dot_general x31 -> x0, matrix products: 77.5 us -> none  [the longest x7 40.9 us: shards(): jnp.einsum('jt,jcbhd->ctbhd', routing, level_part, precision=lax.Precisio...]
    while x24 -> x0, local copies, waits for them, and re-layouts: 59.3 us -> none  [the longest x4 56.8 us: shards(): lax.map(one_block, (query_blocks, grad_blocks, key_pairs, valid_all))]
    reduce_scatter x1 -> x0, waiting for transfers between devices: 50.3 us -> none  [shards(): total = lax.psum_scatter(total, 'head', scatter_dimension=2, tiled=True)]
    ppermute x18, starting transfers between devices: 79.3 us -> 46.9 us  [the longest x14 39 us: flipped(): lax.ppermute(value, 'seq', [(i, i ^ mask) for i in range(lax.axis_size('s...]
    pallas_call x0 -> x3, Pallas kernels: none -> 31.9 us  [the longest x1 25 us: shards(): pl.pallas_call(attend_kernel, out_shape=[half, half, jax.ShapeDtypeStruct...]
    all_gather x1 -> x0, waiting for transfers between devices: 29.8 us -> none  [shards(): all_heads = lax.all_gather(stacked, 'head', axis=2, tiled=True)]
    gather x7 -> x0, local copies, waits for them, and re-layouts: 20.2 us -> none  [shards(): partner_list.append(jnp.take(arriving, chosen, axis=1))]
  transfers between devices with their start and end apart: 20 -> 18, of which waited for: 15 -> 5; matrix products, arithmetic and copies ran while one was open for 10% -> 2% of each run, Pallas kernels for 0% -> 0%
where the time goes in v1:
time: 163 us; the launch traced here: 162 us
  waiting for transfers between devices  72.4 us (44%)
  starting transfers between devices  46.9 us (29%)
  Pallas kernels  31.9 us (20%)
  local copies, waits for them, and re-layouts  7.83 us (5%)
  other arithmetic  2.37 us (1%)
    ppermute x14, waiting for transfers between devices, flipped(): lax.ppermute(value, 'seq', [(i, i ^ mask) for i in range(lax.axis_size('s...  60.7 us
    ppermute x14, starting transfers between devices, flipped(): lax.ppermute(value, 'seq', [(i, i ^ mask) for i in range(lax.axis_size('s...  39 us
    pallas_call x1, Pallas kernels, shards(): pl.pallas_call(attend_kernel, out_shape=[half, half, jax.ShapeDtypeStruct...  25 us
    ppermute x2, waiting for transfers between devices, past_end(): return lax.ppermute(value, 'seq', pairs)  11.8 us
    unnamed x21, local copies, waits for them, and re-layouts  7.57 us
    ppermute x2, starting transfers between devices, past_end(): return lax.ppermute(value, 'seq', pairs)  5.67 us
    pallas_call x1, Pallas kernels, shards(): pl.pallas_call(finish_kernel, out_shape=[jax.ShapeDtypeStruct((rows * 16,...  3.77 us
  transfers between devices with their start and end apart: 18, of which 5 were waited for; matrix products, arithmetic and copies ran while one was open for 2% of the time, Pallas kernels for 0%

profile of v1, /device:TPU:1, one launch (start us, length us, event | category | flops | bytes accessed | tf_op | source)
XLA Modules:
  0.0 162.2 jit_solution(16163688757207489921)
XLA Ops:
  0.6 0.8 copy.14
  1.6 1.2 copy-done
  2.8 1.2 copy-done.1
  4.0 0.9 copy-done.6
  5.0 0.9 copy-done.7
  5.9 3.1 %pack.1 = (bf16[4,2,256,128]{3,2,1,0:T(8,128)(2,1)S(1)}, bf16[4,1040,128]{2,1,0:T(8,128)(2,1)S(1)}, bf16[4,1040,128]{2,1,0:T(8,128)(2,1)}) custom-call(s32[17]{0:T(128)S(1)} %pad_add_fusion.2.scalars, bf16[4096,128]{1,0:T(8,128)(2,1)S(1)} %bitcast.11, bf16[4096,128]{1,0:T(8,128)(2,1)S(1)} %bitcast.12, bf16[1024,128]{1,0:T(8,128)(2,1)S(1)} %bitcast.13, ...), custom_call_target="tpu_custom_call" | custom-call | tf_op jit(solution)/shard_map/pack/pallas_call | solution.py:263
  9.0 2.0 %collective-permute-start.8 = (bf16[4,1040,128]{2,1,0:T(8,128)(2,1)}, bf16[4,1040,128]{2,1,0:T(8,128)(2,1)S(1)}, u32[]{:S(2)}, u32[]{:S(2)}) collective-permute-start(bf16[4,1040,128]{2,1,0:T(8,128)(2,1)} %get-tuple-element.24), channel_id=1, source_target_pairs={{0,1},{1,0},{2,3},{3,2},{4,5},{5,4},{6,7},{7,6},{8,9},{9,8},{10,11... | collective-permute-start | bytes 3194888 | tf_op jit(solution)/shard_map/ppermute | solution.py:249
  11.0 3.0 %collective-permute-start.6 = (bf16[4,2,256,128]{3,2,1,0:T(8,128)(2,1)S(1)}, bf16[4,2,256,128]{3,2,1,0:T(8,128)(2,1)S(1)}, u32[]{:S(2)}, u32[]{:S(2)}) collective-permute-start(bf16[4,2,256,128]{3,2,1,0:T(8,128)(2,1)S(1)} %get-tuple-element.22.refs_0_), channel_id=1, source_target_pairs={{0,64},{2,66},{4,68},{6,70},{8,72},{10,74},{12,76},{14,78},{16,80}... | collective-permute-start | bytes 1572872 | tf_op jit(solution)/shard_map/ppermute | solution.py:238
  14.0 1.6 %collective-permute-start.5 = (bf16[4,2,256,128]{3,2,1,0:T(8,128)(2,1)S(1)}, bf16[4,2,256,128]{3,2,1,0:T(8,128)(2,1)}, u32[]{:S(2)}, u32[]{:S(2)}) collective-permute-start(bf16[4,2,256,128]{3,2,1,0:T(8,128)(2,1)S(1)} %get-tuple-element.22.refs_0_), channel_id=1, source_target_pairs={{0,32},{2,34},{4,36},{6,38},{8,40},{10,42},{12,44},{14,46},{16,48}... | collective-permute-start | bytes 1572872 | tf_op jit(solution)/shard_map/ppermute | solution.py:238
  15.7 1.3 collective-permute-start.2
  17.0 3.8 %collective-permute-start = (bf16[4,2,128,128]{3,2,1,0:T(8,128)(2,1)S(1)}, bf16[4,2,128,128]{3,2,1,0:T(8,128)(2,1)S(1)}, u32[]{:S(2)}, u32[]{:S(2)}) collective-permute-start(bf16[4,2,128,128]{3,2,1,0:T(8,128)(2,1)S(1)} %slice_select_fusion), channel_id=1, source_target_pairs={{2,4},{4,2},{6,8},{8,6},{10,12},{12,10},{14,16},{16,14},{18,20},{2... | collective-permute-start | bytes 786440 | tf_op jit(solution)/shard_map/ppermute | solution.py:245
  20.8 11.8 %collective-permute-done.refs_1_ = bf16[4,2,128,128]{3,2,1,0:T(8,128)(2,1)S(1)} collective-permute-done((bf16[4,2,128,128]{3,2,1,0:T(8,128)(2,1)S(1)}, bf16[4,2,128,128]{3,2,1,0:T(8,128)(2,1)S(1)}, u32[]{:S(2)}, u32[]{:S(2)}) %collective-permute-start) | collective-permute-done | bytes 262176 | tf_op jit(solution)/shard_map/ppermute | solution.py:245
  32.5 2.4 %collective-permute-start.4 = (bf16[4,2,256,128]{3,2,1,0:T(8,128)(2,1)S(1)}, bf16[4,2,256,128]{3,2,1,0:T(8,128)(2,1)}, u32[]{:S(2)}, u32[]{:S(2)}) collective-permute-start(bf16[4,2,256,128]{3,2,1,0:T(8,128)(2,1)S(1)} %get-tuple-element.22.refs_0_), channel_id=1, source_target_pairs={{0,16},{2,18},{4,20},{6,22},{8,24},{10,26},{12,28},{14,30},{16,0},... | collective-permute-start | bytes 1572872 | tf_op jit(solution)/shard_map/ppermute | solution.py:238
  35.0 1.7 %collective-permute-done.6.refs_7_ = bf16[4,2,256,128]{3,2,1,0:T(8,128)(2,1)S(1)} collective-permute-done((bf16[4,2,256,128]{3,2,1,0:T(8,128)(2,1)S(1)}, bf16[4,2,256,128]{3,2,1,0:T(8,128)(2,1)S(1)}, u32[]{:S(2)}, u32[]{:S(2)}) %collective-permute-start.6) | collective-permute-done | bytes 524320 | tf_op jit(solution)/shard_map/ppermute | solution.py:238
  36.6 8.7 %collective-permute-start.1 = (bf16[4,2,256,128]{3,2,1,0:T(8,128)(2,1)S(1)}, bf16[4,2,256,128]{3,2,1,0:T(8,128)(2,1)}, u32[]{:S(2)}, u32[]{:S(2)}) collective-permute-start(bf16[4,2,256,128]{3,2,1,0:T(8,128)(2,1)S(1)} %get-tuple-element.22.refs_0_), channel_id=1, source_target_pairs={{0,2},{2,0},{4,6},{6,4},{8,10},{10,8},{12,14},{14,12},{16,18},{18,... | collective-permute-start | bytes 1572872 | tf_op jit(solution)/shard_map/ppermute | solution.py:238
  45.3 6.6 %collective-permute-start.7 = (bf16[4,2,256,128]{3,2,1,0:T(8,128)(2,1)S(1)}, bf16[4,2,256,128]{3,2,1,0:T(8,128)(2,1)}, u32[]{:S(2)}, u32[]{:S(2)}) collective-permute-start(bf16[4,2,256,128]{3,2,1,0:T(8,128)(2,1)S(1)} %collective-permute-done.6.refs_7_), channel_id=1, source_target_pairs={{0,192},{2,194},{4,196},{6,198},{8,200},{10,202},{12,204},{14,206}... | collective-permute-start | bytes 1572872 | tf_op jit(solution)/shard_map/ppermute | solution.py:238
  51.9 0.8 collective-permute-start.3
  53.2 21.2 %collective-permute-done.7.refs_8_ = bf16[4,2,256,128]{3,2,1,0:T(8,128)(2,1)} collective-permute-done((bf16[4,2,256,128]{3,2,1,0:T(8,128)(2,1)S(1)}, bf16[4,2,256,128]{3,2,1,0:T(8,128)(2,1)}, u32[]{:S(2)}, u32[]{:S(2)}) %collective-permute-start.7) | collective-permute-done | bytes 524320 | tf_op jit(solution)/shard_map/ppermute | solution.py:238
  74.4 25.0 %attend.1 = (bf16[4,1024,128]{2,1,0:T(8,128)(2,1)S(1)}, bf16[4,1024,128]{2,1,0:T(8,128)(2,1)}, f32[4,2,256,128]{3,2,1,0:T(8,128)S(1)}, bf16[4,2,128,128]{3,2,1,0...) custom-call(s32[16]{0:T(128)S(1)} %pad_add_fusion.1.scalars, ...), custom_call_target="tpu_custom_call" | custom-call | tf_op jit(solution)/shard_map/attend/pallas_call | solution.py:298
  99.5 4.6 %collective-permute-start.13 = (bf16[4,2,256,128]{3,2,1,0:T(8,128)(2,1)S(1)}, bf16[4,2,256,128]{3,2,1,0:T(8,128)(2,1)S(1)}, u32[]{:S(2)}, u32[]{:S(2)}) collective-permute-start(bf16[4,2,256,128]{3,2,1,0:T(8,128)(2,1)S(1)} %get-tuple-element.32), channel_id=1, source_target_pairs={{0,192},{2,194},{4,196},{6,198},{8,200},{10,202},{12,204},{14,206}... | collective-permute-start | bytes 1572872 | tf_op jit(solution)/shard_map/ppermute | solution.py:238
  104.1 0.8 collective-permute-start.15
  104.9 1.9 %collective-permute-start.10 = (bf16[4,2,128,128]{3,2,1,0:T(8,128)(2,1)S(1)}, bf16[4,2,128,128]{3,2,1,0:T(8,128)(2,1)S(1)}, u32[]{:S(2)}, u32[]{:S(2)}) collective-permute-start(bf16[4,2,128,128]{3,2,1,0:T(8,128)(2,1)S(1)} %get-tuple-element.28), channel_id=1, source_target_pairs={{2,4},{4,2},{6,8},{8,6},{10,12},{12,10},{14,16},{16,14},{18,20},{2... | collective-permute-start | bytes 786440 | tf_op jit(solution)/shard_map/ppermute | solution.py:245
  106.9 3.0 %collective-permute-start.12 = (bf16[4,2,256,128]{3,2,1,0:T(8,128)(2,1)}, bf16[4,2,256,128]{3,2,1,0:T(8,128)(2,1)S(1)}, u32[]{:S(2)}, u32[]{:S(2)}) collective-permute-start(bf16[4,2,256,128]{3,2,1,0:T(8,128)(2,1)} %get-tuple-element.30), channel_id=1, source_target_pairs={{0,16},{2,18},{4,20},{6,22},{8,24},{10,26},{12,28},{14,30},{16,0},... | collective-permute-start | bytes 1572872 | tf_op jit(solution)/shard_map/ppermute | solution.py:238
  110.0 14.2 %collective-permute-done.13 = bf16[4,2,256,128]{3,2,1,0:T(8,128)(2,1)S(1)} collective-permute-done((bf16[4,2,256,128]{3,2,1,0:T(8,128)(2,1)S(1)}, bf16[4,2,256,128]{3,2,1,0:T(8,128)(2,1)S(1)}, u32[]{:S(2)}, u32[]{:S(2)}) %collective-permute-start.13) | collective-permute-done | bytes 524320 | tf_op jit(solution)/shard_map/ppermute | solution.py:238
  124.4 0.9 add_convert_fusion.1
  125.3 0.8 collective-permute-start.17
  126.1 0.9 add_convert_fusion
  127.0 5.2 %collective-permute-start.14 = (bf16[4,2,256,128]{3,2,1,0:T(8,128)(2,1)}, bf16[4,2,256,128]{3,2,1,0:T(8,128)(2,1)S(1)}, u32[]{:S(2)}, u32[]{:S(2)}) collective-permute-start(bf16[4,2,256,128]{3,2,1,0:T(8,128)(2,1)} %add_convert_fusion.1), channel_id=1, source_target_pairs={{0,64},{2,66},{4,68},{6,70},{8,72},{10,74},{12,76},{14,78},{16,80}... | collective-permute-start | bytes 1572872 | tf_op jit(solution)/shard_map/ppermute | solution.py:238
  132.3 23.7 %collective-permute-done.14.refs_6_ = bf16[4,2,256,128]{3,2,1,0:T(8,128)(2,1)S(1)} collective-permute-done((bf16[4,2,256,128]{3,2,1,0:T(8,128)(2,1)}, bf16[4,2,256,128]{3,2,1,0:T(8,128)(2,1)S(1)}, u32[]{:S(2)}, u32[]{:S(2)}) %collective-permute-start.14) | collective-permute-done | bytes 524320 | tf_op jit(solution)/shard_map/ppermute | solution.py:238
  156.0 1.2 copy-done.3
  157.2 1.2 copy-done.5
  158.4 3.8 %finish.1 = (bf16[4096,128]{1,0:T(8,128)(2,1)}, bf16[4096,128]{1,0:T(8,128)(2,1)}, bf16[1024,128]{1,0:T(8,128)(2,1)}, bf16[1024,128]{1,0:T(8,128)(2,1)}) custom-call(s32[2]{0:T(128)S(1)} %pad_add_fusion.scalars, bf16[4,1024,128]{2,1,0:T(8,128)(2,1)S(1)} %copy-done.3, bf16[4,1024,128]{2,1,0:T(8,128)(2,1)S(1)} %collective-permute-done.9.refs_1_, ...), custom_call_target="tpu_custom_call" | custom-call | tf_op jit(solution)/shard_map/finish/pallas_call | solution.py:335
  (39 shorter events, 1.1 us)
Async XLA Ops:
  1.5 1.2 copy-start
  2.8 1.2 copy-start.1
  4.0 0.9 copy-start.6
  5.0 0.9 copy-start.7
  5.9 46.9 %copy-start.9 = (s32[7]{0:T(128)S(1)}, s32[7]{0:T(128)}, u32[]{:S(2)}) copy-start(s32[7]{0:T(128)} %param.12) | copy-start | bytes 88
  5.9 46.9 %copy-start.8 = (s32[2,7]{1,0:T(2,128)S(1)}, s32[2,7]{1,0:T(2,128)}, u32[]{:S(2)}) copy-start(s32[2,7]{1,0:T(2,128)} %param.13) | copy-start | bytes 172
  9.0 65.4 %collective-permute-start.8 = (bf16[4,1040,128]{2,1,0:T(8,128)(2,1)}, bf16[4,1040,128]{2,1,0:T(8,128)(2,1)S(1)}, u32[]{:S(2)}, u32[]{:S(2)}) collective-permute-start(bf16[4,1040,128]{2,1,0:T(8,128)(2,1)} %get-tuple-element.24), channel_id=1, source_target_pairs={{0,1},{1,0},{2,3},{3,2},{4,5},{5,4},{6,7},{7,6},{8,9},{9,8},{10,11... | collective-permute-start | bytes 3194888 | tf_op jit(solution)/shard_map/ppermute | solution.py:249
  11.0 25.6 %collective-permute-start.6 = (bf16[4,2,256,128]{3,2,1,0:T(8,128)(2,1)S(1)}, bf16[4,2,256,128]{3,2,1,0:T(8,128)(2,1)S(1)}, u32[]{:S(2)}, u32[]{:S(2)}) collective-permute-start(bf16[4,2,256,128]{3,2,1,0:T(8,128)(2,1)S(1)} %get-tuple-element.22.refs_0_), channel_id=1, source_target_pairs={{0,64},{2,66},{4,68},{6,70},{8,72},{10,74},{12,76},{14,78},{16,80}... | collective-permute-start | bytes 1572872 | tf_op jit(solution)/shard_map/ppermute | solution.py:238
  14.0 31.3 %collective-permute-start.5 = (bf16[4,2,256,128]{3,2,1,0:T(8,128)(2,1)S(1)}, bf16[4,2,256,128]{3,2,1,0:T(8,128)(2,1)}, u32[]{:S(2)}, u32[]{:S(2)}) collective-permute-start(bf16[4,2,256,128]{3,2,1,0:T(8,128)(2,1)S(1)} %get-tuple-element.22.refs_0_), channel_id=1, source_target_pairs={{0,32},{2,34},{4,36},{6,38},{8,40},{10,42},{12,44},{14,46},{16,48}... | collective-permute-start | bytes 1572872 | tf_op jit(solution)/shard_map/ppermute | solution.py:238
  15.7 36.3 %collective-permute-start.2 = (bf16[4,2,256,128]{3,2,1,0:T(8,128)(2,1)S(1)}, bf16[4,2,256,128]{3,2,1,0:T(8,128)(2,1)}, u32[]{:S(2)}, u32[]{:S(2)}) collective-permute-start(bf16[4,2,256,128]{3,2,1,0:T(8,128)(2,1)S(1)} %get-tuple-element.22.refs_0_), channel_id=1, source_target_pairs={{0,4},{2,6},{4,0},{6,2},{8,12},{10,14},{12,8},{14,10},{16,20},{18,... | collective-permute-start | bytes 1572872 | tf_op jit(solution)/shard_map/ppermute | solution.py:238
  17.0 15.5 %collective-permute-start = (bf16[4,2,128,128]{3,2,1,0:T(8,128)(2,1)S(1)}, bf16[4,2,128,128]{3,2,1,0:T(8,128)(2,1)S(1)}, u32[]{:S(2)}, u32[]{:S(2)}) collective-permute-start(bf16[4,2,128,128]{3,2,1,0:T(8,128)(2,1)S(1)} %slice_select_fusion), channel_id=1, source_target_pairs={{2,4},{4,2},{6,8},{8,6},{10,12},{12,10},{14,16},{16,14},{18,20},{2... | collective-permute-start | bytes 786440 | tf_op jit(solution)/shard_map/ppermute | solution.py:245
  32.5 20.7 %collective-permute-start.4 = (bf16[4,2,256,128]{3,2,1,0:T(8,128)(2,1)S(1)}, bf16[4,2,256,128]{3,2,1,0:T(8,128)(2,1)}, u32[]{:S(2)}, u32[]{:S(2)}) collective-permute-start(bf16[4,2,256,128]{3,2,1,0:T(8,128)(2,1)S(1)} %get-tuple-element.22.refs_0_), channel_id=1, source_target_pairs={{0,16},{2,18},{4,20},{6,22},{8,24},{10,26},{12,28},{14,30},{16,0},... | collective-permute-start | bytes 1572872 | tf_op jit(solution)/shard_map/ppermute | solution.py:238
  36.6 16.6 %collective-permute-start.1 = (bf16[4,2,256,128]{3,2,1,0:T(8,128)(2,1)S(1)}, bf16[4,2,256,128]{3,2,1,0:T(8,128)(2,1)}, u32[]{:S(2)}, u32[]{:S(2)}) collective-permute-start(bf16[4,2,256,128]{3,2,1,0:T(8,128)(2,1)S(1)} %get-tuple-element.22.refs_0_), channel_id=1, source_target_pairs={{0,2},{2,0},{4,6},{6,4},{8,10},{10,8},{12,14},{14,12},{16,18},{18,... | collective-permute-start | bytes 1572872 | tf_op jit(solution)/shard_map/ppermute | solution.py:238
  45.3 29.1 %collective-permute-start.7 = (bf16[4,2,256,128]{3,2,1,0:T(8,128)(2,1)S(1)}, bf16[4,2,256,128]{3,2,1,0:T(8,128)(2,1)}, u32[]{:S(2)}, u32[]{:S(2)}) collective-permute-start(bf16[4,2,256,128]{3,2,1,0:T(8,128)(2,1)S(1)} %collective-permute-done.6.refs_7_), channel_id=1, source_target_pairs={{0,192},{2,194},{4,196},{6,198},{8,200},{10,202},{12,204},{14,206}... | collective-permute-start | bytes 1572872 | tf_op jit(solution)/shard_map/ppermute | solution.py:238
  51.9 22.5 %collective-permute-start.3 = (bf16[4,2,256,128]{3,2,1,0:T(8,128)(2,1)}, bf16[4,2,256,128]{3,2,1,0:T(8,128)(2,1)}, u32[]{:S(2)}, u32[]{:S(2)}) collective-permute-start(bf16[4,2,256,128]{3,2,1,0:T(8,128)(2,1)} %collective-permute-done.2.refs_3_), channel_id=1, source_target_pairs={{0,12},{2,14},{4,8},{6,10},{8,4},{10,6},{12,0},{14,2},{16,28},{18,... | collective-permute-start | bytes 1572872 | tf_op jit(solution)/shard_map/ppermute | solution.py:238
  99.5 27.6 %copy-start.2 = (bf16[4,1024,128]{2,1,0:T(8,128)(2,1)}, bf16[4,1024,128]{2,1,0:T(8,128)(2,1)S(1)}, u32[]{:S(2)}) copy-start(bf16[4,1024,128]{2,1,0:T(8,128)(2,1)S(1)} %get-tuple-element.25.refs_0_) | copy-start | bytes 3145732
  99.5 27.6 %copy-start.4 = (f32[4,2,256,128]{3,2,1,0:T(8,128)}, f32[4,2,256,128]{3,2,1,0:T(8,128)S(1)}, u32[]{:S(2)}) copy-start(f32[4,2,256,128]{3,2,1,0:T(8,128)S(1)} %get-tuple-element.27.refs_2_) | copy-start | bytes 3145732
  99.5 24.6 %collective-permute-start.13 = (bf16[4,2,256,128]{3,2,1,0:T(8,128)(2,1)S(1)}, bf16[4,2,256,128]{3,2,1,0:T(8,128)(2,1)S(1)}, u32[]{:S(2)}, u32[]{:S(2)}) collective-permute-start(bf16[4,2,256,128]{3,2,1,0:T(8,128)(2,1)S(1)} %get-tuple-element.32), channel_id=1, source_target_pairs={{0,192},{2,194},{4,196},{6,198},{8,200},{10,202},{12,204},{14,206}... | collective-permute-start | bytes 1572872 | tf_op jit(solution)/shard_map/ppermute | solution.py:238
  104.1 21.2 %collective-permute-start.15 = (bf16[4,2,256,128]{3,2,1,0:T(8,128)(2,1)S(1)}, bf16[4,2,256,128]{3,2,1,0:T(8,128)(2,1)S(1)}, u32[]{:S(2)}, u32[]{:S(2)}) collective-permute-start(bf16[4,2,256,128]{3,2,1,0:T(8,128)(2,1)S(1)} %get-tuple-element.34), channel_id=1, source_target_pairs={{0,12},{2,14},{4,8},{6,10},{8,4},{10,6},{12,0},{14,2},{16,28},{18,... | collective-permute-start | bytes 1572872 | tf_op jit(solution)/shard_map/ppermute | solution.py:238
  104.9 22.1 %collective-permute-start.10 = (bf16[4,2,128,128]{3,2,1,0:T(8,128)(2,1)S(1)}, bf16[4,2,128,128]{3,2,1,0:T(8,128)(2,1)S(1)}, u32[]{:S(2)}, u32[]{:S(2)}) collective-permute-start(bf16[4,2,128,128]{3,2,1,0:T(8,128)(2,1)S(1)} %get-tuple-element.28), channel_id=1, source_target_pairs={{2,4},{4,2},{6,8},{8,6},{10,12},{12,10},{14,16},{16,14},{18,20},{2... | collective-permute-start | bytes 786440 | tf_op jit(solution)/shard_map/ppermute | solution.py:245
  106.8 25.4 %collective-permute-start.11 = (bf16[4,2,256,128]{3,2,1,0:T(8,128)(2,1)S(1)}, bf16[4,2,256,128]{3,2,1,0:T(8,128)(2,1)S(1)}, u32[]{:S(2)}, u32[]{:S(2)}) collective-permute-start(bf16[4,2,256,128]{3,2,1,0:T(8,128)(2,1)S(1)} %get-tuple-element.29), channel_id=1, source_target_pairs={{0,32},{2,34},{4,36},{6,38},{8,40},{10,42},{12,44},{14,46},{16,48}... | collective-permute-start | bytes 1572872 | tf_op jit(solution)/shard_map/ppermute | solution.py:238
  106.9 25.4 %collective-permute-start.12 = (bf16[4,2,256,128]{3,2,1,0:T(8,128)(2,1)}, bf16[4,2,256,128]{3,2,1,0:T(8,128)(2,1)S(1)}, u32[]{:S(2)}, u32[]{:S(2)}) collective-permute-start(bf16[4,2,256,128]{3,2,1,0:T(8,128)(2,1)} %get-tuple-element.30), channel_id=1, source_target_pairs={{0,16},{2,18},{4,20},{6,22},{8,24},{10,26},{12,28},{14,30},{16,0},... | collective-permute-start | bytes 1572872 | tf_op jit(solution)/shard_map/ppermute | solution.py:238
  124.1 31.9 %collective-permute-start.9 = (bf16[4,1024,128]{2,1,0:T(8,128)(2,1)}, bf16[4,1024,128]{2,1,0:T(8,128)(2,1)S(1)}, u32[]{:S(2)}, u32[]{:S(2)}) collective-permute-start(bf16[4,1024,128]{2,1,0:T(8,128)(2,1)} %get-tuple-element.26), channel_id=1, source_target_pairs={{0,1},{1,0},{2,3},{3,2},{4,5},{5,4},{6,7},{7,6},{8,9},{9,8},{10,11... | collective-permute-start | bytes 3145736 | tf_op jit(solution)/shard_map/ppermute | solution.py:249
  125.3 7.0 %collective-permute-start.17 = (bf16[4,2,256,128]{3,2,1,0:T(8,128)(2,1)}, bf16[4,2,256,128]{3,2,1,0:T(8,128)(2,1)S(1)}, u32[]{:S(2)}, u32[]{:S(2)}) collective-permute-start(bf16[4,2,256,128]{3,2,1,0:T(8,128)(2,1)} %get-tuple-element.35), channel_id=1, source_target_pairs={{0,2},{2,0},{4,6},{6,4},{8,10},{10,8},{12,14},{14,12},{16,18},{18,... | collective-permute-start | bytes 1572872 | tf_op jit(solution)/shard_map/ppermute | solution.py:238
  127.0 28.9 %collective-permute-start.14 = (bf16[4,2,256,128]{3,2,1,0:T(8,128)(2,1)}, bf16[4,2,256,128]{3,2,1,0:T(8,128)(2,1)S(1)}, u32[]{:S(2)}, u32[]{:S(2)}) collective-permute-start(bf16[4,2,256,128]{3,2,1,0:T(8,128)(2,1)} %add_convert_fusion.1), channel_id=1, source_target_pairs={{0,64},{2,66},{4,68},{6,70},{8,72},{10,74},{12,76},{14,78},{16,80}... | collective-permute-start | bytes 1572872 | tf_op jit(solution)/shard_map/ppermute | solution.py:238
  132.2 23.7 %collective-permute-start.16 = (bf16[4,2,256,128]{3,2,1,0:T(8,128)(2,1)}, bf16[4,2,256,128]{3,2,1,0:T(8,128)(2,1)}, u32[]{:S(2)}, u32[]{:S(2)}) collective-permute-start(bf16[4,2,256,128]{3,2,1,0:T(8,128)(2,1)} %add_convert_fusion), channel_id=1, source_target_pairs={{0,4},{2,6},{4,0},{6,2},{8,12},{10,14},{12,8},{14,10},{16,20},{18,... | collective-permute-start | bytes 1572872 | tf_op jit(solution)/shard_map/ppermute | solution.py:238
  156.0 1.2 copy-start.3
  157.2 1.2 copy-start.5

commit v2 on v1

v2 whole, which is shorter than its diff:
```python
import functools
import math

import jax
import jax.numpy as jnp
from jax import lax
from jax.experimental import pallas as pl
from jax.experimental.pallas import tpu as pltpu
from jax.sharding import PartitionSpec as P

BLOCK = 128
HEAD_DIM = 128
CHUNKS = 2
LOCAL_HEADS = 4
PER = LOCAL_HEADS // CHUNKS
LEVELS = 7
BAND_SLOTS = 3
SLOTS = BAND_SLOTS + LEVELS
ROWS = 512
PAD = 8
PACK_MIB = 56
SIDES_MIB = 52
NEG = -1e30
F32 = jnp.float32
BF16 = jnp.bfloat16
WHOLE = pl.BlockSpec(memory_space=pltpu.VMEM)
FAR = pl.BlockSpec(memory_space=pltpu.HBM)
SCALARS = pl.BlockSpec(memory_space=pltpu.SMEM)


def vmem(mib):
    return pltpu.CompilerParams(vmem_limit_bytes=mib << 20)


def dot(lhs, rhs, lhs_dim, rhs_dim):
    return lax.dot_general(
        lhs, rhs, (((lhs_dim,), (rhs_dim,)), ((), ())), preferred_element_type=F32
    )


def query_order(place, rows_first):
    ordered = lax.broadcasted_iota(jnp.int32, (256, 256), rows_first)
    natural = lax.broadcasted_iota(jnp.int32, (256, 256), 1 - rows_first)
    source = (ordered & 15) * 16 + ((ordered >> 4) ^ (place * 8))
    return (natural == source).astype(BF16)


def key_order(rows_first):
    ordered = lax.broadcasted_iota(jnp.int32, (256, 256), rows_first)
    natural = lax.broadcasted_iota(jnp.int32, (256, 256), 1 - rows_first)
    return (natural == (ordered & 63) * 4 + (ordered >> 6)).astype(BF16)


def pieces_of(ref, store, sems, count):
    rows = ref.shape[0] // count
    copies = [
        pltpu.make_async_copy(
            ref.at[pl.ds(i * rows, rows)], store.at[pl.ds(i * rows, rows)], sems.at[i]
        )
        for i in range(count)
    ]
    for copy in copies:
        copy.start()
    return copies


def pack_pairs_kernel(scalars, key, value, *refs):
    whole, first, second, ends, key_in, value_in, sems = refs
    even = scalars[0] == 0
    copies = [
        pieces_of(ref, store, sems.at[member], 2)
        for member, (ref, store) in enumerate(((key, key_in), (value, value_in)))
    ]
    order = key_order(0)
    for block in range(2):
        for member, store in enumerate((key_in, value_in)):
            copies[member][block].wait()
            for inner in (0, 64):
                start = block * 512 + inner * 4
                rows = dot(order, store[start : start + 256], 1, 0).astype(BF16)
                span = slice(block * BLOCK + inner, block * BLOCK + inner + 64)
                end = slice(inner, inner + 64)
                for head in range(LOCAL_HEADS):
                    piece = rows[head * 64 : head * 64 + 64]
                    whole[head, member, span] = piece
                    (first, second)[head // PER][head % PER, member, span] = piece
                    if block == 0:
                        ends[head, member, end] = piece
                    else:
                        ends[head, member, end] = jnp.where(even, ends[head, member, end], piece)


def pack_sides_kernel(scalars, query, grad, unused, *refs):
    place = scalars[0]
    keeps, sends = refs[:CHUNKS], refs[CHUNKS : 2 * CHUNKS]
    stores, sems = refs[2 * CHUNKS : 2 * CHUNKS + 2], refs[2 * CHUNKS + 2]
    copies = [
        pieces_of(ref, store, sems.at[member], 4)
        for member, (ref, store) in enumerate(zip((query, grad), stores))
    ]
    order = query_order(place, 0)
    for part in range(16):
        for member, store in enumerate(stores):
            if part % 4 == 0:
                copies[member][part // 4].wait()
            rows = dot(order, store[part * 256 : part * 256 + 256], 1, 0).astype(BF16)
            block, inner = part // 8, (part % 8) * 16
            for head in range(2 * LOCAL_HEADS):
                target = (keeps, sends)[head // LOCAL_HEADS]
                local = head % LOCAL_HEADS
                for group in range(2):
                    start = (member * 2 + block) * 256 + group * 128 + inner
                    first = (head * 2 + group) * 16
                    target[local // PER][local % PER, start : start + 16] = rows[first : first + 16]
    sublane = lax.broadcasted_iota(jnp.int32, (16, HEAD_DIM), 0)
    for head in range(2 * LOCAL_HEADS):
        target = (keeps, sends)[head // LOCAL_HEADS]
        local = head % LOCAL_HEADS
        actual = head ^ (place * LOCAL_HEADS)
        width = jnp.where(sublane == 0, scalars[1 + actual * 2], scalars[2 + actual * 2])
        target[local // PER][local % PER, 1024:1040] = width.astype(F32).astype(BF16)


def attend_kernel(base, reused, scalars, *refs):
    own, ext = refs[:2]
    arrived = refs[2 : 2 + LEVELS]
    sides = refs[2 + LEVELS : 4 + LEVELS]
    refs = refs[4 + LEVELS + reused :]
    side_outs, terms_out, ext_out = refs[:2], refs[2], refs[3]
    level_outs = refs[4 : 4 + LEVELS]
    (scores, exps, dscores, pairs, side_in, side_store, acc, ext_store, level_store) = refs[
        4 + LEVELS : 13 + LEVELS
    ]
    pair_sems, side_sems, out_sems = refs[13 + LEVELS :]
    device = scalars[0]
    last = scalars[1]
    even = (device & 1) == 0
    odd = jnp.logical_not(even)
    scale = HEAD_DIM**-0.5
    log_scale = scale * math.log2(math.e)

    def chosen(block, level):
        return scalars[2 + block * LEVELS + level]

    def at_head(ref, head):
        return ref.at[head + base if ref.shape[0] == LOCAL_HEADS else head]

    def copy_pair(head, block, source, slot, count):
        unit = head * 2 + block
        return pltpu.make_async_copy(
            source,
            pairs.at[unit, :, pl.ds(slot * BLOCK, count * BLOCK)],
            pair_sems.at[unit],
        )

    def side_copies(head):
        return [
            pltpu.make_async_copy(sides[i].at[head], side_in.at[head, i], side_sems.at[head, i])
            for i in range(2)
        ]

    for head in range(PER):
        for copy in side_copies(head):
            copy.start()
        for block in range(2):
            side = 1 - block
            from_ext = even if block == 0 else odd
            copy_pair(head, block, at_head(own, head), 0, 2).start()
            pl.when(from_ext)(copy_pair(head, block, at_head(ext, head), 2, 1).start)
            nearby = at_head(arrived[0], head).at[:, pl.ds(side * BLOCK, BLOCK)]
            pl.when(jnp.logical_not(from_ext))(copy_pair(head, block, nearby, 2, 1).start)
            for level in range(LEVELS):
                at = pl.ds(pl.multiple_of(chosen(block, level) * BLOCK, BLOCK), BLOCK)
                source = at_head(arrived[level], head).at[:, at]
                copy_pair(head, block, source, BAND_SLOTS + level, 1).start()

    def out_copies(head):
        copies = [(side_store.at[head, i], side_outs[i].at[head]) for i in range(2)]
        copies.append((acc.at[head, :, pl.ds(0, 2 * BLOCK)], at_head(terms_out, head)))
        copies.append((ext_store.at[head], at_head(ext_out, head)))
        copies += [
            (level_store.at[head, level], at_head(level_outs[level], head).at[:, pl.ds(0, 2 * BLOCK)])
            for level in range(LEVELS)
        ]
        return [
            pltpu.make_async_copy(source, target, out_sems.at[head, i])
            for i, (source, target) in enumerate(copies)
        ]

    def one_head(head, carry):
        acc[head] = jnp.zeros(acc.shape[1:], F32)
        for copy in side_copies(head):
            copy.wait()
        widths = jnp.concatenate(
            [
                side_in[head, i, 1024:1040].astype(F32)[group : group + 1]
                for i in range(2)
                for group in range(2)
            ],
            axis=1,
        )
        width_bias = jnp.where(widths > 1.5, 0.0, NEG)
        for block in range(2):
            unit = head * 2 + block
            side = 1 - block
            outer_valid = device > 0 if block == 0 else device < last
            from_ext = even if block == 0 else odd
            query_t, grad_t = (
                jnp.concatenate(
                    [
                        jnp.transpose(
                            side_in[
                                head,
                                i,
                                (member * 2 + block) * 256 : (member * 2 + block) * 256 + 256,
                            ]
                        )
                        for i in range(2)
                    ],
                    axis=1,
                )
                for member in range(2)
            )
            copy_pair(head, block, at_head(own, head), 0, 2).wait()
            for slot in range(2, SLOTS):
                copy_pair(head, block, at_head(ext, head), slot, 1).wait()
            keys, values = pairs.at[unit, 0], pairs.at[unit, 1]
            outer_bias = width_bias + jnp.where(outer_valid, 0.0, NEG)
            peak = jnp.full((8, ROWS), NEG, F32)
            for slot in range(SLOTS):
                span = slice(slot * BLOCK, slot * BLOCK + BLOCK)
                part = dot(keys[span], query_t, 1, 0)
                if slot == side:
                    part = part + width_bias
                if slot == 2:
                    part = part + outer_bias
                scores[span] = part
                peak = jnp.maximum(peak, jnp.max(part.reshape(BLOCK // 8, 8, ROWS), axis=0))
            peak = jnp.max(peak, axis=0, keepdims=True) * log_scale
            total = jnp.zeros((8, ROWS), F32)
            for slot in range(SLOTS):
                span = slice(slot * BLOCK, slot * BLOCK + BLOCK)
                part = jnp.exp2(scores[span] * log_scale - peak)
                total = total + jnp.sum(part.reshape(BLOCK // 8, 8, ROWS), axis=0)
                exps[span] = part.astype(BF16)
            inverse = 1.0 / jnp.sum(total, axis=0, keepdims=True)
            out_t = (dot(values[...], exps[...], 0, 0) * inverse).astype(BF16)
            grad_t = (grad_t.astype(F32) * inverse).astype(BF16)
            delta = jnp.sum(out_t.astype(F32) * grad_t.astype(F32), axis=0, keepdims=True)
            for slot in range(SLOTS):
                span = slice(slot * BLOCK, slot * BLOCK + BLOCK)
                part = dot(values[span], grad_t, 1, 0)
                dscores[span] = (exps[span].astype(F32) * (part - delta)).astype(BF16)
            dquery_t = (dot(keys[...], dscores[...], 0, 0) * scale).astype(BF16)
            for member, rows_t in enumerate((out_t, dquery_t)):
                first = (member * 2 + block) * 256
                for i in range(2):
                    side_store[head, i, first : first + 256] = jnp.transpose(
                        rows_t[:, i * 256 : i * 256 + 256]
                    )
            outer_row = jnp.where(from_ext, 2, 3 + side)
            for member, (lhs, rhs, factor) in enumerate(
                ((dscores, query_t, scale), (exps, grad_t, None))
            ):
                terms = dot(lhs[...], rhs, 1, 1)
                if factor is not None:
                    terms = terms * factor
                acc[head, member, 0 : 2 * BLOCK] += terms[0 : 2 * BLOCK]
                targets = [outer_row] + [
                    3 + 2 * level + chosen(block, level) for level in range(LEVELS)
                ]
                for slot, row in enumerate(targets):
                    at = pl.ds(pl.multiple_of(row * BLOCK, BLOCK), BLOCK)
                    first = (2 + slot) * BLOCK
                    acc[head, member, at] += terms[first : first + BLOCK]
        for member in range(2):
            ext_store[head, member] = acc[head, member, 2 * BLOCK : 3 * BLOCK].astype(BF16)
            for level in range(LEVELS):
                first = (3 + 2 * level) * BLOCK
                level_store[head, level, member] = acc[
                    head, member, first : first + 2 * BLOCK
                ].astype(BF16)
        for copy in out_copies(head):
            copy.start()
        return carry

    lax.fori_loop(0, PER, one_head, 0)
    for head in range(PER):
        for copy in out_copies(head):
            copy.wait()


def finish_sides_kernel(scalars, *refs):
    sources, targets = refs[:-2], refs[-2:]
    order = query_order(scalars[0], 1)
    for member, target in enumerate(targets):
        for part in range(16):
            block, inner = part // 8, (part % 8) * 16
            pieces = []
            for head in range(2 * LOCAL_HEADS):
                local = head % LOCAL_HEADS
                source = sources[(head // LOCAL_HEADS) * CHUNKS + local // PER]
                for group in range(2):
                    start = (member * 2 + block) * 256 + group * 128 + inner
                    pieces.append(source[local % PER, start : start + 16])
            rows = jnp.concatenate(pieces, axis=0)
            target[part * 256 : part * 256 + 256] = dot(order, rows, 1, 0).astype(BF16)


def finish_pairs_kernel(scalars, *refs):
    even = scalars[0] == 0
    count = (len(refs) - 3) // 2
    far, targets, ins, sems = refs[:count], refs[count : count + 2], refs[count + 2 : -1], refs[-1]
    copies = [
        pltpu.make_async_copy(source, store, sems.at[i])
        for i, (source, store) in enumerate(zip(far, ins))
    ]
    for copy in copies:
        copy.start()
    for copy in copies:
        copy.wait()
    beyond, whole, split = ins[0], ins[1:5], ins[5:]
    order = key_order(1)
    for member, target in enumerate(targets):
        for part in range(4):
            span = slice(part * 64, part * 64 + 64)
            inner = slice((part % 2) * 64, (part % 2) * 64 + 64)
            pieces = []
            for head in range(LOCAL_HEADS):
                total = beyond[head, member, inner].astype(F32)
                total = jnp.where(even if part < 2 else jnp.logical_not(even), total, 0.0)
                for ref in whole:
                    total = total + ref[head, member, span].astype(F32)
                for ref in split[head // PER :: CHUNKS]:
                    total = total + ref[head % PER, member, span].astype(F32)
                pieces.append(total.astype(BF16))
            rows = jnp.concatenate(pieces, axis=0)
            target[part * 256 : part * 256 + 256] = dot(order, rows, 1, 0).astype(BF16)


def flipped(value, mask):
    return lax.ppermute(value, "seq", [(i, i ^ mask) for i in range(lax.axis_size("seq"))])


def past_end(value):
    pairs = []
    for i in range(1, lax.axis_size("seq") - 1, 2):
        pairs += [(i, i + 1), (i + 1, i)]
    return lax.ppermute(value, "seq", pairs)


def other_head(value):
    return lax.ppermute(value, "head", [(0, 1), (1, 0)])


def added(first, second):
    return (first.astype(F32) + second.astype(F32)).astype(BF16)


def shards(query, key_in, value, grad_out, band_width, stride_bits, partner_table):
    rows = key_in.shape[0]
    device = lax.axis_index("seq").astype(jnp.int32)
    place = lax.axis_index("head").astype(jnp.int32)
    odd = device & 1
    match = (stride_bits[None, :] == jnp.arange(LEVELS, dtype=jnp.int32)[:, None]).astype(jnp.int32)
    chosen = jnp.sum(partner_table[:, None, :] * match[None], axis=2)
    scalars = jnp.concatenate(
        [device[None], jnp.full((1,), lax.axis_size("seq") - 1, jnp.int32), chosen.reshape(-1)]
    )

    whole = jax.ShapeDtypeStruct((LOCAL_HEADS, 2, rows, HEAD_DIM), BF16)
    pair = jax.ShapeDtypeStruct((PER, 2, rows, HEAD_DIM), BF16)
    padded = jax.ShapeDtypeStruct((PER, 2, rows + PAD, HEAD_DIM), BF16)
    terms = jax.ShapeDtypeStruct((PER, 2, rows, HEAD_DIM), F32)
    ends = jax.ShapeDtypeStruct((LOCAL_HEADS, 2, BLOCK, HEAD_DIM), BF16)
    sides = jax.ShapeDtypeStruct((PER, 1040, HEAD_DIM), BF16)
    half = jax.ShapeDtypeStruct((PER, 1024, HEAD_DIM), BF16)

    own, own_a, own_b, own_end = pl.pallas_call(
        pack_pairs_kernel,
        out_shape=[whole, padded, padded, ends],
        in_specs=[SCALARS] + [FAR] * 2,
        out_specs=[WHOLE] * 4,
        scratch_shapes=[pltpu.VMEM((rows * 4, HEAD_DIM), BF16)] * 2
        + [pltpu.SemaphoreType.DMA((2, 2))],
        compiler_params=vmem(PACK_MIB),
        name="pack_pairs",
    )(odd[None], key_in.reshape(-1, HEAD_DIM), value.reshape(-1, HEAD_DIM))

    z2_a = flipped(own_a, 32)
    z1 = flipped(own, 16)
    y1 = flipped(own, 2)
    core = flipped(own, 1)
    x = flipped(own, 8)
    keep_a, keep_b, send_a, send_b = pl.pallas_call(
        pack_sides_kernel,
        out_shape=[sides] * (2 * CHUNKS),
        in_specs=[SCALARS] + [FAR] * 3,
        out_specs=[WHOLE] * (2 * CHUNKS),
        scratch_shapes=[pltpu.VMEM((rows * 16, HEAD_DIM), BF16)] * 2
        + [pltpu.SemaphoreType.DMA((2, 4))],
        compiler_params=vmem(SIDES_MIB),
        name="pack_sides",
    )(
        jnp.concatenate([place[None], band_width.reshape(-1)]),
        query.reshape(-1, HEAD_DIM),
        grad_out.reshape(-1, HEAD_DIM),
        core,
    )
    to_z2, to_ext, to_head = lax.optimization_barrier((own_b, own_end, send_a, z1, x, z2_a))[:3]
    z6_a = flipped(z2_a, 96)
    z2_b = flipped(to_z2, 32)
    other_a = other_head(to_head)
    y3 = flipped(y1, 6)
    ext = past_end(to_ext)
    to_head = lax.optimization_barrier((send_b, z2_b, z6_a, other_a, y3, ext))[0]
    z6_b = flipped(z2_b, 96)
    other_b = other_head(to_head)

    def attend(chunk, keep, other, z2, z6, reused):
        ins = [scalars, own, ext, core, y1, y3, x, z1, z2, z6, keep, other, *reused]
        outs = [half, half, terms, ends, *[whole] * 5, padded, padded]
        return pl.pallas_call(
            functools.partial(attend_kernel, chunk * PER, len(reused)),
            out_shape=outs,
            in_specs=[SCALARS] + [FAR] * (len(ins) - 1),
            out_specs=[FAR] * len(outs),
            scratch_shapes=[
                pltpu.VMEM((SLOTS * BLOCK, ROWS), F32),
                pltpu.VMEM((SLOTS * BLOCK, ROWS), BF16),
                pltpu.VMEM((SLOTS * BLOCK, ROWS), BF16),
                pltpu.VMEM((2 * PER, 2, SLOTS * BLOCK, HEAD_DIM), BF16),
                pltpu.VMEM((PER, 2, 1040, HEAD_DIM), BF16),
                pltpu.VMEM((PER, 2, 1024, HEAD_DIM), BF16),
                pltpu.VMEM((PER, 2, (3 + 2 * LEVELS) * BLOCK, HEAD_DIM), F32),
                pltpu.VMEM((PER, 2, BLOCK, HEAD_DIM), BF16),
                pltpu.VMEM((PER, LEVELS, 2, rows, HEAD_DIM), BF16),
                pltpu.SemaphoreType.DMA((2 * PER,)),
                pltpu.SemaphoreType.DMA((PER, 2)),
                pltpu.SemaphoreType.DMA((PER, 4 + LEVELS)),
            ],
            input_output_aliases={12 + i: 3 + i for i in range(len(reused))},
            compiler_params=vmem(18),
            cost_estimate=pl.CostEstimate(
                flops=PER * 2 * 12 * SLOTS * BLOCK * ROWS * HEAD_DIM,
                transcendentals=PER * 2 * SLOTS * BLOCK * ROWS,
                bytes_accessed=PER * 24 * rows * HEAD_DIM * 4,
            ),
            name="attend",
        )(*ins)

    first = attend(0, keep_a, other_a, z2_a, z6_a, [])
    keep_out_a, other_out_a, terms_a = first[:3]
    z2_terms_a, z4_terms_a = first[9:]
    far_a = flipped(z4_terms_a, 96)
    swapped_a = other_head(other_out_a)
    second = attend(1, keep_b, other_b, z2_b, z6_b, first[3:9])
    keep_out_b, other_out_b, terms_b, ext_terms, core_terms, y1_terms, y2_terms = second[:7]
    x_terms, z1_terms, z2_terms_b, z4_terms_b = second[7:]
    to_z6, to_y3, to_x, to_ext, far_a, swapped_a = lax.optimization_barrier(
        (z4_terms_b, y2_terms, x_terms, ext_terms, far_a, swapped_a)
    )
    far_b = flipped(to_z6, 96)
    back_z2_a = flipped(added(z2_terms_a, far_a), 32)
    near = flipped(to_y3, 6)
    back_x = flipped(to_x, 8)
    back_ext = past_end(to_ext)
    far_b, back_z2_a, near, back_x, back_ext, z1_terms, core_terms, other_out_b = (
        lax.optimization_barrier(
            (far_b, back_z2_a, near, back_x, back_ext, z1_terms, core_terms, other_out_b)
        )
    )
    back_z2_b = flipped(added(z2_terms_b, far_b), 32)
    back_y = flipped(added(y1_terms, near), 2)
    swapped_b = other_head(other_out_b)
    back_z1 = flipped(z1_terms, 16)
    back_core = flipped(core_terms, 1)

    out, dquery = pl.pallas_call(
        finish_sides_kernel,
        out_shape=[jax.ShapeDtypeStruct((rows * 16, HEAD_DIM), BF16)] * 2,
        in_specs=[SCALARS] + [WHOLE] * (2 * CHUNKS),
        out_specs=[WHOLE] * 2,
        compiler_params=vmem(8),
        name="finish_sides",
    )(place[None], keep_out_a, keep_out_b, swapped_a, swapped_b)
    sums = [back_ext, back_core, back_y, back_x, back_z1]
    sums += [terms_a, terms_b, back_z2_a, back_z2_b]
    dkey, dvalue = pl.pallas_call(
        finish_pairs_kernel,
        out_shape=[jax.ShapeDtypeStruct((rows * 4, HEAD_DIM), BF16)] * 2,
        in_specs=[SCALARS] + [FAR] * len(sums),
        out_specs=[WHOLE] * 2,
        scratch_shapes=[pltpu.VMEM(part.shape, part.dtype) for part in sums]
        + [pltpu.SemaphoreType.DMA((len(sums),))],
        compiler_params=vmem(16),
        name="finish_pairs",
    )(odd[None], *sums)
    return (
        out.reshape(query.shape),
        dquery.reshape(query.shape),
        dkey.reshape(key_in.shape),
        dvalue.reshape(key_in.shape),
    )


def solution(mesh):
    placed = (
        P("seq", None, "head", None),
        P("seq", "head", None),
        P("seq", "head", None),
        P("seq", None, "head", None),
        P(None, "head"),
        P(),
        P("seq", None),
    )
    return jax.shard_map(
        shards,
        mesh=mesh,
        in_specs=placed,
        out_specs=(
            P("seq", None, "head", None),
            P("seq", None, "head", None),
            P("seq", "head", None),
            P("seq", "head", None),
        ),
        check_vma=False,
    )
```

time: 163 us -> 142 us (0.87)
  waiting for transfers between devices: 72.4 us -> 46 us
  Pallas kernels: 31.9 us -> 44.8 us
  local copies, waits for them, and re-layouts: 7.83 us -> 2.86 us
  other arithmetic: 2.37 us -> 0.65 us
    ppermute x14 -> x18, waiting for transfers between devices: 60.7 us -> 33.5 us  [flipped(): lax.ppermute(value, 'seq', [(i, i ^ mask) for i in range(lax.axis_size('s...]
    pallas_call x3 -> x6, Pallas kernels: 31.9 us -> 44.8 us  [the longest x2 32.6 us: attend(): pl.pallas_call(functools.partial(attend_kernel, chunk * PER, len(reused))...]
    ppermute x2 -> x4, waiting for transfers between devices: 0.01 us -> 6.39 us  [other_head(): return lax.ppermute(value, 'head', [(0, 1), (1, 0)])]
    ppermute x2, waiting for transfers between devices: 11.8 us -> 6.06 us  [past_end(): return lax.ppermute(value, 'seq', pairs)]
    unnamed x21 -> x13, local copies, waits for them, and re-layouts: 7.57 us -> 2.6 us
    ppermute x14 -> x18, starting transfers between devices: 39 us -> 38.9 us  [flipped(): lax.ppermute(value, 'seq', [(i, i ^ mask) for i in range(lax.axis_size('s...]
  transfers between devices with their start and end apart: 18 -> 24, of which waited for: 5 -> 10; matrix products, arithmetic and copies ran while one was open for 2% -> 1% of each run, Pallas kernels for 0% -> 28%
where the time goes in v2:
time: 142 us; the launch traced here: 141 us
  starting transfers between devices  46.1 us (32%)
  waiting for transfers between devices  46 us (32%)
  Pallas kernels  44.8 us (32%)
  local copies, waits for them, and re-layouts  2.86 us (2%)
    ppermute x18, starting transfers between devices, flipped(): lax.ppermute(value, 'seq', [(i, i ^ mask) for i in range(lax.axis_size('s...  38.9 us
    ppermute x18, waiting for transfers between devices, flipped(): lax.ppermute(value, 'seq', [(i, i ^ mask) for i in range(lax.axis_size('s...  33.5 us
    pallas_call x2, Pallas kernels, attend(): pl.pallas_call(functools.partial(attend_kernel, chunk * PER, len(reused))...  32.6 us
    ppermute x4, waiting for transfers between devices, other_head(): return lax.ppermute(value, 'head', [(0, 1), (1, 0)])  6.39 us
    ppermute x2, waiting for transfers between devices, past_end(): return lax.ppermute(value, 'seq', pairs)  6.06 us
    ppermute x2, starting transfers between devices, past_end(): return lax.ppermute(value, 'seq', pairs)  5.58 us
    pallas_call x1, Pallas kernels, shards(): pl.pallas_call(pack_sides_kernel, out_shape=[sides] * (2 * CHUNKS), in_sp...  5.13 us
  transfers between devices with their start and end apart: 24, of which 10 were waited for; matrix products, arithmetic and copies ran while one was open for 1% of the time, Pallas kernels for 28%

profile of v2, /device:TPU:1, one launch (start us, length us, event | category | flops | bytes accessed | tf_op | source)
XLA Modules:
  0.0 141.3 jit_solution(6479579914444762732)
XLA Ops:
  0.6 2.8 %pack_pairs.1 = (bf16[4,2,256,128]{3,2,1,0:T(8,128)(2,1)}, bf16[2,2,264,128]{3,2,1,0:T(8,128)(2,1)}, bf16[2,2,264,128]{3,2,1,0:T(8,128)(2,1)}, bf16[4,2,128,128]{3,2,1,0:T(8,128)(2,1)}) custom-call(s32[1]{0:T(128)} %bitcast.2.scalars, bf16[1024,128]{1,0:T(8,128)(2,1)} %bitcast.13, bf16[1024,128]{1,0:T(8,128)(2,1)} %bitcast.14), custom_call_target="tpu_custom_call" | custom-call | tf_op jit(solution)/shard_map/pack_pairs/pallas_call | solution.py:379
  3.5 3.3 %collective-permute-start = (bf16[4,2,256,128]{3,2,1,0:T(8,128)(2,1)}, bf16[4,2,256,128]{3,2,1,0:T(8,128)(2,1)S(1)}, u32[]{:S(2)}, u32[]{:S(2)}) collective-permute-start(bf16[4,2,256,128]{3,2,1,0:T(8,128)(2,1)} %get-tuple-element.56.refs_0_), channel_id=1, source_target_pairs={{0,2},{2,0},{4,6},{6,4},{8,10},{10,8},{12,14},{14,12},{16,18},{18,... | collective-permute-start | bytes 1572872 | tf_op jit(solution)/shard_map/ppermute | solution.py:342
  6.8 1.0 collective-permute-start.2
  7.8 1.6 %collective-permute-start.1 = (bf16[4,2,256,128]{3,2,1,0:T(8,128)(2,1)}, bf16[4,2,256,128]{3,2,1,0:T(8,128)(2,1)S(1)}, u32[]{:S(2)}, u32[]{:S(2)}) collective-permute-start(bf16[4,2,256,128]{3,2,1,0:T(8,128)(2,1)} %get-tuple-element.56.refs_0_), channel_id=1, source_target_pairs={{0,32},{2,34},{4,36},{6,38},{8,40},{10,42},{12,44},{14,46},{16,48}... | collective-permute-start | bytes 1572872 | tf_op jit(solution)/shard_map/ppermute | solution.py:342
  9.5 1.3 collective-permute-start.5
  10.8 3.0 %collective-permute-start.3 = (bf16[2,2,264,128]{3,2,1,0:T(8,128)(2,1)}, bf16[2,2,264,128]{3,2,1,0:T(8,128)(2,1)S(1)}, u32[]{:S(2)}, u32[]{:S(2)}) collective-permute-start(bf16[2,2,264,128]{3,2,1,0:T(8,128)(2,1)} %get-tuple-element.60), channel_id=1, source_target_pairs={{0,64},{2,66},{4,68},{6,70},{8,72},{10,74},{12,76},{14,78},{16,80}... | collective-permute-start | bytes 811016 | tf_op jit(solution)/shard_map/ppermute | solution.py:342
  14.7 5.1 %pack_sides.1 = (bf16[2,1040,128]{2,1,0:T(8,128)(2,1)S(1)}, bf16[2,1040,128]{2,1,0:T(8,128)(2,1)S(1)}, bf16[2,1040,128]{2,1,0:T(8,128)(2,1)}, bf16[2,1040,128]{2,1,0:T(8,128)(2,1)}) custom-call(s32[17]{0:T(128)S(1)} %pad_add_fusion.1.scalars, bf16[4096,128]{1,0:T(8,128)(2,1)} %bitcast.11, bf16[4096,128]{1,0:T(8,128)(2,1)} %bitcast.12, ...), custom_call_target="tpu_custom_call" | custom-call | tf_op jit(solution)/shard_map/pack_sides/pallas_call | solution.py:395
  19.8 6.7 %collective-permute-done.3.refs_7_ = bf16[2,2,264,128]{3,2,1,0:T(8,128)(2,1)S(1)} collective-permute-done((bf16[2,2,264,128]{3,2,1,0:T(8,128)(2,1)}, bf16[2,2,264,128]{3,2,1,0:T(8,128)(2,1)S(1)}, u32[]{:S(2)}, u32[]{:S(2)}) %collective-permute-start.3) | collective-permute-done | bytes 270368 | tf_op jit(solution)/shard_map/ppermute | solution.py:342
  28.5 2.7 %collective-permute-start.6 = (bf16[4,2,256,128]{3,2,1,0:T(8,128)(2,1)}, bf16[4,2,256,128]{3,2,1,0:T(8,128)(2,1)}, u32[]{:S(2)}, u32[]{:S(2)}) collective-permute-start(bf16[4,2,256,128]{3,2,1,0:T(8,128)(2,1)} %collective-permute-done.5.refs_3_), channel_id=1, source_target_pairs={{0,12},{2,14},{4,8},{6,10},{8,4},{10,6},{12,0},{14,2},{16,28},{18,... | collective-permute-start | bytes 1572872 | tf_op jit(solution)/shard_map/ppermute | solution.py:342
  31.3 6.0 %collective-permute-start.7 = (bf16[2,2,264,128]{3,2,1,0:T(8,128)(2,1)S(1)}, bf16[2,2,264,128]{3,2,1,0:T(8,128)(2,1)}, u32[]{:S(2)}, u32[]{:S(2)}) collective-permute-start(bf16[2,2,264,128]{3,2,1,0:T(8,128)(2,1)S(1)} %collective-permute-done.3.refs_7_), channel_id=1, source_target_pairs={{0,192},{2,194},{4,196},{6,198},{8,200},{10,202},{12,204},{14,206}... | collective-permute-start | bytes 811016 | tf_op jit(solution)/shard_map/ppermute | solution.py:342
  37.3 3.7 %collective-permute-start.4 = (bf16[4,2,128,128]{3,2,1,0:T(8,128)(2,1)}, bf16[4,2,128,128]{3,2,1,0:T(8,128)(2,1)}, u32[]{:S(2)}, u32[]{:S(2)}) collective-permute-start(bf16[4,2,128,128]{3,2,1,0:T(8,128)(2,1)} %get-tuple-element.61), channel_id=1, source_target_pairs={{2,4},{4,2},{6,8},{8,6},{10,12},{12,10},{14,16},{16,14},{18,20},{2... | collective-permute-start | bytes 786440 | tf_op jit(solution)/shard_map/ppermute | solution.py:349
  42.2 7.2 %collective-permute-done.7.refs_8_ = bf16[2,2,264,128]{3,2,1,0:T(8,128)(2,1)} collective-permute-done((bf16[2,2,264,128]{3,2,1,0:T(8,128)(2,1)S(1)}, bf16[2,2,264,128]{3,2,1,0:T(8,128)(2,1)}, u32[]{:S(2)}, u32[]{:S(2)}) %collective-permute-start.7) | collective-permute-done | bytes 270368 | tf_op jit(solution)/shard_map/ppermute | solution.py:342
  49.3 3.7 %collective-permute-done.9.refs_7_ = bf16[2,2,264,128]{3,2,1,0:T(8,128)(2,1)} collective-permute-done((bf16[2,2,264,128]{3,2,1,0:T(8,128)(2,1)}, bf16[2,2,264,128]{3,2,1,0:T(8,128)(2,1)}, u32[]{:S(2)}, u32[]{:S(2)}) %collective-permute-start.9) | collective-permute-done | bytes 270368 | tf_op jit(solution)/shard_map/ppermute | solution.py:342
  53.0 1.2 collective-permute-start.11
  54.3 2.5 %collective-permute-start.10 = (bf16[2,2,264,128]{3,2,1,0:T(8,128)(2,1)}, bf16[2,2,264,128]{3,2,1,0:T(8,128)(2,1)S(1)}, u32[]{:S(2)}, u32[]{:S(2)}) collective-permute-start(bf16[2,2,264,128]{3,2,1,0:T(8,128)(2,1)} %collective-permute-done.9.refs_7_), channel_id=1, source_target_pairs={{0,192},{2,194},{4,196},{6,198},{8,200},{10,202},{12,204},{14,206}... | collective-permute-start | bytes 811016 | tf_op jit(solution)/shard_map/ppermute | solution.py:342
  56.8 1.0 copy-done.2
  57.9 16.3 %attend.2 = (bf16[2,1024,128]{2,1,0:T(8,128)(2,1)S(1)}, bf16[2,1024,128]{2,1,0:T(8,128)(2,1)S(1)}, f32[2,2,256,128]{3,2,1,0:T(8,128)S(1)}, bf16[4,2,128,128]{3,2...) custom-call(s32[16]{0:T(128)S(1)} %pad_add_fusion.scalars, ...), custom_call_target="tpu_custom_call" | custom-call | flops 4026531840 | bytes 6291456 | tf_op jit(solution)/shard_map/attend/pallas_call | solution.py:423
  74.3 1.4 collective-permute-start.12
  75.6 16.3 %attend.3 = (bf16[2,1024,128]{2,1,0:T(8,128)(2,1)S(1)}, bf16[2,1024,128]{2,1,0:T(8,128)(2,1)S(1)}, f32[2,2,256,128]{3,2,1,0:T(8,128)S(1)}, bf16[4,2,128,128]{3,2...) custom-call(s32[16]{0:T(128)S(1)} %pad_add_fusion.scalars, ...), custom_call_target="tpu_custom_call", output_to_operand_aliasing={{3}: (12, {}), {4}: (13, {}), {5}: (14, {}), {6}: (15, {}),... | custom-call | flops 4026531840 | bytes 6291456 | tf_op jit(solution)/shard_map/attend/pallas_call | solution.py:423
  92.0 4.5 %collective-permute-start.16 = (bf16[4,2,256,128]{3,2,1,0:T(8,128)(2,1)S(1)}, bf16[4,2,256,128]{3,2,1,0:T(8,128)(2,1)S(1)}, u32[]{:S(2)}, u32[]{:S(2)}) collective-permute-start(bf16[4,2,256,128]{3,2,1,0:T(8,128)(2,1)S(1)} %get-tuple-element.86), channel_id=1, source_target_pairs={{0,12},{2,14},{4,8},{6,10},{8,4},{10,6},{12,0},{14,2},{16,28},{18,... | collective-permute-start | bytes 1572872 | tf_op jit(solution)/shard_map/ppermute | solution.py:342
  96.5 1.3 collective-permute-start.17
  97.7 2.5 %collective-permute-start.14 = (bf16[2,2,264,128]{3,2,1,0:T(8,128)(2,1)S(1)}, bf16[2,2,264,128]{3,2,1,0:T(8,128)(2,1)S(1)}, u32[]{:S(2)}, u32[]{:S(2)}) collective-permute-start(bf16[2,2,264,128]{3,2,1,0:T(8,128)(2,1)S(1)} %get-tuple-element.83), channel_id=1, source_target_pairs={{0,192},{2,194},{4,196},{6,198},{8,200},{10,202},{12,204},{14,206}... | collective-permute-start | bytes 811016 | tf_op jit(solution)/shard_map/ppermute | solution.py:342
  100.8 1.9 %collective-permute-start.18 = (bf16[4,2,128,128]{3,2,1,0:T(8,128)(2,1)S(1)}, bf16[4,2,128,128]{3,2,1,0:T(8,128)(2,1)S(1)}, u32[]{:S(2)}, u32[]{:S(2)}) collective-permute-start(bf16[4,2,128,128]{3,2,1,0:T(8,128)(2,1)S(1)} %get-tuple-element.88), channel_id=1, source_target_pairs={{2,4},{4,2},{6,8},{8,6},{10,12},{12,10},{14,16},{16,14},{18,20},{2... | collective-permute-start | bytes 786440 | tf_op jit(solution)/shard_map/ppermute | solution.py:349
  102.7 6.1 %collective-permute-done.18.refs_0_ = bf16[4,2,128,128]{3,2,1,0:T(8,128)(2,1)S(1)} collective-permute-done((bf16[4,2,128,128]{3,2,1,0:T(8,128)(2,1)S(1)}, bf16[4,2,128,128]{3,2,1,0:T(8,128)(2,1)S(1)}, u32[]{:S(2)}, u32[]{:S(2)}) %collective-permute-start.18) | collective-permute-done | bytes 262176 | tf_op jit(solution)/shard_map/ppermute | solution.py:349
  108.8 2.6 %collective-permute-done.14 = bf16[2,2,264,128]{3,2,1,0:T(8,128)(2,1)S(1)} collective-permute-done((bf16[2,2,264,128]{3,2,1,0:T(8,128)(2,1)S(1)}, bf16[2,2,264,128]{3,2,1,0:T(8,128)(2,1)S(1)}, u32[]{:S(2)}, u32[]{:S(2)}) %collective-permute-start.14) | collective-permute-done | bytes 270368 | tf_op jit(solution)/shard_map/ppermute | solution.py:342
  111.3 3.3 %collective-permute-done.15.refs_7_ = bf16[2,2,264,128]{3,2,1,0:T(8,128)(2,1)S(1)} collective-permute-done((bf16[2,2,264,128]{3,2,1,0:T(8,128)(2,1)S(1)}, bf16[2,2,264,128]{3,2,1,0:T(8,128)(2,1)S(1)}, u32[]{:S(2)}, u32[]{:S(2)}) %collective-permute-start.15) | collective-permute-done | bytes 270368 | tf_op jit(solution)/shard_map/ppermute | solution.py:342
  114.6 1.0 collective-permute-start.20
  115.9 5.3 %collective-permute-start.22 = (bf16[4,2,256,128]{3,2,1,0:T(8,128)(2,1)S(1)}, bf16[4,2,256,128]{3,2,1,0:T(8,128)(2,1)S(1)}, u32[]{:S(2)}, u32[]{:S(2)}) collective-permute-start(bf16[4,2,256,128]{3,2,1,0:T(8,128)(2,1)S(1)} %get-tuple-element.100), channel_id=1, source_target_pairs={{0,32},{2,34},{4,36},{6,38},{8,40},{10,42},{12,44},{14,46},{16,48}... | collective-permute-start | bytes 1572872 | tf_op jit(solution)/shard_map/ppermute | solution.py:342
  121.4 6.4 %collective-permute-done.19.refs_3_ = bf16[2,1024,128]{2,1,0:T(8,128)(2,1)S(1)} collective-permute-done((bf16[2,1024,128]{2,1,0:T(8,128)(2,1)S(1)}, bf16[2,1024,128]{2,1,0:T(8,128)(2,1)S(1)}, u32[]{:S(2)}, u32[]{:S(2)}) %collective-permute-start.19) | collective-permute-done | bytes 524320 | tf_op jit(solution)/shard_map/ppermute | solution.py:353
  127.7 2.3 %finish_sides.1 = (bf16[4096,128]{1,0:T(8,128)(2,1)}, bf16[4096,128]{1,0:T(8,128)(2,1)}) custom-call(s32[1]{0:T(128)} %bitcast.scalars, bf16[2,1024,128]{2,1,0:T(8,128)(2,1)S(1)} %get-tuple-element.64.refs_0_, bf16[2,1024,128]{2,1,0:T(8,128)(2,1)S(1)} %get-tuple-element.75.refs_1_, bf16[2,1024,128]{2,1,0:T(8,128)(2,1)S(1)} %collective-permute-done.13.refs_2_, ...), custom_call_target="tpu_custom_call" | custom-call | tf_op jit(solution)/shard_map/finish_sides/pallas_call | solution.py:479
  130.1 8.3 %collective-permute-done.23.refs_8_ = bf16[2,2,264,128]{3,2,1,0:T(8,128)(2,1)S(1)} collective-permute-done((bf16[2,2,264,128]{3,2,1,0:T(8,128)(2,1)S(1)}, bf16[2,2,264,128]{3,2,1,0:T(8,128)(2,1)S(1)}, u32[]{:S(2)}, u32[]{:S(2)}) %collective-permute-start.23) | collective-permute-done | bytes 270368 | tf_op jit(solution)/shard_map/ppermute | solution.py:342
  139.3 1.8 %finish_pairs.1 = (bf16[1024,128]{1,0:T(8,128)(2,1)}, bf16[1024,128]{1,0:T(8,128)(2,1)}) custom-call(s32[1]{0:T(128)} %bitcast.2.scalars, bf16[4,2,128,128]{3,2,1,0:T(8,128)(2,1)S(1)} %collective-permute-done.18.refs_0_, bf16[4,2,256,128]{3,2,1,0:T(8,128)(2,1)S(1)} %collective-permute-done.20.refs_1_, ...), custom_call_target="tpu_custom_call" | custom-call | tf_op jit(solution)/shard_map/finish_pairs/pallas_call | solution.py:489
  (45 shorter events, 6.2 us)
Async XLA Ops:
  3.5 11.2 %collective-permute-start = (bf16[4,2,256,128]{3,2,1,0:T(8,128)(2,1)}, bf16[4,2,256,128]{3,2,1,0:T(8,128)(2,1)S(1)}, u32[]{:S(2)}, u32[]{:S(2)}) collective-permute-start(bf16[4,2,256,128]{3,2,1,0:T(8,128)(2,1)} %get-tuple-element.56.refs_0_), channel_id=1, source_target_pairs={{0,2},{2,0},{4,6},{6,4},{8,10},{10,8},{12,14},{14,12},{16,18},{18,... | collective-permute-start | bytes 1572872 | tf_op jit(solution)/shard_map/ppermute | solution.py:342
  6.8 19.7 %collective-permute-start.2 = (bf16[4,2,256,128]{3,2,1,0:T(8,128)(2,1)}, bf16[4,2,256,128]{3,2,1,0:T(8,128)(2,1)S(1)}, u32[]{:S(2)}, u32[]{:S(2)}) collective-permute-start(bf16[4,2,256,128]{3,2,1,0:T(8,128)(2,1)} %get-tuple-element.56.refs_0_), channel_id=1, source_target_pairs={{0,16},{2,18},{4,20},{6,22},{8,24},{10,26},{12,28},{14,30},{16,0},... | collective-permute-start | bytes 1572872 | tf_op jit(solution)/shard_map/ppermute | solution.py:342
  7.8 19.6 %collective-permute-start.1 = (bf16[4,2,256,128]{3,2,1,0:T(8,128)(2,1)}, bf16[4,2,256,128]{3,2,1,0:T(8,128)(2,1)S(1)}, u32[]{:S(2)}, u32[]{:S(2)}) collective-permute-start(bf16[4,2,256,128]{3,2,1,0:T(8,128)(2,1)} %get-tuple-element.56.refs_0_), channel_id=1, source_target_pairs={{0,32},{2,34},{4,36},{6,38},{8,40},{10,42},{12,44},{14,46},{16,48}... | collective-permute-start | bytes 1572872 | tf_op jit(solution)/shard_map/ppermute | solution.py:342
  9.5 19.1 %collective-permute-start.5 = (bf16[4,2,256,128]{3,2,1,0:T(8,128)(2,1)}, bf16[4,2,256,128]{3,2,1,0:T(8,128)(2,1)}, u32[]{:S(2)}, u32[]{:S(2)}) collective-permute-start(bf16[4,2,256,128]{3,2,1,0:T(8,128)(2,1)} %get-tuple-element.56.refs_0_), channel_id=1, source_target_pairs={{0,4},{2,6},{4,0},{6,2},{8,12},{10,14},{12,8},{14,10},{16,20},{18,... | collective-permute-start | bytes 1572872 | tf_op jit(solution)/shard_map/ppermute | solution.py:342
  10.8 15.8 %collective-permute-start.3 = (bf16[2,2,264,128]{3,2,1,0:T(8,128)(2,1)}, bf16[2,2,264,128]{3,2,1,0:T(8,128)(2,1)S(1)}, u32[]{:S(2)}, u32[]{:S(2)}) collective-permute-start(bf16[2,2,264,128]{3,2,1,0:T(8,128)(2,1)} %get-tuple-element.60), channel_id=1, source_target_pairs={{0,64},{2,66},{4,68},{6,70},{8,72},{10,74},{12,76},{14,78},{16,80}... | collective-permute-start | bytes 811016 | tf_op jit(solution)/shard_map/ppermute | solution.py:342
  13.8 0.7 copy-start.3
  14.7 42.1 %copy-start = (bf16[4,2,256,128]{3,2,1,0:T(8,128)(2,1)S(1)}, bf16[4,2,256,128]{3,2,1,0:T(8,128)(2,1)}, u32[]{:S(2)}) copy-start(bf16[4,2,256,128]{3,2,1,0:T(8,128)(2,1)} %get-tuple-element.56.refs_0_) | copy-start | bytes 1572868
  27.4 0.8 copy-start.1
  28.2 13.6 %copy-start.5 = (s32[7]{0:T(128)S(1)}, s32[7]{0:T(128)}, u32[]{:S(2)}) copy-start(s32[7]{0:T(128)} %param.12) | copy-start | bytes 88
  28.2 13.6 %copy-start.4 = (s32[2,7]{1,0:T(2,128)S(1)}, s32[2,7]{1,0:T(2,128)}, u32[]{:S(2)}) copy-start(s32[2,7]{1,0:T(2,128)} %param.13) | copy-start | bytes 172
  28.2 24.8 %collective-permute-start.8 = (bf16[2,1040,128]{2,1,0:T(8,128)(2,1)}, bf16[2,1040,128]{2,1,0:T(8,128)(2,1)S(1)}, u32[]{:S(2)}, u32[]{:S(2)}) collective-permute-start(bf16[2,1040,128]{2,1,0:T(8,128)(2,1)} %get-tuple-element.63), channel_id=1, source_target_pairs={{0,1},{1,0},{2,3},{3,2},{4,5},{5,4},{6,7},{7,6},{8,9},{9,8},{10,11... | collective-permute-start | bytes 1597448 | tf_op jit(solution)/shard_map/ppermute | solution.py:353
  28.5 24.5 %collective-permute-start.6 = (bf16[4,2,256,128]{3,2,1,0:T(8,128)(2,1)}, bf16[4,2,256,128]{3,2,1,0:T(8,128)(2,1)}, u32[]{:S(2)}, u32[]{:S(2)}) collective-permute-start(bf16[4,2,256,128]{3,2,1,0:T(8,128)(2,1)} %collective-permute-done.5.refs_3_), channel_id=1, source_target_pairs={{0,12},{2,14},{4,8},{6,10},{8,4},{10,6},{12,0},{14,2},{16,28},{18,... | collective-permute-start | bytes 1572872 | tf_op jit(solution)/shard_map/ppermute | solution.py:342
  31.3 18.1 %collective-permute-start.7 = (bf16[2,2,264,128]{3,2,1,0:T(8,128)(2,1)S(1)}, bf16[2,2,264,128]{3,2,1,0:T(8,128)(2,1)}, u32[]{:S(2)}, u32[]{:S(2)}) collective-permute-start(bf16[2,2,264,128]{3,2,1,0:T(8,128)(2,1)S(1)} %collective-permute-done.3.refs_7_), channel_id=1, source_target_pairs={{0,192},{2,194},{4,196},{6,198},{8,200},{10,202},{12,204},{14,206}... | collective-permute-start | bytes 811016 | tf_op jit(solution)/shard_map/ppermute | solution.py:342
  37.3 12.0 %collective-permute-start.4 = (bf16[4,2,128,128]{3,2,1,0:T(8,128)(2,1)}, bf16[4,2,128,128]{3,2,1,0:T(8,128)(2,1)}, u32[]{:S(2)}, u32[]{:S(2)}) collective-permute-start(bf16[4,2,128,128]{3,2,1,0:T(8,128)(2,1)} %get-tuple-element.61), channel_id=1, source_target_pairs={{2,4},{4,2},{6,8},{8,6},{10,12},{12,10},{14,16},{16,14},{18,20},{2... | collective-permute-start | bytes 786440 | tf_op jit(solution)/shard_map/ppermute | solution.py:349
  41.0 12.1 %collective-permute-start.9 = (bf16[2,2,264,128]{3,2,1,0:T(8,128)(2,1)}, bf16[2,2,264,128]{3,2,1,0:T(8,128)(2,1)}, u32[]{:S(2)}, u32[]{:S(2)}) collective-permute-start(bf16[2,2,264,128]{3,2,1,0:T(8,128)(2,1)} %get-tuple-element.65), channel_id=1, source_target_pairs={{0,64},{2,66},{4,68},{6,70},{8,72},{10,74},{12,76},{14,78},{16,80}... | collective-permute-start | bytes 811016 | tf_op jit(solution)/shard_map/ppermute | solution.py:342
  53.0 22.6 %collective-permute-start.11 = (bf16[2,1040,128]{2,1,0:T(8,128)(2,1)}, bf16[2,1040,128]{2,1,0:T(8,128)(2,1)S(1)}, u32[]{:S(2)}, u32[]{:S(2)}) collective-permute-start(bf16[2,1040,128]{2,1,0:T(8,128)(2,1)} %get-tuple-element.68), channel_id=1, source_target_pairs={{0,1},{1,0},{2,3},{3,2},{4,5},{5,4},{6,7},{7,6},{8,9},{9,8},{10,11... | collective-permute-start | bytes 1597448 | tf_op jit(solution)/shard_map/ppermute | solution.py:353
  54.3 21.3 %collective-permute-start.10 = (bf16[2,2,264,128]{3,2,1,0:T(8,128)(2,1)}, bf16[2,2,264,128]{3,2,1,0:T(8,128)(2,1)S(1)}, u32[]{:S(2)}, u32[]{:S(2)}) collective-permute-start(bf16[2,2,264,128]{3,2,1,0:T(8,128)(2,1)} %collective-permute-done.9.refs_7_), channel_id=1, source_target_pairs={{0,192},{2,194},{4,196},{6,198},{8,200},{10,202},{12,204},{14,206}... | collective-permute-start | bytes 811016 | tf_op jit(solution)/shard_map/ppermute | solution.py:342
  56.8 1.0 copy-start.2
  74.2 17.8 %collective-permute-start.13 = (bf16[2,1024,128]{2,1,0:T(8,128)(2,1)S(1)}, bf16[2,1024,128]{2,1,0:T(8,128)(2,1)S(1)}, u32[]{:S(2)}, u32[]{:S(2)}) collective-permute-start(bf16[2,1024,128]{2,1,0:T(8,128)(2,1)S(1)} %get-tuple-element.81), channel_id=1, source_target_pairs={{0,1},{1,0},{2,3},{3,2},{4,5},{5,4},{6,7},{7,6},{8,9},{9,8},{10,11... | collective-permute-start | bytes 1572872 | tf_op jit(solution)/shard_map/ppermute | solution.py:353
  74.3 17.7 %collective-permute-start.12 = (bf16[2,2,264,128]{3,2,1,0:T(8,128)(2,1)S(1)}, bf16[2,2,264,128]{3,2,1,0:T(8,128)(2,1)S(1)}, u32[]{:S(2)}, u32[]{:S(2)}) collective-permute-start(bf16[2,2,264,128]{3,2,1,0:T(8,128)(2,1)S(1)} %get-tuple-element.80), channel_id=1, source_target_pairs={{0,192},{2,194},{4,196},{6,198},{8,200},{10,202},{12,204},{14,206}... | collective-permute-start | bytes 811016 | tf_op jit(solution)/shard_map/ppermute | solution.py:342
  92.0 22.6 %collective-permute-start.16 = (bf16[4,2,256,128]{3,2,1,0:T(8,128)(2,1)S(1)}, bf16[4,2,256,128]{3,2,1,0:T(8,128)(2,1)S(1)}, u32[]{:S(2)}, u32[]{:S(2)}) collective-permute-start(bf16[4,2,256,128]{3,2,1,0:T(8,128)(2,1)S(1)} %get-tuple-element.86), channel_id=1, source_target_pairs={{0,12},{2,14},{4,8},{6,10},{8,4},{10,6},{12,0},{14,2},{16,28},{18,... | collective-permute-start | bytes 1572872 | tf_op jit(solution)/shard_map/ppermute | solution.py:342
  96.5 18.2 %collective-permute-start.17 = (bf16[4,2,256,128]{3,2,1,0:T(8,128)(2,1)S(1)}, bf16[4,2,256,128]{3,2,1,0:T(8,128)(2,1)S(1)}, u32[]{:S(2)}, u32[]{:S(2)}) collective-permute-start(bf16[4,2,256,128]{3,2,1,0:T(8,128)(2,1)S(1)} %get-tuple-element.87), channel_id=1, source_target_pairs={{0,16},{2,18},{4,20},{6,22},{8,24},{10,26},{12,28},{14,30},{16,0},... | collective-permute-start | bytes 1572872 | tf_op jit(solution)/shard_map/ppermute | solution.py:342
  97.7 13.6 %collective-permute-start.14 = (bf16[2,2,264,128]{3,2,1,0:T(8,128)(2,1)S(1)}, bf16[2,2,264,128]{3,2,1,0:T(8,128)(2,1)S(1)}, u32[]{:S(2)}, u32[]{:S(2)}) collective-permute-start(bf16[2,2,264,128]{3,2,1,0:T(8,128)(2,1)S(1)} %get-tuple-element.83), channel_id=1, source_target_pairs={{0,192},{2,194},{4,196},{6,198},{8,200},{10,202},{12,204},{14,206}... | collective-permute-start | bytes 811016 | tf_op jit(solution)/shard_map/ppermute | solution.py:342
  100.3 14.3 %collective-permute-start.15 = (bf16[2,2,264,128]{3,2,1,0:T(8,128)(2,1)S(1)}, bf16[2,2,264,128]{3,2,1,0:T(8,128)(2,1)S(1)}, u32[]{:S(2)}, u32[]{:S(2)}) collective-permute-start(bf16[2,2,264,128]{3,2,1,0:T(8,128)(2,1)S(1)} %add_convert_fusion.2), channel_id=1, source_target_pairs={{0,64},{2,66},{4,68},{6,70},{8,72},{10,74},{12,76},{14,78},{16,80}... | collective-permute-start | bytes 811016 | tf_op jit(solution)/shard_map/ppermute | solution.py:342
  100.8 8.0 %collective-permute-start.18 = (bf16[4,2,128,128]{3,2,1,0:T(8,128)(2,1)S(1)}, bf16[4,2,128,128]{3,2,1,0:T(8,128)(2,1)S(1)}, u32[]{:S(2)}, u32[]{:S(2)}) collective-permute-start(bf16[4,2,128,128]{3,2,1,0:T(8,128)(2,1)S(1)} %get-tuple-element.88), channel_id=1, source_target_pairs={{2,4},{4,2},{6,8},{8,6},{10,12},{12,10},{14,16},{16,14},{18,20},{2... | collective-permute-start | bytes 786440 | tf_op jit(solution)/shard_map/ppermute | solution.py:349
  114.6 13.1 %collective-permute-start.19 = (bf16[2,1024,128]{2,1,0:T(8,128)(2,1)S(1)}, bf16[2,1024,128]{2,1,0:T(8,128)(2,1)S(1)}, u32[]{:S(2)}, u32[]{:S(2)}) collective-permute-start(bf16[2,1024,128]{2,1,0:T(8,128)(2,1)S(1)} %get-tuple-element.92), channel_id=1, source_target_pairs={{0,1},{1,0},{2,3},{3,2},{4,5},{5,4},{6,7},{7,6},{8,9},{9,8},{10,11... | collective-permute-start | bytes 1572872 | tf_op jit(solution)/shard_map/ppermute | solution.py:353
  114.6 23.7 %collective-permute-start.20 = (bf16[4,2,256,128]{3,2,1,0:T(8,128)(2,1)S(1)}, bf16[4,2,256,128]{3,2,1,0:T(8,128)(2,1)S(1)}, u32[]{:S(2)}, u32[]{:S(2)}) collective-permute-start(bf16[4,2,256,128]{3,2,1,0:T(8,128)(2,1)S(1)} %get-tuple-element.96), channel_id=1, source_target_pairs={{0,2},{2,0},{4,6},{6,4},{8,10},{10,8},{12,14},{14,12},{16,18},{18,... | collective-permute-start | bytes 1572872 | tf_op jit(solution)/shard_map/ppermute | solution.py:342
  115.8 22.5 %collective-permute-start.21 = (bf16[4,2,256,128]{3,2,1,0:T(8,128)(2,1)S(1)}, bf16[4,2,256,128]{3,2,1,0:T(8,128)(2,1)S(1)}, u32[]{:S(2)}, u32[]{:S(2)}) collective-permute-start(bf16[4,2,256,128]{3,2,1,0:T(8,128)(2,1)S(1)} %add_convert_fusion), channel_id=1, source_target_pairs={{0,4},{2,6},{4,0},{6,2},{8,12},{10,14},{12,8},{14,10},{16,20},{18,... | collective-permute-start | bytes 1572872 | tf_op jit(solution)/shard_map/ppermute | solution.py:342
  115.9 23.4 %collective-permute-start.22 = (bf16[4,2,256,128]{3,2,1,0:T(8,128)(2,1)S(1)}, bf16[4,2,256,128]{3,2,1,0:T(8,128)(2,1)S(1)}, u32[]{:S(2)}, u32[]{:S(2)}) collective-permute-start(bf16[4,2,256,128]{3,2,1,0:T(8,128)(2,1)S(1)} %get-tuple-element.100), channel_id=1, source_target_pairs={{0,32},{2,34},{4,36},{6,38},{8,40},{10,42},{12,44},{14,46},{16,48}... | collective-permute-start | bytes 1572872 | tf_op jit(solution)/shard_map/ppermute | solution.py:342
  121.3 17.1 %collective-permute-start.23 = (bf16[2,2,264,128]{3,2,1,0:T(8,128)(2,1)S(1)}, bf16[2,2,264,128]{3,2,1,0:T(8,128)(2,1)S(1)}, u32[]{:S(2)}, u32[]{:S(2)}) collective-permute-start(bf16[2,2,264,128]{3,2,1,0:T(8,128)(2,1)S(1)} %add_convert_fusion.1), channel_id=1, source_target_pairs={{0,64},{2,66},{4,68},{6,70},{8,72},{10,74},{12,76},{14,78},{16,80}... | collective-permute-start | bytes 811016 | tf_op jit(solution)/shard_map/ppermute | solution.py:342

commit v3 on v2

--- a/solution.py
+++ b/solution.py
@@ -19,7 +19,8 @@
 ROWS = 512
 PAD = 8
 PACK_MIB = 56
-SIDES_MIB = 52
+SIDES_MIB = 8
+ATT_MIB = 18
 NEG = -1e30
 F32 = jnp.float32
 BF16 = jnp.bfloat16
@@ -290,6 +291,23 @@
             copy.wait()
 
 
+def attend_scratch(rows):
+    return [
+        pltpu.VMEM((SLOTS * BLOCK, ROWS), F32),
+        pltpu.VMEM((SLOTS * BLOCK, ROWS), BF16),
+        pltpu.VMEM((SLOTS * BLOCK, ROWS), BF16),
+        pltpu.VMEM((2 * PER, 2, SLOTS * BLOCK, HEAD_DIM), BF16),
+        pltpu.VMEM((PER, 2, 1040, HEAD_DIM), BF16),
+        pltpu.VMEM((PER, 2, 1024, HEAD_DIM), BF16),
+        pltpu.VMEM((PER, 2, (3 + 2 * LEVELS) * BLOCK, HEAD_DIM), F32),
+        pltpu.VMEM((PER, 2, BLOCK, HEAD_DIM), BF16),
+        pltpu.VMEM((PER, LEVELS, 2, rows, HEAD_DIM), BF16),
+        pltpu.SemaphoreType.DMA((2 * PER,)),
+        pltpu.SemaphoreType.DMA((PER, 2)),
+        pltpu.SemaphoreType.DMA((PER, 4 + LEVELS)),
+    ]
+
+
 def finish_sides_kernel(scalars, *refs):
     sources, targets = refs[:-2], refs[-2:]
     order = query_order(scalars[0], 1)
@@ -319,7 +337,7 @@
         copy.start()
     for copy in copies:
         copy.wait()
-    beyond, whole, split = ins[0], ins[1:5], ins[5:]
+    beyond, whole, split = ins[0], ins[1:4], ins[4:]
     order = key_order(1)
     for member, target in enumerate(targets):
         for part in range(4):
@@ -388,10 +406,11 @@
     )(odd[None], key_in.reshape(-1, HEAD_DIM), value.reshape(-1, HEAD_DIM))
 
     z2_a = flipped(own_a, 32)
-    z1 = flipped(own, 16)
+    z1_a = flipped(own_a, 16)
     y1 = flipped(own, 2)
     core = flipped(own, 1)
     x = flipped(own, 8)
+    ext = past_end(lax.optimization_barrier((own_end, core))[0])
     keep_a, keep_b, send_a, send_b = pl.pallas_call(
         pack_sides_kernel,
         out_shape=[sides] * (2 * CHUNKS),
@@ -407,40 +426,27 @@
         grad_out.reshape(-1, HEAD_DIM),
         core,
     )
-    to_z2, to_ext, to_head = lax.optimization_barrier((own_b, own_end, send_a, z1, x, z2_a))[:3]
+    to_z2, to_head = lax.optimization_barrier((own_b, send_a))
     z6_a = flipped(z2_a, 96)
     z2_b = flipped(to_z2, 32)
     other_a = other_head(to_head)
     y3 = flipped(y1, 6)
-    ext = past_end(to_ext)
-    to_head = lax.optimization_barrier((send_b, z2_b, z6_a, other_a, y3, ext))[0]
+    to_head, to_z1 = lax.optimization_barrier((send_b, to_z2))
     z6_b = flipped(z2_b, 96)
+    z1_b = flipped(to_z1, 16)
     other_b = other_head(to_head)
 
-    def attend(chunk, keep, other, z2, z6, reused):
+    def attend(chunk, keep, other, z1, z2, z6, reused):
         ins = [scalars, own, ext, core, y1, y3, x, z1, z2, z6, keep, other, *reused]
-        outs = [half, half, terms, ends, *[whole] * 5, padded, padded]
+        outs = [half, half, terms, ends, *[whole] * 4, padded, padded, padded]
         return pl.pallas_call(
             functools.partial(attend_kernel, chunk * PER, len(reused)),
             out_shape=outs,
             in_specs=[SCALARS] + [FAR] * (len(ins) - 1),
             out_specs=[FAR] * len(outs),
-            scratch_shapes=[
-                pltpu.VMEM((SLOTS * BLOCK, ROWS), F32),
-                pltpu.VMEM((SLOTS * BLOCK, ROWS), BF16),
-                pltpu.VMEM((SLOTS * BLOCK, ROWS), BF16),
-                pltpu.VMEM((2 * PER, 2, SLOTS * BLOCK, HEAD_DIM), BF16),
-                pltpu.VMEM((PER, 2, 1040, HEAD_DIM), BF16),
-                pltpu.VMEM((PER, 2, 1024, HEAD_DIM), BF16),
-                pltpu.VMEM((PER, 2, (3 + 2 * LEVELS) * BLOCK, HEAD_DIM), F32),
-                pltpu.VMEM((PER, 2, BLOCK, HEAD_DIM), BF16),
-                pltpu.VMEM((PER, LEVELS, 2, rows, HEAD_DIM), BF16),
-                pltpu.SemaphoreType.DMA((2 * PER,)),
-                pltpu.SemaphoreType.DMA((PER, 2)),
-                pltpu.SemaphoreType.DMA((PER, 4 + LEVELS)),
-            ],
+            scratch_shapes=attend_scratch(rows),
             input_output_aliases={12 + i: 3 + i for i in range(len(reused))},
-            compiler_params=vmem(18),
+            compiler_params=vmem(ATT_MIB),
             cost_estimate=pl.CostEstimate(
                 flops=PER * 2 * 12 * SLOTS * BLOCK * ROWS * HEAD_DIM,
                 transcendentals=PER * 2 * SLOTS * BLOCK * ROWS,
@@ -449,31 +455,32 @@
             name="attend",
         )(*ins)
 
-    first = attend(0, keep_a, other_a, z2_a, z6_a, [])
+    first = attend(0, keep_a, other_a, z1_a, z2_a, z6_a, [])
     keep_out_a, other_out_a, terms_a = first[:3]
-    z2_terms_a, z4_terms_a = first[9:]
+    z1_terms_a, z2_terms_a, z4_terms_a = first[8:]
     far_a = flipped(z4_terms_a, 96)
     swapped_a = other_head(other_out_a)
-    second = attend(1, keep_b, other_b, z2_b, z6_b, first[3:9])
+    back_z1_a = flipped(z1_terms_a, 16)
+    second = attend(1, keep_b, other_b, z1_b, z2_b, z6_b, first[3:8])
     keep_out_b, other_out_b, terms_b, ext_terms, core_terms, y1_terms, y2_terms = second[:7]
-    x_terms, z1_terms, z2_terms_b, z4_terms_b = second[7:]
-    to_z6, to_y3, to_x, to_ext, far_a, swapped_a = lax.optimization_barrier(
-        (z4_terms_b, y2_terms, x_terms, ext_terms, far_a, swapped_a)
+    x_terms, z1_terms_b, z2_terms_b, z4_terms_b = second[7:]
+    to_z6, to_y3, to_x, to_ext, far_a, swapped_a, back_z1_a = lax.optimization_barrier(
+        (z4_terms_b, y2_terms, x_terms, ext_terms, far_a, swapped_a, back_z1_a)
     )
     far_b = flipped(to_z6, 96)
     back_z2_a = flipped(added(z2_terms_a, far_a), 32)
     near = flipped(to_y3, 6)
     back_x = flipped(to_x, 8)
     back_ext = past_end(to_ext)
-    far_b, back_z2_a, near, back_x, back_ext, z1_terms, core_terms, other_out_b = (
+    far_b, back_z2_a, near, back_x, back_ext, z1_terms_b, core_terms, other_out_b = (
         lax.optimization_barrier(
-            (far_b, back_z2_a, near, back_x, back_ext, z1_terms, core_terms, other_out_b)
+            (far_b, back_z2_a, near, back_x, back_ext, z1_terms_b, core_terms, other_out_b)
         )
     )
     back_z2_b = flipped(added(z2_terms_b, far_b), 32)
     back_y = flipped(added(y1_terms, near), 2)
     swapped_b = other_head(other_out_b)
-    back_z1 = flipped(z1_terms, 16)
+    back_z1_b = flipped(z1_terms_b, 16)
     back_core = flipped(core_terms, 1)
 
     out, dquery = pl.pallas_call(
@@ -484,8 +491,8 @@
         compiler_params=vmem(8),
         name="finish_sides",
     )(place[None], keep_out_a, keep_out_b, swapped_a, swapped_b)
-    sums = [back_ext, back_core, back_y, back_x, back_z1]
-    sums += [terms_a, terms_b, back_z2_a, back_z2_b]
+    sums = [back_ext, back_core, back_y, back_x, terms_a, terms_b]
+    sums += [back_z1_a, back_z1_b, back_z2_a, back_z2_b]
     dkey, dvalue = pl.pallas_call(
         finish_pairs_kernel,
         out_shape=[jax.ShapeDtypeStruct((rows * 4, HEAD_DIM), BF16)] * 2,

time: 142 us -> 131 us (0.923)
  waiting for transfers between devices: 46 us -> 28.3 us
  starting transfers between devices: 46.1 us -> 54.4 us
  Pallas kernels: 44.8 us -> 42.1 us
  local copies, waits for them, and re-layouts: 2.86 us -> 4.52 us
    ppermute x18 -> x20, waiting for transfers between devices: 33.5 us -> 17.2 us  [flipped(): lax.ppermute(value, 'seq', [(i, i ^ mask) for i in range(lax.axis_size('s...]
    ppermute x18 -> x20, starting transfers between devices: 38.9 us -> 47.7 us  [flipped(): lax.ppermute(value, 'seq', [(i, i ^ mask) for i in range(lax.axis_size('s...]
    pallas_call x1, Pallas kernels: 5.13 us -> 3.29 us  [shards(): pl.pallas_call(pack_sides_kernel, out_shape=[sides] * (2 * CHUNKS), in_sp...]
    unnamed x13, local copies, waits for them, and re-layouts: 2.6 us -> 4.26 us
  transfers between devices with their start and end apart: 24 -> 26, of which waited for: 10 -> 9; matrix products, arithmetic and copies ran while one was open for 1% -> 1% of each run, Pallas kernels for 28% -> 29%
where the time goes in v3:
time: 131 us
  starting transfers between devices  54.4 us (42%)
  Pallas kernels  42.1 us (32%)
  waiting for transfers between devices  28.3 us (22%)
  local copies, waits for them, and re-layouts  4.52 us (3%)
    ppermute x20, starting transfers between devices, flipped(): lax.ppermute(value, 'seq', [(i, i ^ mask) for i in range(lax.axis_size('s...  47.7 us
    pallas_call x2, Pallas kernels, attend(): pl.pallas_call(functools.partial(attend_kernel, chunk * PER, len(reused))...  31.8 us
    ppermute x20, waiting for transfers between devices, flipped(): lax.ppermute(value, 'seq', [(i, i ^ mask) for i in range(lax.axis_size('s...  17.2 us
    ppermute x2, waiting for transfers between devices, past_end(): return lax.ppermute(value, 'seq', pairs)  6.06 us
    ppermute x2, starting transfers between devices, past_end(): return lax.ppermute(value, 'seq', pairs)  5.24 us
    ppermute x4, waiting for transfers between devices, other_head(): return lax.ppermute(value, 'head', [(0, 1), (1, 0)])  5.08 us
    unnamed x13, local copies, waits for them, and re-layouts  4.26 us
    pallas_call x1, Pallas kernels, shards(): pl.pallas_call(pack_sides_kernel, out_shape=[sides] * (2 * CHUNKS), in_sp...  3.29 us
  transfers between devices with their start and end apart: 26, of which 9 were waited for; matrix products, arithmetic and copies ran while one was open for 1% of the time, Pallas kernels for 29%

profile of v3, /device:TPU:1, one launch (start us, length us, event | category | flops | bytes accessed | tf_op | source)
XLA Modules:
  0.0 130.9 jit_solution(3075281223207471969)
XLA Ops:
  0.6 2.8 %pack_pairs.1 = (bf16[4,2,256,128]{3,2,1,0:T(8,128)(2,1)}, bf16[2,2,264,128]{3,2,1,0:T(8,128)(2,1)}, bf16[2,2,264,128]{3,2,1,0:T(8,128)(2,1)}, bf16[4,2,128,128]{3,2,1,0:T(8,128)(2,1)}) custom-call(s32[1]{0:T(128)} %bitcast.2.scalars, bf16[1024,128]{1,0:T(8,128)(2,1)} %bitcast.13, bf16[1024,128]{1,0:T(8,128)(2,1)} %bitcast.14), custom_call_target="tpu_custom_call" | custom-call | tf_op jit(solution)/shard_map/pack_pairs/pallas_call | solution.py:397
  3.5 3.3 %collective-permute-start = (bf16[4,2,256,128]{3,2,1,0:T(8,128)(2,1)}, bf16[4,2,256,128]{3,2,1,0:T(8,128)(2,1)S(1)}, u32[]{:S(2)}, u32[]{:S(2)}) collective-permute-start(bf16[4,2,256,128]{3,2,1,0:T(8,128)(2,1)} %get-tuple-element.58.refs_0_), channel_id=1, source_target_pairs={{0,2},{2,0},{4,6},{6,4},{8,10},{10,8},{12,14},{14,12},{16,18},{18,... | collective-permute-start | bytes 1572872 | tf_op jit(solution)/shard_map/ppermute | solution.py:360
  6.8 2.3 %collective-permute-start.4 = (bf16[4,2,256,128]{3,2,1,0:T(8,128)(2,1)}, bf16[4,2,256,128]{3,2,1,0:T(8,128)(2,1)}, u32[]{:S(2)}, u32[]{:S(2)}) collective-permute-start(bf16[4,2,256,128]{3,2,1,0:T(8,128)(2,1)} %get-tuple-element.58.refs_0_), channel_id=1, source_target_pairs={{0,16},{2,18},{4,20},{6,22},{8,24},{10,26},{12,28},{14,30},{16,0},... | collective-permute-start | bytes 1572872 | tf_op jit(solution)/shard_map/ppermute | solution.py:360
  9.1 3.0 %collective-permute-start.6 = (bf16[2,2,264,128]{3,2,1,0:T(8,128)(2,1)}, bf16[2,2,264,128]{3,2,1,0:T(8,128)(2,1)S(1)}, u32[]{:S(2)}, u32[]{:S(2)}) collective-permute-start(bf16[2,2,264,128]{3,2,1,0:T(8,128)(2,1)} %get-tuple-element.61), channel_id=1, source_target_pairs={{0,64},{2,66},{4,68},{6,70},{8,72},{10,74},{12,76},{14,78},{16,80}... | collective-permute-start | bytes 811016 | tf_op jit(solution)/shard_map/ppermute | solution.py:360
  12.1 1.6 %collective-permute-start.5 = (bf16[2,2,264,128]{3,2,1,0:T(8,128)(2,1)}, bf16[2,2,264,128]{3,2,1,0:T(8,128)(2,1)}, u32[]{:S(2)}, u32[]{:S(2)}) collective-permute-start(bf16[2,2,264,128]{3,2,1,0:T(8,128)(2,1)} %get-tuple-element.61), channel_id=1, source_target_pairs={{0,32},{2,34},{4,36},{6,38},{8,40},{10,42},{12,44},{14,46},{16,48}... | collective-permute-start | bytes 811016 | tf_op jit(solution)/shard_map/ppermute | solution.py:360
  14.7 1.2 copy-done
  17.1 3.3 %pack_sides.1 = (bf16[2,1040,128]{2,1,0:T(8,128)(2,1)S(1)}, bf16[2,1040,128]{2,1,0:T(8,128)(2,1)S(1)}, bf16[2,1040,128]{2,1,0:T(8,128)(2,1)S(1)}, bf16[2,1040,128]{2,1,0:T(8,128)(2,1)S(1)}) custom-call(s32[17]{0:T(128)S(1)} %pad_add_fusion.1.scalars, bf16[4096,128]{1,0:T(8,128)(2,1)S(1)} %bitcast.11, bf16[4096,128]{1,0:T(8,128)(2,1)S(1)} %bitcast.12, ...), custom_call_target="tpu_custom_call" | custom-call | tf_op jit(solution)/shard_map/pack_sides/pallas_call | solution.py:414
  20.8 1.9 %collective-permute-start.3 = (bf16[4,2,256,128]{3,2,1,0:T(8,128)(2,1)}, bf16[4,2,256,128]{3,2,1,0:T(8,128)(2,1)}, u32[]{:S(2)}, u32[]{:S(2)}) collective-permute-start(bf16[4,2,256,128]{3,2,1,0:T(8,128)(2,1)} %collective-permute-done.2.refs_3_), channel_id=1, source_target_pairs={{0,12},{2,14},{4,8},{6,10},{8,4},{10,6},{12,0},{14,2},{16,28},{18,... | collective-permute-start | bytes 1572872 | tf_op jit(solution)/shard_map/ppermute | solution.py:360
  22.7 1.7 %collective-permute-done.6.refs_7_ = bf16[2,2,264,128]{3,2,1,0:T(8,128)(2,1)S(1)} collective-permute-done((bf16[2,2,264,128]{3,2,1,0:T(8,128)(2,1)}, bf16[2,2,264,128]{3,2,1,0:T(8,128)(2,1)S(1)}, u32[]{:S(2)}, u32[]{:S(2)}) %collective-permute-start.6) | collective-permute-done | bytes 270368 | tf_op jit(solution)/shard_map/ppermute | solution.py:360
  24.4 3.8 %collective-permute-start.7 = (bf16[2,2,264,128]{3,2,1,0:T(8,128)(2,1)S(1)}, bf16[2,2,264,128]{3,2,1,0:T(8,128)(2,1)}, u32[]{:S(2)}, u32[]{:S(2)}) collective-permute-start(bf16[2,2,264,128]{3,2,1,0:T(8,128)(2,1)S(1)} %collective-permute-done.6.refs_7_), channel_id=1, source_target_pairs={{0,192},{2,194},{4,196},{6,198},{8,200},{10,202},{12,204},{14,206}... | collective-permute-start | bytes 811016 | tf_op jit(solution)/shard_map/ppermute | solution.py:360
  28.2 3.3 %collective-permute-start.1 = (bf16[4,2,128,128]{3,2,1,0:T(8,128)(2,1)}, bf16[4,2,128,128]{3,2,1,0:T(8,128)(2,1)}, u32[]{:S(2)}, u32[]{:S(2)}) collective-permute-start(bf16[4,2,128,128]{3,2,1,0:T(8,128)(2,1)} %get-tuple-element.60), channel_id=1, source_target_pairs={{2,4},{4,2},{6,8},{8,6},{10,12},{12,10},{14,16},{16,14},{18,20},{2... | collective-permute-start | bytes 786440 | tf_op jit(solution)/shard_map/ppermute | solution.py:367
  31.5 3.1 %collective-permute-start.10 = (bf16[2,2,264,128]{3,2,1,0:T(8,128)(2,1)}, bf16[2,2,264,128]{3,2,1,0:T(8,128)(2,1)}, u32[]{:S(2)}, u32[]{:S(2)}) collective-permute-start(bf16[2,2,264,128]{3,2,1,0:T(8,128)(2,1)} %get-tuple-element.69), channel_id=1, source_target_pairs={{0,64},{2,66},{4,68},{6,70},{8,72},{10,74},{12,76},{14,78},{16,80}... | collective-permute-start | bytes 811016 | tf_op jit(solution)/shard_map/ppermute | solution.py:360
  35.0 2.0 %collective-permute-done.7.refs_8_ = bf16[2,2,264,128]{3,2,1,0:T(8,128)(2,1)} collective-permute-done((bf16[2,2,264,128]{3,2,1,0:T(8,128)(2,1)S(1)}, bf16[2,2,264,128]{3,2,1,0:T(8,128)(2,1)}, u32[]{:S(2)}, u32[]{:S(2)}) %collective-permute-start.7) | collective-permute-done | bytes 270368 | tf_op jit(solution)/shard_map/ppermute | solution.py:360
  37.7 5.4 %collective-permute-start.9 = (bf16[2,2,264,128]{3,2,1,0:T(8,128)(2,1)}, bf16[2,2,264,128]{3,2,1,0:T(8,128)(2,1)S(1)}, u32[]{:S(2)}, u32[]{:S(2)}) collective-permute-start(bf16[2,2,264,128]{3,2,1,0:T(8,128)(2,1)} %get-tuple-element.69), channel_id=1, source_target_pairs={{0,32},{2,34},{4,36},{6,38},{8,40},{10,42},{12,44},{14,46},{16,48}... | collective-permute-start | bytes 811016 | tf_op jit(solution)/shard_map/ppermute | solution.py:360
  43.1 3.1 %collective-permute-done.10.refs_7_ = bf16[2,2,264,128]{3,2,1,0:T(8,128)(2,1)} collective-permute-done((bf16[2,2,264,128]{3,2,1,0:T(8,128)(2,1)}, bf16[2,2,264,128]{3,2,1,0:T(8,128)(2,1)}, u32[]{:S(2)}, u32[]{:S(2)}) %collective-permute-start.10) | collective-permute-done | bytes 270368 | tf_op jit(solution)/shard_map/ppermute | solution.py:360
  47.2 15.8 %attend.2 = (bf16[2,1024,128]{2,1,0:T(8,128)(2,1)S(1)}, bf16[2,1024,128]{2,1,0:T(8,128)(2,1)S(1)}, f32[2,2,256,128]{3,2,1,0:T(8,128)S(1)}, bf16[4,2,128,128]{3,2...) custom-call(s32[16]{0:T(128)S(1)} %pad_add_fusion.scalars, ...), custom_call_target="tpu_custom_call" | custom-call | flops 4026531840 | bytes 6291456 | tf_op jit(solution)/shard_map/attend/pallas_call | solution.py:442
  63.5 3.6 %collective-permute-start.13 = (bf16[2,2,264,128]{3,2,1,0:T(8,128)(2,1)S(1)}, bf16[2,2,264,128]{3,2,1,0:T(8,128)(2,1)S(1)}, u32[]{:S(2)}, u32[]{:S(2)}) collective-permute-start(bf16[2,2,264,128]{3,2,1,0:T(8,128)(2,1)S(1)} %get-tuple-element.82), channel_id=1, source_target_pairs={{0,192},{2,194},{4,196},{6,198},{8,200},{10,202},{12,204},{14,206}... | collective-permute-start | bytes 811016 | tf_op jit(solution)/shard_map/ppermute | solution.py:360
  67.0 2.3 %collective-permute-start.15 = (bf16[2,2,264,128]{3,2,1,0:T(8,128)(2,1)S(1)}, bf16[2,2,264,128]{3,2,1,0:T(8,128)(2,1)S(1)}, u32[]{:S(2)}, u32[]{:S(2)}) collective-permute-start(bf16[2,2,264,128]{3,2,1,0:T(8,128)(2,1)S(1)} %get-tuple-element.84), channel_id=1, source_target_pairs={{0,32},{2,34},{4,36},{6,38},{8,40},{10,42},{12,44},{14,46},{16,48}... | collective-permute-start | bytes 811016 | tf_op jit(solution)/shard_map/ppermute | solution.py:360
  69.3 16.0 %attend.3 = (bf16[2,1024,128]{2,1,0:T(8,128)(2,1)S(1)}, bf16[2,1024,128]{2,1,0:T(8,128)(2,1)S(1)}, f32[2,2,256,128]{3,2,1,0:T(8,128)S(1)}, bf16[4,2,128,128]{3,2...) custom-call(s32[16]{0:T(128)S(1)} %pad_add_fusion.scalars, ...), custom_call_target="tpu_custom_call", output_to_operand_aliasing={{3}: (12, {}), {4}: (13, {}), {5}: (14, {}), {6}: (15, {}),... | custom-call | flops 4026531840 | bytes 6291456 | tf_op jit(solution)/shard_map/attend/pallas_call | solution.py:442
  85.3 2.7 %collective-permute-start.18 = (bf16[4,2,256,128]{3,2,1,0:T(8,128)(2,1)S(1)}, bf16[4,2,256,128]{3,2,1,0:T(8,128)(2,1)S(1)}, u32[]{:S(2)}, u32[]{:S(2)}) collective-permute-start(bf16[4,2,256,128]{3,2,1,0:T(8,128)(2,1)S(1)} %get-tuple-element.89), channel_id=1, source_target_pairs={{0,12},{2,14},{4,8},{6,10},{8,4},{10,6},{12,0},{14,2},{16,28},{18,... | collective-permute-start | bytes 1572872 | tf_op jit(solution)/shard_map/ppermute | solution.py:360
  88.1 4.5 %collective-permute-start.19 = (bf16[4,2,256,128]{3,2,1,0:T(8,128)(2,1)S(1)}, bf16[4,2,256,128]{3,2,1,0:T(8,128)(2,1)S(1)}, u32[]{:S(2)}, u32[]{:S(2)}) collective-permute-start(bf16[4,2,256,128]{3,2,1,0:T(8,128)(2,1)S(1)} %get-tuple-element.90), channel_id=1, source_target_pairs={{0,16},{2,18},{4,20},{6,22},{8,24},{10,26},{12,28},{14,30},{16,0},... | collective-permute-start | bytes 1572872 | tf_op jit(solution)/shard_map/ppermute | solution.py:360
  93.1 2.5 %collective-permute-start.17 = (bf16[2,2,264,128]{3,2,1,0:T(8,128)(2,1)S(1)}, bf16[2,2,264,128]{3,2,1,0:T(8,128)(2,1)S(1)}, u32[]{:S(2)}, u32[]{:S(2)}) collective-permute-start(bf16[2,2,264,128]{3,2,1,0:T(8,128)(2,1)S(1)} %add_convert_fusion.2), channel_id=1, source_target_pairs={{0,64},{2,66},{4,68},{6,70},{8,72},{10,74},{12,76},{14,78},{16,80}... | collective-permute-start | bytes 811016 | tf_op jit(solution)/shard_map/ppermute | solution.py:360
  95.5 1.9 %collective-permute-start.20 = (bf16[4,2,128,128]{3,2,1,0:T(8,128)(2,1)S(1)}, bf16[4,2,128,128]{3,2,1,0:T(8,128)(2,1)S(1)}, u32[]{:S(2)}, u32[]{:S(2)}) collective-permute-start(bf16[4,2,128,128]{3,2,1,0:T(8,128)(2,1)S(1)} %get-tuple-element.91), channel_id=1, source_target_pairs={{2,4},{4,2},{6,8},{8,6},{10,12},{12,10},{14,16},{16,14},{18,20},{2... | collective-permute-start | bytes 786440 | tf_op jit(solution)/shard_map/ppermute | solution.py:367
  97.4 6.1 %collective-permute-done.20.refs_0_ = bf16[4,2,128,128]{3,2,1,0:T(8,128)(2,1)S(1)} collective-permute-done((bf16[4,2,128,128]{3,2,1,0:T(8,128)(2,1)S(1)}, bf16[4,2,128,128]{3,2,1,0:T(8,128)(2,1)S(1)}, u32[]{:S(2)}, u32[]{:S(2)}) %collective-permute-start.20) | collective-permute-done | bytes 262176 | tf_op jit(solution)/shard_map/ppermute | solution.py:367
  103.5 1.3 %collective-permute-done.16 = bf16[2,2,264,128]{3,2,1,0:T(8,128)(2,1)S(1)} collective-permute-done((bf16[2,2,264,128]{3,2,1,0:T(8,128)(2,1)S(1)}, bf16[2,2,264,128]{3,2,1,0:T(8,128)(2,1)S(1)}, u32[]{:S(2)}, u32[]{:S(2)}) %collective-permute-start.16) | collective-permute-done | bytes 270368 | tf_op jit(solution)/shard_map/ppermute | solution.py:360
  104.8 3.0 %collective-permute-done.17.refs_8_ = bf16[2,2,264,128]{3,2,1,0:T(8,128)(2,1)S(1)} collective-permute-done((bf16[2,2,264,128]{3,2,1,0:T(8,128)(2,1)S(1)}, bf16[2,2,264,128]{3,2,1,0:T(8,128)(2,1)S(1)}, u32[]{:S(2)}, u32[]{:S(2)}) %collective-permute-start.17) | collective-permute-done | bytes 270368 | tf_op jit(solution)/shard_map/ppermute | solution.py:360
  109.0 5.1 %collective-permute-start.24 = (bf16[2,2,264,128]{3,2,1,0:T(8,128)(2,1)S(1)}, bf16[2,2,264,128]{3,2,1,0:T(8,128)(2,1)S(1)}, u32[]{:S(2)}, u32[]{:S(2)}) collective-permute-start(bf16[2,2,264,128]{3,2,1,0:T(8,128)(2,1)S(1)} %get-tuple-element.106), channel_id=1, source_target_pairs={{0,32},{2,34},{4,36},{6,38},{8,40},{10,42},{12,44},{14,46},{16,48}... | collective-permute-start | bytes 811016 | tf_op jit(solution)/shard_map/ppermute | solution.py:360
  115.4 5.1 %collective-permute-done.21.refs_3_ = bf16[2,1024,128]{2,1,0:T(8,128)(2,1)S(1)} collective-permute-done((bf16[2,1024,128]{2,1,0:T(8,128)(2,1)S(1)}, bf16[2,1024,128]{2,1,0:T(8,128)(2,1)S(1)}, u32[]{:S(2)}, u32[]{:S(2)}) %collective-permute-start.21) | collective-permute-done | bytes 524320 | tf_op jit(solution)/shard_map/ppermute | solution.py:371
  120.5 2.3 %finish_sides.1 = (bf16[4096,128]{1,0:T(8,128)(2,1)}, bf16[4096,128]{1,0:T(8,128)(2,1)}) custom-call(s32[1]{0:T(128)} %bitcast.scalars, bf16[2,1024,128]{2,1,0:T(8,128)(2,1)S(1)} %get-tuple-element.66.refs_0_, bf16[2,1024,128]{2,1,0:T(8,128)(2,1)S(1)} %get-tuple-element.77.refs_1_, bf16[2,1024,128]{2,1,0:T(8,128)(2,1)S(1)} %collective-permute-done.14.refs_2_, ...), custom_call_target="tpu_custom_call" | custom-call | tf_op jit(solution)/shard_map/finish_sides/pallas_call | solution.py:486
  122.8 2.4 %collective-permute-done.24.refs_7_ = bf16[2,2,264,128]{3,2,1,0:T(8,128)(2,1)S(1)} collective-permute-done((bf16[2,2,264,128]{3,2,1,0:T(8,128)(2,1)S(1)}, bf16[2,2,264,128]{3,2,1,0:T(8,128)(2,1)S(1)}, u32[]{:S(2)}, u32[]{:S(2)}) %collective-permute-start.24) | collective-permute-done | bytes 270368 | tf_op jit(solution)/shard_map/ppermute | solution.py:360
  125.2 3.7 %collective-permute-done.25.refs_9_ = bf16[2,2,264,128]{3,2,1,0:T(8,128)(2,1)S(1)} collective-permute-done((bf16[2,2,264,128]{3,2,1,0:T(8,128)(2,1)S(1)}, bf16[2,2,264,128]{3,2,1,0:T(8,128)(2,1)S(1)}, u32[]{:S(2)}, u32[]{:S(2)}) %collective-permute-start.25) | collective-permute-done | bytes 270368 | tf_op jit(solution)/shard_map/ppermute | solution.py:360
  128.9 1.9 %finish_pairs.1 = (bf16[1024,128]{1,0:T(8,128)(2,1)}, bf16[1024,128]{1,0:T(8,128)(2,1)}) custom-call(s32[1]{0:T(128)} %bitcast.2.scalars, bf16[4,2,128,128]{3,2,1,0:T(8,128)(2,1)S(1)} %collective-permute-done.20.refs_0_, bf16[4,2,256,128]{3,2,1,0:T(8,128)(2,1)S(1)} %collective-permute-done.22.refs_1_, ...), custom_call_target="tpu_custom_call" | custom-call | tf_op jit(solution)/shard_map/finish_pairs/pallas_call | solution.py:496
  (49 shorter events, 8.1 us)
Async XLA Ops:
  3.5 11.2 %collective-permute-start = (bf16[4,2,256,128]{3,2,1,0:T(8,128)(2,1)}, bf16[4,2,256,128]{3,2,1,0:T(8,128)(2,1)S(1)}, u32[]{:S(2)}, u32[]{:S(2)}) collective-permute-start(bf16[4,2,256,128]{3,2,1,0:T(8,128)(2,1)} %get-tuple-element.58.refs_0_), channel_id=1, source_target_pairs={{0,2},{2,0},{4,6},{6,4},{8,10},{10,8},{12,14},{14,12},{16,18},{18,... | collective-permute-start | bytes 1572872 | tf_op jit(solution)/shard_map/ppermute | solution.py:360
  6.8 14.0 %collective-permute-start.2 = (bf16[4,2,256,128]{3,2,1,0:T(8,128)(2,1)}, bf16[4,2,256,128]{3,2,1,0:T(8,128)(2,1)}, u32[]{:S(2)}, u32[]{:S(2)}) collective-permute-start(bf16[4,2,256,128]{3,2,1,0:T(8,128)(2,1)} %get-tuple-element.58.refs_0_), channel_id=1, source_target_pairs={{0,4},{2,6},{4,0},{6,2},{8,12},{10,14},{12,8},{14,10},{16,20},{18,... | collective-permute-start | bytes 1572872 | tf_op jit(solution)/shard_map/ppermute | solution.py:360
  6.8 24.7 %collective-permute-start.4 = (bf16[4,2,256,128]{3,2,1,0:T(8,128)(2,1)}, bf16[4,2,256,128]{3,2,1,0:T(8,128)(2,1)}, u32[]{:S(2)}, u32[]{:S(2)}) collective-permute-start(bf16[4,2,256,128]{3,2,1,0:T(8,128)(2,1)} %get-tuple-element.58.refs_0_), channel_id=1, source_target_pairs={{0,16},{2,18},{4,20},{6,22},{8,24},{10,26},{12,28},{14,30},{16,0},... | collective-permute-start | bytes 1572872 | tf_op jit(solution)/shard_map/ppermute | solution.py:360
  9.1 15.3 %collective-permute-start.6 = (bf16[2,2,264,128]{3,2,1,0:T(8,128)(2,1)}, bf16[2,2,264,128]{3,2,1,0:T(8,128)(2,1)S(1)}, u32[]{:S(2)}, u32[]{:S(2)}) collective-permute-start(bf16[2,2,264,128]{3,2,1,0:T(8,128)(2,1)} %get-tuple-element.61), channel_id=1, source_target_pairs={{0,64},{2,66},{4,68},{6,70},{8,72},{10,74},{12,76},{14,78},{16,80}... | collective-permute-start | bytes 811016 | tf_op jit(solution)/shard_map/ppermute | solution.py:360
  12.1 16.1 %collective-permute-start.5 = (bf16[2,2,264,128]{3,2,1,0:T(8,128)(2,1)}, bf16[2,2,264,128]{3,2,1,0:T(8,128)(2,1)}, u32[]{:S(2)}, u32[]{:S(2)}) collective-permute-start(bf16[2,2,264,128]{3,2,1,0:T(8,128)(2,1)} %get-tuple-element.61), channel_id=1, source_target_pairs={{0,32},{2,34},{4,36},{6,38},{8,40},{10,42},{12,44},{14,46},{16,48}... | collective-permute-start | bytes 811016 | tf_op jit(solution)/shard_map/ppermute | solution.py:360
  13.8 0.7 copy-start.3
  14.7 1.2 copy-start
  15.9 1.2 copy-start.1
  20.4 14.2 %copy-start.5 = (s32[7]{0:T(128)S(1)}, s32[7]{0:T(128)}, u32[]{:S(2)}) copy-start(s32[7]{0:T(128)} %param.12) | copy-start | bytes 88
  20.4 25.8 %collective-permute-start.8 = (bf16[2,1040,128]{2,1,0:T(8,128)(2,1)S(1)}, bf16[2,1040,128]{2,1,0:T(8,128)(2,1)S(1)}, u32[]{:S(2)}, u32[]{:S(2)}) collective-permute-start(bf16[2,1040,128]{2,1,0:T(8,128)(2,1)S(1)} %get-tuple-element.65), channel_id=1, source_target_pairs={{0,1},{1,0},{2,3},{3,2},{4,5},{5,4},{6,7},{7,6},{8,9},{9,8},{10,11... | collective-permute-start | bytes 1597448 | tf_op jit(solution)/shard_map/ppermute | solution.py:371
  20.8 25.4 %collective-permute-start.3 = (bf16[4,2,256,128]{3,2,1,0:T(8,128)(2,1)}, bf16[4,2,256,128]{3,2,1,0:T(8,128)(2,1)}, u32[]{:S(2)}, u32[]{:S(2)}) collective-permute-start(bf16[4,2,256,128]{3,2,1,0:T(8,128)(2,1)} %collective-permute-done.2.refs_3_), channel_id=1, source_target_pairs={{0,12},{2,14},{4,8},{6,10},{8,4},{10,6},{12,0},{14,2},{16,28},{18,... | collective-permute-start | bytes 1572872 | tf_op jit(solution)/shard_map/ppermute | solution.py:360
  24.4 12.6 %collective-permute-start.7 = (bf16[2,2,264,128]{3,2,1,0:T(8,128)(2,1)S(1)}, bf16[2,2,264,128]{3,2,1,0:T(8,128)(2,1)}, u32[]{:S(2)}, u32[]{:S(2)}) collective-permute-start(bf16[2,2,264,128]{3,2,1,0:T(8,128)(2,1)S(1)} %collective-permute-done.6.refs_7_), channel_id=1, source_target_pairs={{0,192},{2,194},{4,196},{6,198},{8,200},{10,202},{12,204},{14,206}... | collective-permute-start | bytes 811016 | tf_op jit(solution)/shard_map/ppermute | solution.py:360
  28.2 6.4 %copy-start.4 = (s32[2,7]{1,0:T(2,128)S(1)}, s32[2,7]{1,0:T(2,128)}, u32[]{:S(2)}) copy-start(s32[2,7]{1,0:T(2,128)} %param.13) | copy-start | bytes 172
  28.2 9.5 %collective-permute-start.1 = (bf16[4,2,128,128]{3,2,1,0:T(8,128)(2,1)}, bf16[4,2,128,128]{3,2,1,0:T(8,128)(2,1)}, u32[]{:S(2)}, u32[]{:S(2)}) collective-permute-start(bf16[4,2,128,128]{3,2,1,0:T(8,128)(2,1)} %get-tuple-element.60), channel_id=1, source_target_pairs={{2,4},{4,2},{6,8},{8,6},{10,12},{12,10},{14,16},{16,14},{18,20},{2... | collective-permute-start | bytes 786440 | tf_op jit(solution)/shard_map/ppermute | solution.py:367
  31.5 14.7 %collective-permute-start.10 = (bf16[2,2,264,128]{3,2,1,0:T(8,128)(2,1)}, bf16[2,2,264,128]{3,2,1,0:T(8,128)(2,1)}, u32[]{:S(2)}, u32[]{:S(2)}) collective-permute-start(bf16[2,2,264,128]{3,2,1,0:T(8,128)(2,1)} %get-tuple-element.69), channel_id=1, source_target_pairs={{0,64},{2,66},{4,68},{6,70},{8,72},{10,74},{12,76},{14,78},{16,80}... | collective-permute-start | bytes 811016 | tf_op jit(solution)/shard_map/ppermute | solution.py:360
  37.0 32.3 %collective-permute-start.12 = (bf16[2,1040,128]{2,1,0:T(8,128)(2,1)S(1)}, bf16[2,1040,128]{2,1,0:T(8,128)(2,1)S(1)}, u32[]{:S(2)}, u32[]{:S(2)}) collective-permute-start(bf16[2,1040,128]{2,1,0:T(8,128)(2,1)S(1)} %get-tuple-element.71), channel_id=1, source_target_pairs={{0,1},{1,0},{2,3},{3,2},{4,5},{5,4},{6,7},{7,6},{8,9},{9,8},{10,11... | collective-permute-start | bytes 1597448 | tf_op jit(solution)/shard_map/ppermute | solution.py:371
  37.7 29.4 %collective-permute-start.9 = (bf16[2,2,264,128]{3,2,1,0:T(8,128)(2,1)}, bf16[2,2,264,128]{3,2,1,0:T(8,128)(2,1)S(1)}, u32[]{:S(2)}, u32[]{:S(2)}) collective-permute-start(bf16[2,2,264,128]{3,2,1,0:T(8,128)(2,1)} %get-tuple-element.69), channel_id=1, source_target_pairs={{0,32},{2,34},{4,36},{6,38},{8,40},{10,42},{12,44},{14,46},{16,48}... | collective-permute-start | bytes 811016 | tf_op jit(solution)/shard_map/ppermute | solution.py:360
  46.2 23.1 %collective-permute-start.11 = (bf16[2,2,264,128]{3,2,1,0:T(8,128)(2,1)}, bf16[2,2,264,128]{3,2,1,0:T(8,128)(2,1)S(1)}, u32[]{:S(2)}, u32[]{:S(2)}) collective-permute-start(bf16[2,2,264,128]{3,2,1,0:T(8,128)(2,1)} %collective-permute-done.10.refs_7_), channel_id=1, source_target_pairs={{0,192},{2,194},{4,196},{6,198},{8,200},{10,202},{12,204},{14,206}... | collective-permute-start | bytes 811016 | tf_op jit(solution)/shard_map/ppermute | solution.py:360
  46.2 1.0 copy-start.2
  63.0 22.3 %collective-permute-start.14 = (bf16[2,1024,128]{2,1,0:T(8,128)(2,1)S(1)}, bf16[2,1024,128]{2,1,0:T(8,128)(2,1)S(1)}, u32[]{:S(2)}, u32[]{:S(2)}) collective-permute-start(bf16[2,1024,128]{2,1,0:T(8,128)(2,1)S(1)} %get-tuple-element.83), channel_id=1, source_target_pairs={{0,1},{1,0},{2,3},{3,2},{4,5},{5,4},{6,7},{7,6},{8,9},{9,8},{10,11... | collective-permute-start | bytes 1572872 | tf_op jit(solution)/shard_map/ppermute | solution.py:371
  63.5 21.8 %collective-permute-start.13 = (bf16[2,2,264,128]{3,2,1,0:T(8,128)(2,1)S(1)}, bf16[2,2,264,128]{3,2,1,0:T(8,128)(2,1)S(1)}, u32[]{:S(2)}, u32[]{:S(2)}) collective-permute-start(bf16[2,2,264,128]{3,2,1,0:T(8,128)(2,1)S(1)} %get-tuple-element.82), channel_id=1, source_target_pairs={{0,192},{2,194},{4,196},{6,198},{8,200},{10,202},{12,204},{14,206}... | collective-permute-start | bytes 811016 | tf_op jit(solution)/shard_map/ppermute | solution.py:360
  67.0 18.3 %collective-permute-start.15 = (bf16[2,2,264,128]{3,2,1,0:T(8,128)(2,1)S(1)}, bf16[2,2,264,128]{3,2,1,0:T(8,128)(2,1)S(1)}, u32[]{:S(2)}, u32[]{:S(2)}) collective-permute-start(bf16[2,2,264,128]{3,2,1,0:T(8,128)(2,1)S(1)} %get-tuple-element.84), channel_id=1, source_target_pairs={{0,32},{2,34},{4,36},{6,38},{8,40},{10,42},{12,44},{14,46},{16,48}... | collective-permute-start | bytes 811016 | tf_op jit(solution)/shard_map/ppermute | solution.py:360
  85.3 22.4 %collective-permute-start.18 = (bf16[4,2,256,128]{3,2,1,0:T(8,128)(2,1)S(1)}, bf16[4,2,256,128]{3,2,1,0:T(8,128)(2,1)S(1)}, u32[]{:S(2)}, u32[]{:S(2)}) collective-permute-start(bf16[4,2,256,128]{3,2,1,0:T(8,128)(2,1)S(1)} %get-tuple-element.89), channel_id=1, source_target_pairs={{0,12},{2,14},{4,8},{6,10},{8,4},{10,6},{12,0},{14,2},{16,28},{18,... | collective-permute-start | bytes 1572872 | tf_op jit(solution)/shard_map/ppermute | solution.py:360
  88.1 19.7 %collective-permute-start.19 = (bf16[4,2,256,128]{3,2,1,0:T(8,128)(2,1)S(1)}, bf16[4,2,256,128]{3,2,1,0:T(8,128)(2,1)S(1)}, u32[]{:S(2)}, u32[]{:S(2)}) collective-permute-start(bf16[4,2,256,128]{3,2,1,0:T(8,128)(2,1)S(1)} %get-tuple-element.90), channel_id=1, source_target_pairs={{0,16},{2,18},{4,20},{6,22},{8,24},{10,26},{12,28},{14,30},{16,0},... | collective-permute-start | bytes 1572872 | tf_op jit(solution)/shard_map/ppermute | solution.py:360
  92.5 12.3 %collective-permute-start.16 = (bf16[2,2,264,128]{3,2,1,0:T(8,128)(2,1)S(1)}, bf16[2,2,264,128]{3,2,1,0:T(8,128)(2,1)S(1)}, u32[]{:S(2)}, u32[]{:S(2)}) collective-permute-start(bf16[2,2,264,128]{3,2,1,0:T(8,128)(2,1)S(1)} %get-tuple-element.86), channel_id=1, source_target_pairs={{0,192},{2,194},{4,196},{6,198},{8,200},{10,202},{12,204},{14,206}... | collective-permute-start | bytes 811016 | tf_op jit(solution)/shard_map/ppermute | solution.py:360
  93.1 14.7 %collective-permute-start.17 = (bf16[2,2,264,128]{3,2,1,0:T(8,128)(2,1)S(1)}, bf16[2,2,264,128]{3,2,1,0:T(8,128)(2,1)S(1)}, u32[]{:S(2)}, u32[]{:S(2)}) collective-permute-start(bf16[2,2,264,128]{3,2,1,0:T(8,128)(2,1)S(1)} %add_convert_fusion.2), channel_id=1, source_target_pairs={{0,64},{2,66},{4,68},{6,70},{8,72},{10,74},{12,76},{14,78},{16,80}... | collective-permute-start | bytes 811016 | tf_op jit(solution)/shard_map/ppermute | solution.py:360
  95.5 8.0 %collective-permute-start.20 = (bf16[4,2,128,128]{3,2,1,0:T(8,128)(2,1)S(1)}, bf16[4,2,128,128]{3,2,1,0:T(8,128)(2,1)S(1)}, u32[]{:S(2)}, u32[]{:S(2)}) collective-permute-start(bf16[4,2,128,128]{3,2,1,0:T(8,128)(2,1)S(1)} %get-tuple-element.91), channel_id=1, source_target_pairs={{2,4},{4,2},{6,8},{8,6},{10,12},{12,10},{14,16},{16,14},{18,20},{2... | collective-permute-start | bytes 786440 | tf_op jit(solution)/shard_map/ppermute | solution.py:367
  107.8 12.7 %collective-permute-start.21 = (bf16[2,1024,128]{2,1,0:T(8,128)(2,1)S(1)}, bf16[2,1024,128]{2,1,0:T(8,128)(2,1)S(1)}, u32[]{:S(2)}, u32[]{:S(2)}) collective-permute-start(bf16[2,1024,128]{2,1,0:T(8,128)(2,1)S(1)} %get-tuple-element.95), channel_id=1, source_target_pairs={{0,1},{1,0},{2,3},{3,2},{4,5},{5,4},{6,7},{7,6},{8,9},{9,8},{10,11... | collective-permute-start | bytes 1572872 | tf_op jit(solution)/shard_map/ppermute | solution.py:371
  107.8 21.1 %collective-permute-start.22 = (bf16[4,2,256,128]{3,2,1,0:T(8,128)(2,1)S(1)}, bf16[4,2,256,128]{3,2,1,0:T(8,128)(2,1)S(1)}, u32[]{:S(2)}, u32[]{:S(2)}) collective-permute-start(bf16[4,2,256,128]{3,2,1,0:T(8,128)(2,1)S(1)} %get-tuple-element.99), channel_id=1, source_target_pairs={{0,2},{2,0},{4,6},{6,4},{8,10},{10,8},{12,14},{14,12},{16,18},{18,... | collective-permute-start | bytes 1572872 | tf_op jit(solution)/shard_map/ppermute | solution.py:360
  108.9 19.9 %collective-permute-start.23 = (bf16[4,2,256,128]{3,2,1,0:T(8,128)(2,1)S(1)}, bf16[4,2,256,128]{3,2,1,0:T(8,128)(2,1)S(1)}, u32[]{:S(2)}, u32[]{:S(2)}) collective-permute-start(bf16[4,2,256,128]{3,2,1,0:T(8,128)(2,1)S(1)} %add_convert_fusion), channel_id=1, source_target_pairs={{0,4},{2,6},{4,0},{6,2},{8,12},{10,14},{12,8},{14,10},{16,20},{18,... | collective-permute-start | bytes 1572872 | tf_op jit(solution)/shard_map/ppermute | solution.py:360
  109.0 16.1 %collective-permute-start.24 = (bf16[2,2,264,128]{3,2,1,0:T(8,128)(2,1)S(1)}, bf16[2,2,264,128]{3,2,1,0:T(8,128)(2,1)S(1)}, u32[]{:S(2)}, u32[]{:S(2)}) collective-permute-start(bf16[2,2,264,128]{3,2,1,0:T(8,128)(2,1)S(1)} %get-tuple-element.106), channel_id=1, source_target_pairs={{0,32},{2,34},{4,36},{6,38},{8,40},{10,42},{12,44},{14,46},{16,48}... | collective-permute-start | bytes 811016 | tf_op jit(solution)/shard_map/ppermute | solution.py:360
  114.3 14.6 %collective-permute-start.25 = (bf16[2,2,264,128]{3,2,1,0:T(8,128)(2,1)S(1)}, bf16[2,2,264,128]{3,2,1,0:T(8,128)(2,1)S(1)}, u32[]{:S(2)}, u32[]{:S(2)}) collective-permute-start(bf16[2,2,264,128]{3,2,1,0:T(8,128)(2,1)S(1)} %add_convert_fusion.1), channel_id=1, source_target_pairs={{0,64},{2,66},{4,68},{6,70},{8,72},{10,74},{12,76},{14,78},{16,80}... | collective-permute-start | bytes 811016 | tf_op jit(solution)/shard_map/ppermute | solution.py:360

commit v4 on v3

--- a/solution.py
+++ b/solution.py
@@ -166,7 +166,7 @@
         for block in range(2):
             side = 1 - block
             from_ext = even if block == 0 else odd
-            copy_pair(head, block, at_head(own, head), 0, 2).start()
+            copy_pair(head, block, at_head(own, head).at[:, pl.ds(0, 2 * BLOCK)], 0, 2).start()
             pl.when(from_ext)(copy_pair(head, block, at_head(ext, head), 2, 1).start)
             nearby = at_head(arrived[0], head).at[:, pl.ds(side * BLOCK, BLOCK)]
             pl.when(jnp.logical_not(from_ext))(copy_pair(head, block, nearby, 2, 1).start)
@@ -222,7 +222,7 @@
                 )
                 for member in range(2)
             )
-            copy_pair(head, block, at_head(own, head), 0, 2).wait()
+            copy_pair(head, block, at_head(own, head).at[:, pl.ds(0, 2 * BLOCK)], 0, 2).wait()
             for slot in range(2, SLOTS):
                 copy_pair(head, block, at_head(ext, head), slot, 1).wait()
             keys, values = pairs.at[unit, 0], pairs.at[unit, 1]
@@ -432,12 +432,12 @@
     other_a = other_head(to_head)
     y3 = flipped(y1, 6)
     to_head, to_z1 = lax.optimization_barrier((send_b, to_z2))
-    z6_b = flipped(z2_b, 96)
+    z4_b = flipped(to_z1, 64)
     z1_b = flipped(to_z1, 16)
     other_b = other_head(to_head)
 
-    def attend(chunk, keep, other, z1, z2, z6, reused):
-        ins = [scalars, own, ext, core, y1, y3, x, z1, z2, z6, keep, other, *reused]
+    def attend(chunk, mine, keep, other, z1, z2, z4, reused):
+        ins = [scalars, mine, ext, core, y1, y3, x, z1, z2, z4, keep, other, *reused]
         outs = [half, half, terms, ends, *[whole] * 4, padded, padded, padded]
         return pl.pallas_call(
             functools.partial(attend_kernel, chunk * PER, len(reused)),
@@ -455,33 +455,31 @@
             name="attend",
         )(*ins)
 
-    first = attend(0, keep_a, other_a, z1_a, z2_a, z6_a, [])
+    first = attend(0, own_a, keep_a, other_a, z1_a, z2_a, z6_a, [])
     keep_out_a, other_out_a, terms_a = first[:3]
     z1_terms_a, z2_terms_a, z4_terms_a = first[8:]
     far_a = flipped(z4_terms_a, 96)
     swapped_a = other_head(other_out_a)
     back_z1_a = flipped(z1_terms_a, 16)
-    second = attend(1, keep_b, other_b, z1_b, z2_b, z6_b, first[3:8])
+    second = attend(1, own_b, keep_b, other_b, z1_b, z2_b, z4_b, first[3:8])
     keep_out_b, other_out_b, terms_b, ext_terms, core_terms, y1_terms, y2_terms = second[:7]
     x_terms, z1_terms_b, z2_terms_b, z4_terms_b = second[7:]
-    to_z6, to_y3, to_x, to_ext, far_a, swapped_a, back_z1_a = lax.optimization_barrier(
-        (z4_terms_b, y2_terms, x_terms, ext_terms, far_a, swapped_a, back_z1_a)
+    to_z6, to_y3, to_x, to_ext, to_core, far_a, swapped_a, back_z1_a = lax.optimization_barrier(
+        (z4_terms_b, y2_terms, x_terms, ext_terms, core_terms, far_a, swapped_a, back_z1_a)
     )
     far_b = flipped(to_z6, 96)
     back_z2_a = flipped(added(z2_terms_a, far_a), 32)
     near = flipped(to_y3, 6)
+    back_core = flipped(to_core, 1)
     back_x = flipped(to_x, 8)
-    back_ext = past_end(to_ext)
-    far_b, back_z2_a, near, back_x, back_ext, z1_terms_b, core_terms, other_out_b = (
-        lax.optimization_barrier(
-            (far_b, back_z2_a, near, back_x, back_ext, z1_terms_b, core_terms, other_out_b)
-        )
+    back_ext = past_end(lax.optimization_barrier((to_ext, back_core))[0])
+    far_b, back_z2_a, near, back_x, back_ext, z1_terms_b, other_out_b = lax.optimization_barrier(
+        (far_b, back_z2_a, near, back_x, back_ext, z1_terms_b, other_out_b)
     )
     back_z2_b = flipped(added(z2_terms_b, far_b), 32)
     back_y = flipped(added(y1_terms, near), 2)
     swapped_b = other_head(other_out_b)
     back_z1_b = flipped(z1_terms_b, 16)
-    back_core = flipped(core_terms, 1)
 
     out, dquery = pl.pallas_call(
         finish_sides_kernel,

time: 131 us -> 126 us (0.962)
  the two profiles are of different devices: /device:TPU:1 before, /device:TPU:21 now
where the time goes in v4:
time: 126 us
  starting transfers between devices  47.8 us (38%)
  Pallas kernels  42.1 us (33%)
  waiting for transfers between devices  29.5 us (23%)
  local copies, waits for them, and re-layouts  4.44 us (4%)
    ppermute x20, starting transfers between devices, flipped(): lax.ppermute(value, 'seq', [(i, i ^ mask) for i in range(lax.axis_size('s...  33 us
    pallas_call x2, Pallas kernels, attend(): pl.pallas_call(functools.partial(attend_kernel, chunk * PER, len(reused))...  31.8 us
    ppermute x20, waiting for transfers between devices, flipped(): lax.ppermute(value, 'seq', [(i, i ^ mask) for i in range(lax.axis_size('s...  25.6 us
    ppermute x2, starting transfers between devices, past_end(): return lax.ppermute(value, 'seq', pairs)  9.21 us
    ppermute x4, starting transfers between devices, other_head(): return lax.ppermute(value, 'head', [(0, 1), (1, 0)])  5.62 us
    unnamed x15, local copies, waits for them, and re-layouts  4.18 us
    ppermute x4, waiting for transfers between devices, other_head(): return lax.ppermute(value, 'head', [(0, 1), (1, 0)])  3.92 us
    pallas_call x1, Pallas kernels, shards(): pl.pallas_call(pack_sides_kernel, out_shape=[sides] * (2 * CHUNKS), in_sp...  3.28 us
  transfers between devices with their start and end apart: 26, of which 8 were waited for; matrix products, arithmetic and copies ran while one was open for 1% of the time, Pallas kernels for 30%

profile of v4, /device:TPU:21, one launch (start us, length us, event | category | flops | bytes accessed | tf_op | source)
XLA Modules:
  0.0 125.5 jit_solution(2040633991250956938)
XLA Ops:
  0.6 2.8 %pack_pairs.1 = (bf16[4,2,256,128]{3,2,1,0:T(8,128)(2,1)}, bf16[2,2,264,128]{3,2,1,0:T(8,128)(2,1)}, bf16[2,2,264,128]{3,2,1,0:T(8,128)(2,1)}, bf16[4,2,128,128]{3,2,1,0:T(8,128)(2,1)}) custom-call(s32[1]{0:T(128)} %bitcast.2.scalars, bf16[1024,128]{1,0:T(8,128)(2,1)} %bitcast.13, bf16[1024,128]{1,0:T(8,128)(2,1)} %bitcast.14), custom_call_target="tpu_custom_call" | custom-call | tf_op jit(solution)/shard_map/pack_pairs/pallas_call | solution.py:397
  4.2 1.0 collective-permute-start.2
  5.2 3.0 %collective-permute-start.6 = (bf16[2,2,264,128]{3,2,1,0:T(8,128)(2,1)}, bf16[2,2,264,128]{3,2,1,0:T(8,128)(2,1)}, u32[]{:S(2)}, u32[]{:S(2)}) collective-permute-start(bf16[2,2,264,128]{3,2,1,0:T(8,128)(2,1)} %get-tuple-element.59.refs_0_), channel_id=1, source_target_pairs={{0,64},{2,66},{4,68},{6,70},{8,72},{10,74},{12,76},{14,78},{16,80}... | collective-permute-start | bytes 811016 | tf_op jit(solution)/shard_map/ppermute | solution.py:360
  8.2 1.6 %collective-permute-start.5 = (bf16[2,2,264,128]{3,2,1,0:T(8,128)(2,1)}, bf16[2,2,264,128]{3,2,1,0:T(8,128)(2,1)}, u32[]{:S(2)}, u32[]{:S(2)}) collective-permute-start(bf16[2,2,264,128]{3,2,1,0:T(8,128)(2,1)} %get-tuple-element.59.refs_0_), channel_id=1, source_target_pairs={{0,32},{2,34},{4,36},{6,38},{8,40},{10,42},{12,44},{14,46},{16,48}... | collective-permute-start | bytes 811016 | tf_op jit(solution)/shard_map/ppermute | solution.py:360
  11.0 1.2 copy-done
  12.3 1.2 copy-done.1
  13.5 3.3 %pack_sides.1 = (bf16[2,1040,128]{2,1,0:T(8,128)(2,1)S(1)}, bf16[2,1040,128]{2,1,0:T(8,128)(2,1)S(1)}, bf16[2,1040,128]{2,1,0:T(8,128)(2,1)S(1)}, bf16[2,1040,128]{2,1,0:T(8,128)(2,1)S(1)}) custom-call(s32[17]{0:T(128)S(1)} %pad_add_fusion.1.scalars, bf16[4096,128]{1,0:T(8,128)(2,1)S(1)} %bitcast.11, bf16[4096,128]{1,0:T(8,128)(2,1)S(1)} %bitcast.12, ...), custom_call_target="tpu_custom_call" | custom-call | tf_op jit(solution)/shard_map/pack_sides/pallas_call | solution.py:414
  16.8 1.9 %collective-permute-start.8 = (bf16[2,1040,128]{2,1,0:T(8,128)(2,1)S(1)}, bf16[2,1040,128]{2,1,0:T(8,128)(2,1)S(1)}, u32[]{:S(2)}, u32[]{:S(2)}) collective-permute-start(bf16[2,1040,128]{2,1,0:T(8,128)(2,1)S(1)} %get-tuple-element.66), channel_id=1, source_target_pairs={{0,1},{1,0},{2,3},{3,2},{4,5},{5,4},{6,7},{7,6},{8,9},{9,8},{10,11... | collective-permute-start | bytes 1597448 | tf_op jit(solution)/shard_map/ppermute | solution.py:371
  18.7 2.3 %collective-permute-done.6.refs_7_ = bf16[2,2,264,128]{3,2,1,0:T(8,128)(2,1)} collective-permute-done((bf16[2,2,264,128]{3,2,1,0:T(8,128)(2,1)}, bf16[2,2,264,128]{3,2,1,0:T(8,128)(2,1)}, u32[]{:S(2)}, u32[]{:S(2)}) %collective-permute-start.6) | collective-permute-done | bytes 270368 | tf_op jit(solution)/shard_map/ppermute | solution.py:360
  21.0 3.4 %collective-permute-start.7 = (bf16[2,2,264,128]{3,2,1,0:T(8,128)(2,1)}, bf16[2,2,264,128]{3,2,1,0:T(8,128)(2,1)}, u32[]{:S(2)}, u32[]{:S(2)}) collective-permute-start(bf16[2,2,264,128]{3,2,1,0:T(8,128)(2,1)} %collective-permute-done.6.refs_7_), channel_id=1, source_target_pairs={{0,192},{2,194},{4,196},{6,198},{8,200},{10,202},{12,204},{14,206}... | collective-permute-start | bytes 811016 | tf_op jit(solution)/shard_map/ppermute | solution.py:360
  24.4 4.0 %collective-permute-start.1 = (bf16[4,2,128,128]{3,2,1,0:T(8,128)(2,1)}, bf16[4,2,128,128]{3,2,1,0:T(8,128)(2,1)}, u32[]{:S(2)}, u32[]{:S(2)}) collective-permute-start(bf16[4,2,128,128]{3,2,1,0:T(8,128)(2,1)} %get-tuple-element.62), channel_id=1, source_target_pairs={{2,4},{4,2},{6,8},{8,6},{10,12},{12,10},{14,16},{16,14},{18,20},{2... | collective-permute-start | bytes 786440 | tf_op jit(solution)/shard_map/ppermute | solution.py:367
  28.8 0.9 collective-permute-start.12
  29.8 5.4 %collective-permute-done.7.refs_8_ = bf16[2,2,264,128]{3,2,1,0:T(8,128)(2,1)} collective-permute-done((bf16[2,2,264,128]{3,2,1,0:T(8,128)(2,1)}, bf16[2,2,264,128]{3,2,1,0:T(8,128)(2,1)}, u32[]{:S(2)}, u32[]{:S(2)}) %collective-permute-start.7) | collective-permute-done | bytes 270368 | tf_op jit(solution)/shard_map/ppermute | solution.py:360
  35.2 3.6 %collective-permute-start.11 = (bf16[2,2,264,128]{3,2,1,0:T(8,128)(2,1)S(1)}, bf16[2,2,264,128]{3,2,1,0:T(8,128)(2,1)S(1)}, u32[]{:S(2)}, u32[]{:S(2)}) collective-permute-start(bf16[2,2,264,128]{3,2,1,0:T(8,128)(2,1)S(1)} %copy-done.2), channel_id=1, source_target_pairs={{0,128},{2,130},{4,132},{6,134},{8,136},{10,138},{12,140},{14,142}... | collective-permute-start | bytes 811016 | tf_op jit(solution)/shard_map/ppermute | solution.py:360
  38.8 2.4 %collective-permute-start.9 = (bf16[2,2,264,128]{3,2,1,0:T(8,128)(2,1)S(1)}, bf16[2,2,264,128]{3,2,1,0:T(8,128)(2,1)S(1)}, u32[]{:S(2)}, u32[]{:S(2)}) collective-permute-start(bf16[2,2,264,128]{3,2,1,0:T(8,128)(2,1)S(1)} %copy-done.2), channel_id=1, source_target_pairs={{0,32},{2,34},{4,36},{6,38},{8,40},{10,42},{12,44},{14,46},{16,48}... | collective-permute-start | bytes 811016 | tf_op jit(solution)/shard_map/ppermute | solution.py:360
  41.7 1.0 copy-done.3
  42.7 15.6 %attend.2 = (bf16[2,1024,128]{2,1,0:T(8,128)(2,1)S(1)}, bf16[2,1024,128]{2,1,0:T(8,128)(2,1)S(1)}, f32[2,2,256,128]{3,2,1,0:T(8,128)S(1)}, bf16[4,2,128,128]{3,2...) custom-call(s32[16]{0:T(128)S(1)} %pad_add_fusion.scalars, ...), custom_call_target="tpu_custom_call" | custom-call | flops 4026531840 | bytes 6291456 | tf_op jit(solution)/shard_map/attend/pallas_call | solution.py:442
  59.2 2.9 %collective-permute-start.13 = (bf16[2,2,264,128]{3,2,1,0:T(8,128)(2,1)S(1)}, bf16[2,2,264,128]{3,2,1,0:T(8,128)(2,1)S(1)}, u32[]{:S(2)}, u32[]{:S(2)}) collective-permute-start(bf16[2,2,264,128]{3,2,1,0:T(8,128)(2,1)S(1)} %get-tuple-element.84), channel_id=1, source_target_pairs={{0,192},{2,194},{4,196},{6,198},{8,200},{10,202},{12,204},{14,206}... | collective-permute-start | bytes 811016 | tf_op jit(solution)/shard_map/ppermute | solution.py:360
  62.1 2.0 %collective-permute-done.9.refs_6_ = bf16[2,2,264,128]{3,2,1,0:T(8,128)(2,1)S(1)} collective-permute-done((bf16[2,2,264,128]{3,2,1,0:T(8,128)(2,1)S(1)}, bf16[2,2,264,128]{3,2,1,0:T(8,128)(2,1)S(1)}, u32[]{:S(2)}, u32[]{:S(2)}) %collective-permute-start.9) | collective-permute-done | bytes 270368 | tf_op jit(solution)/shard_map/ppermute | solution.py:360
  64.1 16.2 %attend.3 = (bf16[2,1024,128]{2,1,0:T(8,128)(2,1)S(1)}, bf16[2,1024,128]{2,1,0:T(8,128)(2,1)S(1)}, f32[2,2,256,128]{3,2,1,0:T(8,128)S(1)}, bf16[4,2,128,128]{3,2...) custom-call(s32[16]{0:T(128)S(1)} %pad_add_fusion.scalars, ...), custom_call_target="tpu_custom_call", output_to_operand_aliasing={{3}: (12, {}), {4}: (13, {}), {5}: (14, {}), {6}: (15, {}),... | custom-call | flops 4026531840 | bytes 6291456 | tf_op jit(solution)/shard_map/attend/pallas_call | solution.py:442
  82.1 3.8 %collective-permute-start.16 = (bf16[2,2,264,128]{3,2,1,0:T(8,128)(2,1)S(1)}, bf16[2,2,264,128]{3,2,1,0:T(8,128)(2,1)S(1)}, u32[]{:S(2)}, u32[]{:S(2)}) collective-permute-start(bf16[2,2,264,128]{3,2,1,0:T(8,128)(2,1)S(1)} %get-tuple-element.88), channel_id=1, source_target_pairs={{0,192},{2,194},{4,196},{6,198},{8,200},{10,202},{12,204},{14,206}... | collective-permute-start | bytes 811016 | tf_op jit(solution)/shard_map/ppermute | solution.py:360
  86.3 5.2 %collective-permute-start.21 = (bf16[4,2,128,128]{3,2,1,0:T(8,128)(2,1)S(1)}, bf16[4,2,128,128]{3,2,1,0:T(8,128)(2,1)S(1)}, u32[]{:S(2)}, u32[]{:S(2)}) collective-permute-start(bf16[4,2,128,128]{3,2,1,0:T(8,128)(2,1)S(1)} %get-tuple-element.95), channel_id=1, source_target_pairs={{2,4},{4,2},{6,8},{8,6},{10,12},{12,10},{14,16},{16,14},{18,20},{2... | collective-permute-start | bytes 786440 | tf_op jit(solution)/shard_map/ppermute | solution.py:367
  91.5 5.9 %collective-permute-done.16 = bf16[2,2,264,128]{3,2,1,0:T(8,128)(2,1)S(1)} collective-permute-done((bf16[2,2,264,128]{3,2,1,0:T(8,128)(2,1)S(1)}, bf16[2,2,264,128]{3,2,1,0:T(8,128)(2,1)S(1)}, u32[]{:S(2)}, u32[]{:S(2)}) %collective-permute-start.16) | collective-permute-done | bytes 270368 | tf_op jit(solution)/shard_map/ppermute | solution.py:360
  97.4 2.7 %collective-permute-done.17.refs_8_ = bf16[2,2,264,128]{3,2,1,0:T(8,128)(2,1)S(1)} collective-permute-done((bf16[2,2,264,128]{3,2,1,0:T(8,128)(2,1)S(1)}, bf16[2,2,264,128]{3,2,1,0:T(8,128)(2,1)S(1)}, u32[]{:S(2)}, u32[]{:S(2)}) %collective-permute-start.17) | collective-permute-done | bytes 270368 | tf_op jit(solution)/shard_map/ppermute | solution.py:360
  100.1 1.9 %collective-permute-start.22 = (bf16[2,1024,128]{2,1,0:T(8,128)(2,1)S(1)}, bf16[2,1024,128]{2,1,0:T(8,128)(2,1)S(1)}, u32[]{:S(2)}, u32[]{:S(2)}) collective-permute-start(bf16[2,1024,128]{2,1,0:T(8,128)(2,1)S(1)} %get-tuple-element.98), channel_id=1, source_target_pairs={{0,1},{1,0},{2,3},{3,2},{4,5},{5,4},{6,7},{7,6},{8,9},{9,8},{10,11... | collective-permute-start | bytes 1572872 | tf_op jit(solution)/shard_map/ppermute | solution.py:371
  102.1 5.6 %collective-permute-start.23 = (bf16[4,2,256,128]{3,2,1,0:T(8,128)(2,1)S(1)}, bf16[4,2,256,128]{3,2,1,0:T(8,128)(2,1)S(1)}, u32[]{:S(2)}, u32[]{:S(2)}) collective-permute-start(bf16[4,2,256,128]{3,2,1,0:T(8,128)(2,1)S(1)} %add_convert_fusion), channel_id=1, source_target_pairs={{0,4},{2,6},{4,0},{6,2},{8,12},{10,14},{12,8},{14,10},{16,20},{18,... | collective-permute-start | bytes 1572872 | tf_op jit(solution)/shard_map/ppermute | solution.py:360
  107.7 2.0 %collective-permute-start.24 = (bf16[2,2,264,128]{3,2,1,0:T(8,128)(2,1)S(1)}, bf16[2,2,264,128]{3,2,1,0:T(8,128)(2,1)S(1)}, u32[]{:S(2)}, u32[]{:S(2)}) collective-permute-start(bf16[2,2,264,128]{3,2,1,0:T(8,128)(2,1)S(1)} %get-tuple-element.108), channel_id=1, source_target_pairs={{0,32},{2,34},{4,36},{6,38},{8,40},{10,42},{12,44},{14,46},{16,48}... | collective-permute-start | bytes 811016 | tf_op jit(solution)/shard_map/ppermute | solution.py:360
  109.9 3.9 %collective-permute-done.22.refs_3_ = bf16[2,1024,128]{2,1,0:T(8,128)(2,1)S(1)} collective-permute-done((bf16[2,1024,128]{2,1,0:T(8,128)(2,1)S(1)}, bf16[2,1024,128]{2,1,0:T(8,128)(2,1)S(1)}, u32[]{:S(2)}, u32[]{:S(2)}) %collective-permute-start.22) | collective-permute-done | bytes 524320 | tf_op jit(solution)/shard_map/ppermute | solution.py:371
  113.8 2.3 %finish_sides.1 = (bf16[4096,128]{1,0:T(8,128)(2,1)}, bf16[4096,128]{1,0:T(8,128)(2,1)}) custom-call(s32[1]{0:T(128)} %bitcast.scalars, bf16[2,1024,128]{2,1,0:T(8,128)(2,1)S(1)} %get-tuple-element.67.refs_0_, bf16[2,1024,128]{2,1,0:T(8,128)(2,1)S(1)} %get-tuple-element.78.refs_1_, bf16[2,1024,128]{2,1,0:T(8,128)(2,1)S(1)} %collective-permute-done.14.refs_2_, ...), custom_call_target="tpu_custom_call" | custom-call | tf_op jit(solution)/shard_map/finish_sides/pallas_call | solution.py:484
  116.2 5.1 %collective-permute-done.24.refs_7_ = bf16[2,2,264,128]{3,2,1,0:T(8,128)(2,1)S(1)} collective-permute-done((bf16[2,2,264,128]{3,2,1,0:T(8,128)(2,1)S(1)}, bf16[2,2,264,128]{3,2,1,0:T(8,128)(2,1)S(1)}, u32[]{:S(2)}, u32[]{:S(2)}) %collective-permute-start.24) | collective-permute-done | bytes 270368 | tf_op jit(solution)/shard_map/ppermute | solution.py:360
  121.3 2.2 %collective-permute-done.25.refs_9_ = bf16[2,2,264,128]{3,2,1,0:T(8,128)(2,1)S(1)} collective-permute-done((bf16[2,2,264,128]{3,2,1,0:T(8,128)(2,1)S(1)}, bf16[2,2,264,128]{3,2,1,0:T(8,128)(2,1)S(1)}, u32[]{:S(2)}, u32[]{:S(2)}) %collective-permute-start.25) | collective-permute-done | bytes 270368 | tf_op jit(solution)/shard_map/ppermute | solution.py:360
  123.5 1.9 %finish_pairs.1 = (bf16[1024,128]{1,0:T(8,128)(2,1)}, bf16[1024,128]{1,0:T(8,128)(2,1)}) custom-call(s32[1]{0:T(128)} %bitcast.2.scalars, bf16[4,2,128,128]{3,2,1,0:T(8,128)(2,1)S(1)} %collective-permute-done.21.refs_0_, bf16[4,2,256,128]{3,2,1,0:T(8,128)(2,1)S(1)} %collective-permute-done.20.refs_1_, ...), custom_call_target="tpu_custom_call" | custom-call | tf_op jit(solution)/shard_map/finish_pairs/pallas_call | solution.py:494
  (51 shorter events, 6.3 us)
Async XLA Ops:
  3.5 7.6 %collective-permute-start = (bf16[4,2,256,128]{3,2,1,0:T(8,128)(2,1)}, bf16[4,2,256,128]{3,2,1,0:T(8,128)(2,1)S(1)}, u32[]{:S(2)}, u32[]{:S(2)}) collective-permute-start(bf16[4,2,256,128]{3,2,1,0:T(8,128)(2,1)} %get-tuple-element.61), channel_id=1, source_target_pairs={{0,2},{2,0},{4,6},{6,4},{8,10},{10,8},{12,14},{14,12},{16,18},{18,... | collective-permute-start | bytes 1572872 | tf_op jit(solution)/shard_map/ppermute | solution.py:360
  4.2 14.5 %collective-permute-start.2 = (bf16[4,2,256,128]{3,2,1,0:T(8,128)(2,1)}, bf16[4,2,256,128]{3,2,1,0:T(8,128)(2,1)}, u32[]{:S(2)}, u32[]{:S(2)}) collective-permute-start(bf16[4,2,256,128]{3,2,1,0:T(8,128)(2,1)} %get-tuple-element.61), channel_id=1, source_target_pairs={{0,4},{2,6},{4,0},{6,2},{8,12},{10,14},{12,8},{14,10},{16,20},{18,... | collective-permute-start | bytes 1572872 | tf_op jit(solution)/shard_map/ppermute | solution.py:360
  5.2 15.7 %collective-permute-start.6 = (bf16[2,2,264,128]{3,2,1,0:T(8,128)(2,1)}, bf16[2,2,264,128]{3,2,1,0:T(8,128)(2,1)}, u32[]{:S(2)}, u32[]{:S(2)}) collective-permute-start(bf16[2,2,264,128]{3,2,1,0:T(8,128)(2,1)} %get-tuple-element.59.refs_0_), channel_id=1, source_target_pairs={{0,64},{2,66},{4,68},{6,70},{8,72},{10,74},{12,76},{14,78},{16,80}... | collective-permute-start | bytes 811016 | tf_op jit(solution)/shard_map/ppermute | solution.py:360
  8.2 16.1 %collective-permute-start.5 = (bf16[2,2,264,128]{3,2,1,0:T(8,128)(2,1)}, bf16[2,2,264,128]{3,2,1,0:T(8,128)(2,1)}, u32[]{:S(2)}, u32[]{:S(2)}) collective-permute-start(bf16[2,2,264,128]{3,2,1,0:T(8,128)(2,1)} %get-tuple-element.59.refs_0_), channel_id=1, source_target_pairs={{0,32},{2,34},{4,36},{6,38},{8,40},{10,42},{12,44},{14,46},{16,48}... | collective-permute-start | bytes 811016 | tf_op jit(solution)/shard_map/ppermute | solution.py:360
  9.9 18.9 %collective-permute-start.4 = (bf16[4,2,256,128]{3,2,1,0:T(8,128)(2,1)}, bf16[4,2,256,128]{3,2,1,0:T(8,128)(2,1)}, u32[]{:S(2)}, u32[]{:S(2)}) collective-permute-start(bf16[4,2,256,128]{3,2,1,0:T(8,128)(2,1)} %get-tuple-element.61), channel_id=1, source_target_pairs={{0,16},{2,18},{4,20},{6,22},{8,24},{10,26},{12,28},{14,30},{16,0},... | collective-permute-start | bytes 1572872 | tf_op jit(solution)/shard_map/ppermute | solution.py:360
  11.0 1.2 copy-start
  12.3 1.2 copy-start.1
  13.5 21.7 %copy-start.2 = (bf16[2,2,264,128]{3,2,1,0:T(8,128)(2,1)S(1)}, bf16[2,2,264,128]{3,2,1,0:T(8,128)(2,1)}, u32[]{:S(2)}) copy-start(bf16[2,2,264,128]{3,2,1,0:T(8,128)(2,1)} %get-tuple-element.70.refs_0_) | copy-start | bytes 811012
  16.8 11.6 %copy-start.6 = (s32[7]{0:T(128)S(1)}, s32[7]{0:T(128)}, u32[]{:S(2)}) copy-start(s32[7]{0:T(128)} %param.12) | copy-start | bytes 88
  16.8 24.9 %collective-permute-start.8 = (bf16[2,1040,128]{2,1,0:T(8,128)(2,1)S(1)}, bf16[2,1040,128]{2,1,0:T(8,128)(2,1)S(1)}, u32[]{:S(2)}, u32[]{:S(2)}) collective-permute-start(bf16[2,1040,128]{2,1,0:T(8,128)(2,1)S(1)} %get-tuple-element.66), channel_id=1, source_target_pairs={{0,1},{1,0},{2,3},{3,2},{4,5},{5,4},{6,7},{7,6},{8,9},{9,8},{10,11... | collective-permute-start | bytes 1597448 | tf_op jit(solution)/shard_map/ppermute | solution.py:371
  18.7 22.5 %collective-permute-start.3 = (bf16[4,2,256,128]{3,2,1,0:T(8,128)(2,1)}, bf16[4,2,256,128]{3,2,1,0:T(8,128)(2,1)}, u32[]{:S(2)}, u32[]{:S(2)}) collective-permute-start(bf16[4,2,256,128]{3,2,1,0:T(8,128)(2,1)} %collective-permute-done.2.refs_3_), channel_id=1, source_target_pairs={{0,12},{2,14},{4,8},{6,10},{8,4},{10,6},{12,0},{14,2},{16,28},{18,... | collective-permute-start | bytes 1572872 | tf_op jit(solution)/shard_map/ppermute | solution.py:360
  21.0 14.2 %collective-permute-start.7 = (bf16[2,2,264,128]{3,2,1,0:T(8,128)(2,1)}, bf16[2,2,264,128]{3,2,1,0:T(8,128)(2,1)}, u32[]{:S(2)}, u32[]{:S(2)}) collective-permute-start(bf16[2,2,264,128]{3,2,1,0:T(8,128)(2,1)} %collective-permute-done.6.refs_7_), channel_id=1, source_target_pairs={{0,192},{2,194},{4,196},{6,198},{8,200},{10,202},{12,204},{14,206}... | collective-permute-start | bytes 811016 | tf_op jit(solution)/shard_map/ppermute | solution.py:360
  24.4 4.0 %copy-start.5 = (s32[2,7]{1,0:T(2,128)S(1)}, s32[2,7]{1,0:T(2,128)}, u32[]{:S(2)}) copy-start(s32[2,7]{1,0:T(2,128)} %param.13) | copy-start | bytes 172
  24.4 14.4 %collective-permute-start.1 = (bf16[4,2,128,128]{3,2,1,0:T(8,128)(2,1)}, bf16[4,2,128,128]{3,2,1,0:T(8,128)(2,1)}, u32[]{:S(2)}, u32[]{:S(2)}) collective-permute-start(bf16[4,2,128,128]{3,2,1,0:T(8,128)(2,1)} %get-tuple-element.62), channel_id=1, source_target_pairs={{2,4},{4,2},{6,8},{8,6},{10,12},{12,10},{14,16},{16,14},{18,20},{2... | collective-permute-start | bytes 786440 | tf_op jit(solution)/shard_map/ppermute | solution.py:367
  28.8 35.3 %collective-permute-start.12 = (bf16[2,1040,128]{2,1,0:T(8,128)(2,1)S(1)}, bf16[2,1040,128]{2,1,0:T(8,128)(2,1)S(1)}, u32[]{:S(2)}, u32[]{:S(2)}) collective-permute-start(bf16[2,1040,128]{2,1,0:T(8,128)(2,1)S(1)} %get-tuple-element.72), channel_id=1, source_target_pairs={{0,1},{1,0},{2,3},{3,2},{4,5},{5,4},{6,7},{7,6},{8,9},{9,8},{10,11... | collective-permute-start | bytes 1597448 | tf_op jit(solution)/shard_map/ppermute | solution.py:371
  35.2 24.0 %collective-permute-start.11 = (bf16[2,2,264,128]{3,2,1,0:T(8,128)(2,1)S(1)}, bf16[2,2,264,128]{3,2,1,0:T(8,128)(2,1)S(1)}, u32[]{:S(2)}, u32[]{:S(2)}) collective-permute-start(bf16[2,2,264,128]{3,2,1,0:T(8,128)(2,1)S(1)} %copy-done.2), channel_id=1, source_target_pairs={{0,128},{2,130},{4,132},{6,134},{8,136},{10,138},{12,140},{14,142}... | collective-permute-start | bytes 811016 | tf_op jit(solution)/shard_map/ppermute | solution.py:360
  38.8 25.3 %collective-permute-start.9 = (bf16[2,2,264,128]{3,2,1,0:T(8,128)(2,1)S(1)}, bf16[2,2,264,128]{3,2,1,0:T(8,128)(2,1)S(1)}, u32[]{:S(2)}, u32[]{:S(2)}) collective-permute-start(bf16[2,2,264,128]{3,2,1,0:T(8,128)(2,1)S(1)} %copy-done.2), channel_id=1, source_target_pairs={{0,32},{2,34},{4,36},{6,38},{8,40},{10,42},{12,44},{14,46},{16,48}... | collective-permute-start | bytes 811016 | tf_op jit(solution)/shard_map/ppermute | solution.py:360
  41.2 22.9 %collective-permute-start.10 = (bf16[2,2,264,128]{3,2,1,0:T(8,128)(2,1)S(1)}, bf16[2,2,264,128]{3,2,1,0:T(8,128)(2,1)S(1)}, u32[]{:S(2)}, u32[]{:S(2)}) collective-permute-start(bf16[2,2,264,128]{3,2,1,0:T(8,128)(2,1)S(1)} %copy-done.2), channel_id=1, source_target_pairs={{0,64},{2,66},{4,68},{6,70},{8,72},{10,74},{12,76},{14,78},{16,80}... | collective-permute-start | bytes 811016 | tf_op jit(solution)/shard_map/ppermute | solution.py:360
  41.7 1.0 copy-start.3
  58.3 22.1 %collective-permute-start.14 = (bf16[2,1024,128]{2,1,0:T(8,128)(2,1)S(1)}, bf16[2,1024,128]{2,1,0:T(8,128)(2,1)S(1)}, u32[]{:S(2)}, u32[]{:S(2)}) collective-permute-start(bf16[2,1024,128]{2,1,0:T(8,128)(2,1)S(1)} %get-tuple-element.85), channel_id=1, source_target_pairs={{0,1},{1,0},{2,3},{3,2},{4,5},{5,4},{6,7},{7,6},{8,9},{9,8},{10,11... | collective-permute-start | bytes 1572872 | tf_op jit(solution)/shard_map/ppermute | solution.py:371
  59.2 21.1 %collective-permute-start.13 = (bf16[2,2,264,128]{3,2,1,0:T(8,128)(2,1)S(1)}, bf16[2,2,264,128]{3,2,1,0:T(8,128)(2,1)S(1)}, u32[]{:S(2)}, u32[]{:S(2)}) collective-permute-start(bf16[2,2,264,128]{3,2,1,0:T(8,128)(2,1)S(1)} %get-tuple-element.84), channel_id=1, source_target_pairs={{0,192},{2,194},{4,196},{6,198},{8,200},{10,202},{12,204},{14,206}... | collective-permute-start | bytes 811016 | tf_op jit(solution)/shard_map/ppermute | solution.py:360
  64.1 16.2 %collective-permute-start.15 = (bf16[2,2,264,128]{3,2,1,0:T(8,128)(2,1)S(1)}, bf16[2,2,264,128]{3,2,1,0:T(8,128)(2,1)S(1)}, u32[]{:S(2)}, u32[]{:S(2)}) collective-permute-start(bf16[2,2,264,128]{3,2,1,0:T(8,128)(2,1)S(1)} %get-tuple-element.86), channel_id=1, source_target_pairs={{0,32},{2,34},{4,36},{6,38},{8,40},{10,42},{12,44},{14,46},{16,48}... | collective-permute-start | bytes 811016 | tf_op jit(solution)/shard_map/ppermute | solution.py:360
  80.4 5.9 %collective-permute-start.20 = (bf16[4,2,256,128]{3,2,1,0:T(8,128)(2,1)S(1)}, bf16[4,2,256,128]{3,2,1,0:T(8,128)(2,1)S(1)}, u32[]{:S(2)}, u32[]{:S(2)}) collective-permute-start(bf16[4,2,256,128]{3,2,1,0:T(8,128)(2,1)S(1)} %get-tuple-element.94), channel_id=1, source_target_pairs={{0,2},{2,0},{4,6},{6,4},{8,10},{10,8},{12,14},{14,12},{16,18},{18,... | collective-permute-start | bytes 1572872 | tf_op jit(solution)/shard_map/ppermute | solution.py:360
  81.1 19.0 %collective-permute-start.18 = (bf16[4,2,256,128]{3,2,1,0:T(8,128)(2,1)S(1)}, bf16[4,2,256,128]{3,2,1,0:T(8,128)(2,1)S(1)}, u32[]{:S(2)}, u32[]{:S(2)}) collective-permute-start(bf16[4,2,256,128]{3,2,1,0:T(8,128)(2,1)S(1)} %get-tuple-element.91), channel_id=1, source_target_pairs={{0,12},{2,14},{4,8},{6,10},{8,4},{10,6},{12,0},{14,2},{16,28},{18,... | collective-permute-start | bytes 1572872 | tf_op jit(solution)/shard_map/ppermute | solution.py:360
  81.6 18.5 %collective-permute-start.19 = (bf16[4,2,256,128]{3,2,1,0:T(8,128)(2,1)S(1)}, bf16[4,2,256,128]{3,2,1,0:T(8,128)(2,1)S(1)}, u32[]{:S(2)}, u32[]{:S(2)}) collective-permute-start(bf16[4,2,256,128]{3,2,1,0:T(8,128)(2,1)S(1)} %get-tuple-element.92), channel_id=1, source_target_pairs={{0,16},{2,18},{4,20},{6,22},{8,24},{10,26},{12,28},{14,30},{16,0},... | collective-permute-start | bytes 1572872 | tf_op jit(solution)/shard_map/ppermute | solution.py:360
  82.1 15.3 %collective-permute-start.16 = (bf16[2,2,264,128]{3,2,1,0:T(8,128)(2,1)S(1)}, bf16[2,2,264,128]{3,2,1,0:T(8,128)(2,1)S(1)}, u32[]{:S(2)}, u32[]{:S(2)}) collective-permute-start(bf16[2,2,264,128]{3,2,1,0:T(8,128)(2,1)S(1)} %get-tuple-element.88), channel_id=1, source_target_pairs={{0,192},{2,194},{4,196},{6,198},{8,200},{10,202},{12,204},{14,206}... | collective-permute-start | bytes 811016 | tf_op jit(solution)/shard_map/ppermute | solution.py:360
  86.0 14.2 %collective-permute-start.17 = (bf16[2,2,264,128]{3,2,1,0:T(8,128)(2,1)S(1)}, bf16[2,2,264,128]{3,2,1,0:T(8,128)(2,1)S(1)}, u32[]{:S(2)}, u32[]{:S(2)}) collective-permute-start(bf16[2,2,264,128]{3,2,1,0:T(8,128)(2,1)S(1)} %add_convert_fusion.2), channel_id=1, source_target_pairs={{0,64},{2,66},{4,68},{6,70},{8,72},{10,74},{12,76},{14,78},{16,80}... | collective-permute-start | bytes 811016 | tf_op jit(solution)/shard_map/ppermute | solution.py:360
  86.3 13.8 %collective-permute-start.21 = (bf16[4,2,128,128]{3,2,1,0:T(8,128)(2,1)S(1)}, bf16[4,2,128,128]{3,2,1,0:T(8,128)(2,1)S(1)}, u32[]{:S(2)}, u32[]{:S(2)}) collective-permute-start(bf16[4,2,128,128]{3,2,1,0:T(8,128)(2,1)S(1)} %get-tuple-element.95), channel_id=1, source_target_pairs={{2,4},{4,2},{6,8},{8,6},{10,12},{12,10},{14,16},{16,14},{18,20},{2... | collective-permute-start | bytes 786440 | tf_op jit(solution)/shard_map/ppermute | solution.py:367
  100.1 13.7 %collective-permute-start.22 = (bf16[2,1024,128]{2,1,0:T(8,128)(2,1)S(1)}, bf16[2,1024,128]{2,1,0:T(8,128)(2,1)S(1)}, u32[]{:S(2)}, u32[]{:S(2)}) collective-permute-start(bf16[2,1024,128]{2,1,0:T(8,128)(2,1)S(1)} %get-tuple-element.98), channel_id=1, source_target_pairs={{0,1},{1,0},{2,3},{3,2},{4,5},{5,4},{6,7},{7,6},{8,9},{9,8},{10,11... | collective-permute-start | bytes 1572872 | tf_op jit(solution)/shard_map/ppermute | solution.py:371
  102.1 21.3 %collective-permute-start.23 = (bf16[4,2,256,128]{3,2,1,0:T(8,128)(2,1)S(1)}, bf16[4,2,256,128]{3,2,1,0:T(8,128)(2,1)S(1)}, u32[]{:S(2)}, u32[]{:S(2)}) collective-permute-start(bf16[4,2,256,128]{3,2,1,0:T(8,128)(2,1)S(1)} %add_convert_fusion), channel_id=1, source_target_pairs={{0,4},{2,6},{4,0},{6,2},{8,12},{10,14},{12,8},{14,10},{16,20},{18,... | collective-permute-start | bytes 1572872 | tf_op jit(solution)/shard_map/ppermute | solution.py:360
  107.7 13.6 %collective-permute-start.24 = (bf16[2,2,264,128]{3,2,1,0:T(8,128)(2,1)S(1)}, bf16[2,2,264,128]{3,2,1,0:T(8,128)(2,1)S(1)}, u32[]{:S(2)}, u32[]{:S(2)}) collective-permute-start(bf16[2,2,264,128]{3,2,1,0:T(8,128)(2,1)S(1)} %get-tuple-element.108), channel_id=1, source_target_pairs={{0,32},{2,34},{4,36},{6,38},{8,40},{10,42},{12,44},{14,46},{16,48}... | collective-permute-start | bytes 811016 | tf_op jit(solution)/shard_map/ppermute | solution.py:360
  109.8 13.6 %collective-permute-start.25 = (bf16[2,2,264,128]{3,2,1,0:T(8,128)(2,1)S(1)}, bf16[2,2,264,128]{3,2,1,0:T(8,128)(2,1)S(1)}, u32[]{:S(2)}, u32[]{:S(2)}) collective-permute-start(bf16[2,2,264,128]{3,2,1,0:T(8,128)(2,1)S(1)} %add_convert_fusion.1), channel_id=1, source_target_pairs={{0,64},{2,66},{4,68},{6,70},{8,72},{10,74},{12,76},{14,78},{16,80}... | collective-permute-start | bytes 811016 | tf_op jit(solution)/shard_map/ppermute | solution.py:360
  (1 other events, 0.7 us)

commit v5 on v4

--- a/solution.py
+++ b/solution.py
@@ -464,21 +464,21 @@
     second = attend(1, own_b, keep_b, other_b, z1_b, z2_b, z4_b, first[3:8])
     keep_out_b, other_out_b, terms_b, ext_terms, core_terms, y1_terms, y2_terms = second[:7]
     x_terms, z1_terms_b, z2_terms_b, z4_terms_b = second[7:]
-    to_z6, to_y3, to_x, to_ext, to_core, far_a, swapped_a, back_z1_a = lax.optimization_barrier(
-        (z4_terms_b, y2_terms, x_terms, ext_terms, core_terms, far_a, swapped_a, back_z1_a)
+    to_z6, to_y3, to_head, to_ext, to_core, far_a, swapped_a, back_z1_a = lax.optimization_barrier(
+        (z4_terms_b, y2_terms, other_out_b, ext_terms, core_terms, far_a, swapped_a, back_z1_a)
     )
     far_b = flipped(to_z6, 96)
     back_z2_a = flipped(added(z2_terms_a, far_a), 32)
     near = flipped(to_y3, 6)
     back_core = flipped(to_core, 1)
-    back_x = flipped(to_x, 8)
+    swapped_b = other_head(to_head)
     back_ext = past_end(lax.optimization_barrier((to_ext, back_core))[0])
-    far_b, back_z2_a, near, back_x, back_ext, z1_terms_b, other_out_b = lax.optimization_barrier(
-        (far_b, back_z2_a, near, back_x, back_ext, z1_terms_b, other_out_b)
+    far_b, back_z2_a, near, swapped_b, back_ext, z1_terms_b, x_terms = lax.optimization_barrier(
+        (far_b, back_z2_a, near, swapped_b, back_ext, z1_terms_b, x_terms)
     )
     back_z2_b = flipped(added(z2_terms_b, far_b), 32)
     back_y = flipped(added(y1_terms, near), 2)
-    swapped_b = other_head(other_out_b)
+    back_x = flipped(x_terms, 8)
     back_z1_b = flipped(z1_terms_b, 16)
 
     out, dquery = pl.pallas_call(

time: 126 us -> 126 us (level)
  the two profiles are of different devices: /device:TPU:21 before, /device:TPU:17 now
where the time goes in v5:
time: 126 us
  starting transfers between devices  50.6 us (40%)
  Pallas kernels  42.1 us (33%)
  waiting for transfers between devices  27 us (21%)
  local copies, waits for them, and re-layouts  4.44 us (4%)
    ppermute x20, starting transfers between devices, flipped(): lax.ppermute(value, 'seq', [(i, i ^ mask) for i in range(lax.axis_size('s...  37.4 us
    pallas_call x2, Pallas kernels, attend(): pl.pallas_call(functools.partial(attend_kernel, chunk * PER, len(reused))...  31.8 us
    ppermute x20, waiting for transfers between devices, flipped(): lax.ppermute(value, 'seq', [(i, i ^ mask) for i in range(lax.axis_size('s...  27 us
    ppermute x2, starting transfers between devices, past_end(): return lax.ppermute(value, 'seq', pairs)  9.32 us
    unnamed x15, local copies, waits for them, and re-layouts  4.18 us
    ppermute x4, starting transfers between devices, other_head(): return lax.ppermute(value, 'head', [(0, 1), (1, 0)])  3.89 us
    pallas_call x1, Pallas kernels, shards(): pl.pallas_call(pack_sides_kernel, out_shape=[sides] * (2 * CHUNKS), in_sp...  3.29 us
    pallas_call x1, Pallas kernels, shards(): pl.pallas_call(pack_pairs_kernel, out_shape=[whole, padded, padded, ends]...  2.83 us
  transfers between devices with their start and end apart: 26, of which 7 were waited for; matrix products, arithmetic and copies ran while one was open for 1% of the time, Pallas kernels for 30%

profile of v5, /device:TPU:17, one launch (start us, length us, event | category | flops | bytes accessed | tf_op | source)
XLA Modules:
  0.0 125.8 jit_solution(3857329252167840224)
XLA Ops:
  0.6 2.8 %pack_pairs.1 = (bf16[4,2,256,128]{3,2,1,0:T(8,128)(2,1)}, bf16[2,2,264,128]{3,2,1,0:T(8,128)(2,1)}, bf16[2,2,264,128]{3,2,1,0:T(8,128)(2,1)}, bf16[4,2,128,128]{3,2,1,0:T(8,128)(2,1)}) custom-call(s32[1]{0:T(128)} %bitcast.2.scalars, bf16[1024,128]{1,0:T(8,128)(2,1)} %bitcast.13, bf16[1024,128]{1,0:T(8,128)(2,1)} %bitcast.14), custom_call_target="tpu_custom_call" | custom-call | tf_op jit(solution)/shard_map/pack_pairs/pallas_call | solution.py:397
  4.2 1.0 collective-permute-start.2
  5.3 3.0 %collective-permute-start.6 = (bf16[2,2,264,128]{3,2,1,0:T(8,128)(2,1)}, bf16[2,2,264,128]{3,2,1,0:T(8,128)(2,1)}, u32[]{:S(2)}, u32[]{:S(2)}) collective-permute-start(bf16[2,2,264,128]{3,2,1,0:T(8,128)(2,1)} %get-tuple-element.59.refs_0_), channel_id=1, source_target_pairs={{0,64},{2,66},{4,68},{6,70},{8,72},{10,74},{12,76},{14,78},{16,80}... | collective-permute-start | bytes 811016 | tf_op jit(solution)/shard_map/ppermute | solution.py:360
  8.3 1.6 %collective-permute-start.5 = (bf16[2,2,264,128]{3,2,1,0:T(8,128)(2,1)}, bf16[2,2,264,128]{3,2,1,0:T(8,128)(2,1)}, u32[]{:S(2)}, u32[]{:S(2)}) collective-permute-start(bf16[2,2,264,128]{3,2,1,0:T(8,128)(2,1)} %get-tuple-element.59.refs_0_), channel_id=1, source_target_pairs={{0,32},{2,34},{4,36},{6,38},{8,40},{10,42},{12,44},{14,46},{16,48}... | collective-permute-start | bytes 811016 | tf_op jit(solution)/shard_map/ppermute | solution.py:360
  9.9 2.7 %collective-permute-start.4 = (bf16[4,2,256,128]{3,2,1,0:T(8,128)(2,1)}, bf16[4,2,256,128]{3,2,1,0:T(8,128)(2,1)}, u32[]{:S(2)}, u32[]{:S(2)}) collective-permute-start(bf16[4,2,256,128]{3,2,1,0:T(8,128)(2,1)} %get-tuple-element.61), channel_id=1, source_target_pairs={{0,16},{2,18},{4,20},{6,22},{8,24},{10,26},{12,28},{14,30},{16,0},... | collective-permute-start | bytes 1572872 | tf_op jit(solution)/shard_map/ppermute | solution.py:360
  13.6 1.2 copy-done
  14.8 1.2 copy-done.1
  16.0 3.3 %pack_sides.1 = (bf16[2,1040,128]{2,1,0:T(8,128)(2,1)S(1)}, bf16[2,1040,128]{2,1,0:T(8,128)(2,1)S(1)}, bf16[2,1040,128]{2,1,0:T(8,128)(2,1)S(1)}, bf16[2,1040,128]{2,1,0:T(8,128)(2,1)S(1)}) custom-call(s32[17]{0:T(128)S(1)} %pad_add_fusion.1.scalars, bf16[4096,128]{1,0:T(8,128)(2,1)S(1)} %bitcast.11, bf16[4096,128]{1,0:T(8,128)(2,1)S(1)} %bitcast.12, ...), custom_call_target="tpu_custom_call" | custom-call | tf_op jit(solution)/shard_map/pack_sides/pallas_call | solution.py:414
  19.7 1.2 collective-permute-done.6.refs_7_
  21.0 3.4 %collective-permute-start.7 = (bf16[2,2,264,128]{3,2,1,0:T(8,128)(2,1)}, bf16[2,2,264,128]{3,2,1,0:T(8,128)(2,1)}, u32[]{:S(2)}, u32[]{:S(2)}) collective-permute-start(bf16[2,2,264,128]{3,2,1,0:T(8,128)(2,1)} %collective-permute-done.6.refs_7_), channel_id=1, source_target_pairs={{0,192},{2,194},{4,196},{6,198},{8,200},{10,202},{12,204},{14,206}... | collective-permute-start | bytes 811016 | tf_op jit(solution)/shard_map/ppermute | solution.py:360
  24.3 4.0 %collective-permute-start.1 = (bf16[4,2,128,128]{3,2,1,0:T(8,128)(2,1)}, bf16[4,2,128,128]{3,2,1,0:T(8,128)(2,1)}, u32[]{:S(2)}, u32[]{:S(2)}) collective-permute-start(bf16[4,2,128,128]{3,2,1,0:T(8,128)(2,1)} %get-tuple-element.62), channel_id=1, source_target_pairs={{2,4},{4,2},{6,8},{8,6},{10,12},{12,10},{14,16},{16,14},{18,20},{2... | collective-permute-start | bytes 786440 | tf_op jit(solution)/shard_map/ppermute | solution.py:367
  28.8 1.2 collective-permute-start.12
  30.1 5.1 %collective-permute-done.7.refs_8_ = bf16[2,2,264,128]{3,2,1,0:T(8,128)(2,1)} collective-permute-done((bf16[2,2,264,128]{3,2,1,0:T(8,128)(2,1)}, bf16[2,2,264,128]{3,2,1,0:T(8,128)(2,1)}, u32[]{:S(2)}, u32[]{:S(2)}) %collective-permute-start.7) | collective-permute-done | bytes 270368 | tf_op jit(solution)/shard_map/ppermute | solution.py:360
  35.2 3.6 %collective-permute-start.11 = (bf16[2,2,264,128]{3,2,1,0:T(8,128)(2,1)S(1)}, bf16[2,2,264,128]{3,2,1,0:T(8,128)(2,1)S(1)}, u32[]{:S(2)}, u32[]{:S(2)}) collective-permute-start(bf16[2,2,264,128]{3,2,1,0:T(8,128)(2,1)S(1)} %copy-done.2), channel_id=1, source_target_pairs={{0,128},{2,130},{4,132},{6,134},{8,136},{10,138},{12,140},{14,142}... | collective-permute-start | bytes 811016 | tf_op jit(solution)/shard_map/ppermute | solution.py:360
  38.7 2.4 %collective-permute-start.9 = (bf16[2,2,264,128]{3,2,1,0:T(8,128)(2,1)S(1)}, bf16[2,2,264,128]{3,2,1,0:T(8,128)(2,1)S(1)}, u32[]{:S(2)}, u32[]{:S(2)}) collective-permute-start(bf16[2,2,264,128]{3,2,1,0:T(8,128)(2,1)S(1)} %copy-done.2), channel_id=1, source_target_pairs={{0,32},{2,34},{4,36},{6,38},{8,40},{10,42},{12,44},{14,46},{16,48}... | collective-permute-start | bytes 811016 | tf_op jit(solution)/shard_map/ppermute | solution.py:360
  42.6 15.6 %attend.2 = (bf16[2,1024,128]{2,1,0:T(8,128)(2,1)S(1)}, bf16[2,1024,128]{2,1,0:T(8,128)(2,1)S(1)}, f32[2,2,256,128]{3,2,1,0:T(8,128)S(1)}, bf16[4,2,128,128]{3,2...) custom-call(s32[16]{0:T(128)S(1)} %pad_add_fusion.scalars, ...), custom_call_target="tpu_custom_call" | custom-call | flops 4026531840 | bytes 6291456 | tf_op jit(solution)/shard_map/attend/pallas_call | solution.py:442
  58.2 1.3 %collective-permute-start.14 = (bf16[2,1024,128]{2,1,0:T(8,128)(2,1)S(1)}, bf16[2,1024,128]{2,1,0:T(8,128)(2,1)S(1)}, u32[]{:S(2)}, u32[]{:S(2)}) collective-permute-start(bf16[2,1024,128]{2,1,0:T(8,128)(2,1)S(1)} %get-tuple-element.85), channel_id=1, source_target_pairs={{0,1},{1,0},{2,3},{3,2},{4,5},{5,4},{6,7},{7,6},{8,9},{9,8},{10,11... | collective-permute-start | bytes 1572872 | tf_op jit(solution)/shard_map/ppermute | solution.py:371
  59.5 2.8 %collective-permute-start.13 = (bf16[2,2,264,128]{3,2,1,0:T(8,128)(2,1)S(1)}, bf16[2,2,264,128]{3,2,1,0:T(8,128)(2,1)S(1)}, u32[]{:S(2)}, u32[]{:S(2)}) collective-permute-start(bf16[2,2,264,128]{3,2,1,0:T(8,128)(2,1)S(1)} %get-tuple-element.84), channel_id=1, source_target_pairs={{0,192},{2,194},{4,196},{6,198},{8,200},{10,202},{12,204},{14,206}... | collective-permute-start | bytes 811016 | tf_op jit(solution)/shard_map/ppermute | solution.py:360
  62.3 1.8 %collective-permute-done.9.refs_6_ = bf16[2,2,264,128]{3,2,1,0:T(8,128)(2,1)S(1)} collective-permute-done((bf16[2,2,264,128]{3,2,1,0:T(8,128)(2,1)S(1)}, bf16[2,2,264,128]{3,2,1,0:T(8,128)(2,1)S(1)}, u32[]{:S(2)}, u32[]{:S(2)}) %collective-permute-start.9) | collective-permute-done | bytes 270368 | tf_op jit(solution)/shard_map/ppermute | solution.py:360
  64.1 16.2 %attend.3 = (bf16[2,1024,128]{2,1,0:T(8,128)(2,1)S(1)}, bf16[2,1024,128]{2,1,0:T(8,128)(2,1)S(1)}, f32[2,2,256,128]{3,2,1,0:T(8,128)S(1)}, bf16[4,2,128,128]{3,2...) custom-call(s32[16]{0:T(128)S(1)} %pad_add_fusion.scalars, ...), custom_call_target="tpu_custom_call", output_to_operand_aliasing={{3}: (12, {}), {4}: (13, {}), {5}: (14, {}), {6}: (15, {}),... | custom-call | flops 4026531840 | bytes 6291456 | tf_op jit(solution)/shard_map/attend/pallas_call | solution.py:442
  82.8 4.0 %collective-permute-start.16 = (bf16[2,2,264,128]{3,2,1,0:T(8,128)(2,1)S(1)}, bf16[2,2,264,128]{3,2,1,0:T(8,128)(2,1)S(1)}, u32[]{:S(2)}, u32[]{:S(2)}) collective-permute-start(bf16[2,2,264,128]{3,2,1,0:T(8,128)(2,1)S(1)} %get-tuple-element.88), channel_id=1, source_target_pairs={{0,192},{2,194},{4,196},{6,198},{8,200},{10,202},{12,204},{14,206}... | collective-permute-start | bytes 811016 | tf_op jit(solution)/shard_map/ppermute | solution.py:360
  87.2 5.3 %collective-permute-start.21 = (bf16[4,2,128,128]{3,2,1,0:T(8,128)(2,1)S(1)}, bf16[4,2,128,128]{3,2,1,0:T(8,128)(2,1)S(1)}, u32[]{:S(2)}, u32[]{:S(2)}) collective-permute-start(bf16[4,2,128,128]{3,2,1,0:T(8,128)(2,1)S(1)} %get-tuple-element.95), channel_id=1, source_target_pairs={{2,4},{4,2},{6,8},{8,6},{10,12},{12,10},{14,16},{16,14},{18,20},{2... | collective-permute-start | bytes 786440 | tf_op jit(solution)/shard_map/ppermute | solution.py:367
  92.5 5.8 %collective-permute-done.16 = bf16[2,2,264,128]{3,2,1,0:T(8,128)(2,1)S(1)} collective-permute-done((bf16[2,2,264,128]{3,2,1,0:T(8,128)(2,1)S(1)}, bf16[2,2,264,128]{3,2,1,0:T(8,128)(2,1)S(1)}, u32[]{:S(2)}, u32[]{:S(2)}) %collective-permute-start.16) | collective-permute-done | bytes 270368 | tf_op jit(solution)/shard_map/ppermute | solution.py:360
  98.3 2.8 %collective-permute-done.17.refs_8_ = bf16[2,2,264,128]{3,2,1,0:T(8,128)(2,1)S(1)} collective-permute-done((bf16[2,2,264,128]{3,2,1,0:T(8,128)(2,1)S(1)}, bf16[2,2,264,128]{3,2,1,0:T(8,128)(2,1)S(1)}, u32[]{:S(2)}, u32[]{:S(2)}) %collective-permute-start.17) | collective-permute-done | bytes 270368 | tf_op jit(solution)/shard_map/ppermute | solution.py:360
  101.2 2.8 %collective-permute-start.22 = (bf16[4,2,256,128]{3,2,1,0:T(8,128)(2,1)S(1)}, bf16[4,2,256,128]{3,2,1,0:T(8,128)(2,1)S(1)}, u32[]{:S(2)}, u32[]{:S(2)}) collective-permute-start(bf16[4,2,256,128]{3,2,1,0:T(8,128)(2,1)S(1)} %add_convert_fusion), channel_id=1, source_target_pairs={{0,4},{2,6},{4,0},{6,2},{8,12},{10,14},{12,8},{14,10},{16,20},{18,... | collective-permute-start | bytes 1572872 | tf_op jit(solution)/shard_map/ppermute | solution.py:360
  104.0 3.7 %collective-permute-start.23 = (bf16[4,2,256,128]{3,2,1,0:T(8,128)(2,1)S(1)}, bf16[4,2,256,128]{3,2,1,0:T(8,128)(2,1)S(1)}, u32[]{:S(2)}, u32[]{:S(2)}) collective-permute-start(bf16[4,2,256,128]{3,2,1,0:T(8,128)(2,1)S(1)} %get-tuple-element.104), channel_id=1, source_target_pairs={{0,16},{2,18},{4,20},{6,22},{8,24},{10,26},{12,28},{14,30},{16,0},... | collective-permute-start | bytes 1572872 | tf_op jit(solution)/shard_map/ppermute | solution.py:360
  107.7 2.4 %collective-permute-start.24 = (bf16[2,2,264,128]{3,2,1,0:T(8,128)(2,1)S(1)}, bf16[2,2,264,128]{3,2,1,0:T(8,128)(2,1)S(1)}, u32[]{:S(2)}, u32[]{:S(2)}) collective-permute-start(bf16[2,2,264,128]{3,2,1,0:T(8,128)(2,1)S(1)} %get-tuple-element.108), channel_id=1, source_target_pairs={{0,32},{2,34},{4,36},{6,38},{8,40},{10,42},{12,44},{14,46},{16,48}... | collective-permute-start | bytes 811016 | tf_op jit(solution)/shard_map/ppermute | solution.py:360
  110.2 1.0 collective-permute-start.25
  111.2 2.3 %finish_sides.1 = (bf16[4096,128]{1,0:T(8,128)(2,1)}, bf16[4096,128]{1,0:T(8,128)(2,1)}) custom-call(s32[1]{0:T(128)} %bitcast.scalars, bf16[2,1024,128]{2,1,0:T(8,128)(2,1)S(1)} %get-tuple-element.67.refs_0_, bf16[2,1024,128]{2,1,0:T(8,128)(2,1)S(1)} %get-tuple-element.78.refs_1_, bf16[2,1024,128]{2,1,0:T(8,128)(2,1)S(1)} %collective-permute-done.14.refs_2_, ...), custom_call_target="tpu_custom_call" | custom-call | tf_op jit(solution)/shard_map/finish_sides/pallas_call | solution.py:484
  113.5 9.0 %collective-permute-done.24.refs_7_ = bf16[2,2,264,128]{3,2,1,0:T(8,128)(2,1)S(1)} collective-permute-done((bf16[2,2,264,128]{3,2,1,0:T(8,128)(2,1)S(1)}, bf16[2,2,264,128]{3,2,1,0:T(8,128)(2,1)S(1)}, u32[]{:S(2)}, u32[]{:S(2)}) %collective-permute-start.24) | collective-permute-done | bytes 270368 | tf_op jit(solution)/shard_map/ppermute | solution.py:360
  122.5 1.2 collective-permute-done.25.refs_9_
  123.7 1.9 %finish_pairs.1 = (bf16[1024,128]{1,0:T(8,128)(2,1)}, bf16[1024,128]{1,0:T(8,128)(2,1)}) custom-call(s32[1]{0:T(128)} %bitcast.2.scalars, bf16[4,2,128,128]{3,2,1,0:T(8,128)(2,1)S(1)} %collective-permute-done.21.refs_0_, bf16[4,2,256,128]{3,2,1,0:T(8,128)(2,1)S(1)} %collective-permute-done.20.refs_1_, ...), custom_call_target="tpu_custom_call" | custom-call | tf_op jit(solution)/shard_map/finish_pairs/pallas_call | solution.py:494
  (51 shorter events, 7.1 us)
Async XLA Ops:
  3.5 10.1 %collective-permute-start = (bf16[4,2,256,128]{3,2,1,0:T(8,128)(2,1)}, bf16[4,2,256,128]{3,2,1,0:T(8,128)(2,1)S(1)}, u32[]{:S(2)}, u32[]{:S(2)}) collective-permute-start(bf16[4,2,256,128]{3,2,1,0:T(8,128)(2,1)} %get-tuple-element.61), channel_id=1, source_target_pairs={{0,2},{2,0},{4,6},{6,4},{8,10},{10,8},{12,14},{14,12},{16,18},{18,... | collective-permute-start | bytes 1572872 | tf_op jit(solution)/shard_map/ppermute | solution.py:360
  4.2 15.5 %collective-permute-start.2 = (bf16[4,2,256,128]{3,2,1,0:T(8,128)(2,1)}, bf16[4,2,256,128]{3,2,1,0:T(8,128)(2,1)}, u32[]{:S(2)}, u32[]{:S(2)}) collective-permute-start(bf16[4,2,256,128]{3,2,1,0:T(8,128)(2,1)} %get-tuple-element.61), channel_id=1, source_target_pairs={{0,4},{2,6},{4,0},{6,2},{8,12},{10,14},{12,8},{14,10},{16,20},{18,... | collective-permute-start | bytes 1572872 | tf_op jit(solution)/shard_map/ppermute | solution.py:360
  5.3 15.7 %collective-permute-start.6 = (bf16[2,2,264,128]{3,2,1,0:T(8,128)(2,1)}, bf16[2,2,264,128]{3,2,1,0:T(8,128)(2,1)}, u32[]{:S(2)}, u32[]{:S(2)}) collective-permute-start(bf16[2,2,264,128]{3,2,1,0:T(8,128)(2,1)} %get-tuple-element.59.refs_0_), channel_id=1, source_target_pairs={{0,64},{2,66},{4,68},{6,70},{8,72},{10,74},{12,76},{14,78},{16,80}... | collective-permute-start | bytes 811016 | tf_op jit(solution)/shard_map/ppermute | solution.py:360
  8.3 16.1 %collective-permute-start.5 = (bf16[2,2,264,128]{3,2,1,0:T(8,128)(2,1)}, bf16[2,2,264,128]{3,2,1,0:T(8,128)(2,1)}, u32[]{:S(2)}, u32[]{:S(2)}) collective-permute-start(bf16[2,2,264,128]{3,2,1,0:T(8,128)(2,1)} %get-tuple-element.59.refs_0_), channel_id=1, source_target_pairs={{0,32},{2,34},{4,36},{6,38},{8,40},{10,42},{12,44},{14,46},{16,48}... | collective-permute-start | bytes 811016 | tf_op jit(solution)/shard_map/ppermute | solution.py:360
  9.9 18.9 %collective-permute-start.4 = (bf16[4,2,256,128]{3,2,1,0:T(8,128)(2,1)}, bf16[4,2,256,128]{3,2,1,0:T(8,128)(2,1)}, u32[]{:S(2)}, u32[]{:S(2)}) collective-permute-start(bf16[4,2,256,128]{3,2,1,0:T(8,128)(2,1)} %get-tuple-element.61), channel_id=1, source_target_pairs={{0,16},{2,18},{4,20},{6,22},{8,24},{10,26},{12,28},{14,30},{16,0},... | collective-permute-start | bytes 1572872 | tf_op jit(solution)/shard_map/ppermute | solution.py:360
  13.6 1.2 copy-start
  14.8 1.2 copy-start.1
  16.0 19.1 %copy-start.2 = (bf16[2,2,264,128]{3,2,1,0:T(8,128)(2,1)S(1)}, bf16[2,2,264,128]{3,2,1,0:T(8,128)(2,1)}, u32[]{:S(2)}) copy-start(bf16[2,2,264,128]{3,2,1,0:T(8,128)(2,1)} %get-tuple-element.70.refs_0_) | copy-start | bytes 811012
  19.3 9.1 %copy-start.6 = (s32[7]{0:T(128)S(1)}, s32[7]{0:T(128)}, u32[]{:S(2)}) copy-start(s32[7]{0:T(128)} %param.12) | copy-start | bytes 88
  19.3 22.3 %collective-permute-start.8 = (bf16[2,1040,128]{2,1,0:T(8,128)(2,1)S(1)}, bf16[2,1040,128]{2,1,0:T(8,128)(2,1)S(1)}, u32[]{:S(2)}, u32[]{:S(2)}) collective-permute-start(bf16[2,1040,128]{2,1,0:T(8,128)(2,1)S(1)} %get-tuple-element.66), channel_id=1, source_target_pairs={{0,1},{1,0},{2,3},{3,2},{4,5},{5,4},{6,7},{7,6},{8,9},{9,8},{10,11... | collective-permute-start | bytes 1597448 | tf_op jit(solution)/shard_map/ppermute | solution.py:371
  19.7 21.4 %collective-permute-start.3 = (bf16[4,2,256,128]{3,2,1,0:T(8,128)(2,1)}, bf16[4,2,256,128]{3,2,1,0:T(8,128)(2,1)}, u32[]{:S(2)}, u32[]{:S(2)}) collective-permute-start(bf16[4,2,256,128]{3,2,1,0:T(8,128)(2,1)} %collective-permute-done.2.refs_3_), channel_id=1, source_target_pairs={{0,12},{2,14},{4,8},{6,10},{8,4},{10,6},{12,0},{14,2},{16,28},{18,... | collective-permute-start | bytes 1572872 | tf_op jit(solution)/shard_map/ppermute | solution.py:360
  21.0 14.2 %collective-permute-start.7 = (bf16[2,2,264,128]{3,2,1,0:T(8,128)(2,1)}, bf16[2,2,264,128]{3,2,1,0:T(8,128)(2,1)}, u32[]{:S(2)}, u32[]{:S(2)}) collective-permute-start(bf16[2,2,264,128]{3,2,1,0:T(8,128)(2,1)} %collective-permute-done.6.refs_7_), channel_id=1, source_target_pairs={{0,192},{2,194},{4,196},{6,198},{8,200},{10,202},{12,204},{14,206}... | collective-permute-start | bytes 811016 | tf_op jit(solution)/shard_map/ppermute | solution.py:360
  24.3 4.1 %copy-start.5 = (s32[2,7]{1,0:T(2,128)S(1)}, s32[2,7]{1,0:T(2,128)}, u32[]{:S(2)}) copy-start(s32[2,7]{1,0:T(2,128)} %param.13) | copy-start | bytes 172
  24.3 14.4 %collective-permute-start.1 = (bf16[4,2,128,128]{3,2,1,0:T(8,128)(2,1)}, bf16[4,2,128,128]{3,2,1,0:T(8,128)(2,1)}, u32[]{:S(2)}, u32[]{:S(2)}) collective-permute-start(bf16[4,2,128,128]{3,2,1,0:T(8,128)(2,1)} %get-tuple-element.62), channel_id=1, source_target_pairs={{2,4},{4,2},{6,8},{8,6},{10,12},{12,10},{14,16},{16,14},{18,20},{2... | collective-permute-start | bytes 786440 | tf_op jit(solution)/shard_map/ppermute | solution.py:367
  28.8 35.3 %collective-permute-start.12 = (bf16[2,1040,128]{2,1,0:T(8,128)(2,1)S(1)}, bf16[2,1040,128]{2,1,0:T(8,128)(2,1)S(1)}, u32[]{:S(2)}, u32[]{:S(2)}) collective-permute-start(bf16[2,1040,128]{2,1,0:T(8,128)(2,1)S(1)} %get-tuple-element.72), channel_id=1, source_target_pairs={{0,1},{1,0},{2,3},{3,2},{4,5},{5,4},{6,7},{7,6},{8,9},{9,8},{10,11... | collective-permute-start | bytes 1597448 | tf_op jit(solution)/shard_map/ppermute | solution.py:371
  35.2 24.4 %collective-permute-start.11 = (bf16[2,2,264,128]{3,2,1,0:T(8,128)(2,1)S(1)}, bf16[2,2,264,128]{3,2,1,0:T(8,128)(2,1)S(1)}, u32[]{:S(2)}, u32[]{:S(2)}) collective-permute-start(bf16[2,2,264,128]{3,2,1,0:T(8,128)(2,1)S(1)} %copy-done.2), channel_id=1, source_target_pairs={{0,128},{2,130},{4,132},{6,134},{8,136},{10,138},{12,140},{14,142}... | collective-permute-start | bytes 811016 | tf_op jit(solution)/shard_map/ppermute | solution.py:360
  38.7 25.4 %collective-permute-start.9 = (bf16[2,2,264,128]{3,2,1,0:T(8,128)(2,1)S(1)}, bf16[2,2,264,128]{3,2,1,0:T(8,128)(2,1)S(1)}, u32[]{:S(2)}, u32[]{:S(2)}) collective-permute-start(bf16[2,2,264,128]{3,2,1,0:T(8,128)(2,1)S(1)} %copy-done.2), channel_id=1, source_target_pairs={{0,32},{2,34},{4,36},{6,38},{8,40},{10,42},{12,44},{14,46},{16,48}... | collective-permute-start | bytes 811016 | tf_op jit(solution)/shard_map/ppermute | solution.py:360
  41.2 23.0 %collective-permute-start.10 = (bf16[2,2,264,128]{3,2,1,0:T(8,128)(2,1)S(1)}, bf16[2,2,264,128]{3,2,1,0:T(8,128)(2,1)S(1)}, u32[]{:S(2)}, u32[]{:S(2)}) collective-permute-start(bf16[2,2,264,128]{3,2,1,0:T(8,128)(2,1)S(1)} %copy-done.2), channel_id=1, source_target_pairs={{0,64},{2,66},{4,68},{6,70},{8,72},{10,74},{12,76},{14,78},{16,80}... | collective-permute-start | bytes 811016 | tf_op jit(solution)/shard_map/ppermute | solution.py:360
  41.6 1.0 copy-start.3
  58.2 22.2 %collective-permute-start.14 = (bf16[2,1024,128]{2,1,0:T(8,128)(2,1)S(1)}, bf16[2,1024,128]{2,1,0:T(8,128)(2,1)S(1)}, u32[]{:S(2)}, u32[]{:S(2)}) collective-permute-start(bf16[2,1024,128]{2,1,0:T(8,128)(2,1)S(1)} %get-tuple-element.85), channel_id=1, source_target_pairs={{0,1},{1,0},{2,3},{3,2},{4,5},{5,4},{6,7},{7,6},{8,9},{9,8},{10,11... | collective-permute-start | bytes 1572872 | tf_op jit(solution)/shard_map/ppermute | solution.py:371
  59.5 20.8 %collective-permute-start.13 = (bf16[2,2,264,128]{3,2,1,0:T(8,128)(2,1)S(1)}, bf16[2,2,264,128]{3,2,1,0:T(8,128)(2,1)S(1)}, u32[]{:S(2)}, u32[]{:S(2)}) collective-permute-start(bf16[2,2,264,128]{3,2,1,0:T(8,128)(2,1)S(1)} %get-tuple-element.84), channel_id=1, source_target_pairs={{0,192},{2,194},{4,196},{6,198},{8,200},{10,202},{12,204},{14,206}... | collective-permute-start | bytes 811016 | tf_op jit(solution)/shard_map/ppermute | solution.py:360
  64.1 16.2 %collective-permute-start.15 = (bf16[2,2,264,128]{3,2,1,0:T(8,128)(2,1)S(1)}, bf16[2,2,264,128]{3,2,1,0:T(8,128)(2,1)S(1)}, u32[]{:S(2)}, u32[]{:S(2)}) collective-permute-start(bf16[2,2,264,128]{3,2,1,0:T(8,128)(2,1)S(1)} %get-tuple-element.86), channel_id=1, source_target_pairs={{0,32},{2,34},{4,36},{6,38},{8,40},{10,42},{12,44},{14,46},{16,48}... | collective-permute-start | bytes 811016 | tf_op jit(solution)/shard_map/ppermute | solution.py:360
  80.4 6.8 %collective-permute-start.20 = (bf16[4,2,256,128]{3,2,1,0:T(8,128)(2,1)S(1)}, bf16[4,2,256,128]{3,2,1,0:T(8,128)(2,1)S(1)}, u32[]{:S(2)}, u32[]{:S(2)}) collective-permute-start(bf16[4,2,256,128]{3,2,1,0:T(8,128)(2,1)S(1)} %get-tuple-element.94), channel_id=1, source_target_pairs={{0,2},{2,0},{4,6},{6,4},{8,10},{10,8},{12,14},{14,12},{16,18},{18,... | collective-permute-start | bytes 1572872 | tf_op jit(solution)/shard_map/ppermute | solution.py:360
  81.3 19.7 %collective-permute-start.18 = (bf16[4,2,256,128]{3,2,1,0:T(8,128)(2,1)S(1)}, bf16[4,2,256,128]{3,2,1,0:T(8,128)(2,1)S(1)}, u32[]{:S(2)}, u32[]{:S(2)}) collective-permute-start(bf16[4,2,256,128]{3,2,1,0:T(8,128)(2,1)S(1)} %get-tuple-element.91), channel_id=1, source_target_pairs={{0,12},{2,14},{4,8},{6,10},{8,4},{10,6},{12,0},{14,2},{16,28},{18,... | collective-permute-start | bytes 1572872 | tf_op jit(solution)/shard_map/ppermute | solution.py:360
  81.9 19.2 %collective-permute-start.19 = (bf16[2,1024,128]{2,1,0:T(8,128)(2,1)S(1)}, bf16[2,1024,128]{2,1,0:T(8,128)(2,1)S(1)}, u32[]{:S(2)}, u32[]{:S(2)}) collective-permute-start(bf16[2,1024,128]{2,1,0:T(8,128)(2,1)S(1)} %get-tuple-element.92), channel_id=1, source_target_pairs={{0,1},{1,0},{2,3},{3,2},{4,5},{5,4},{6,7},{7,6},{8,9},{9,8},{10,11... | collective-permute-start | bytes 1572872 | tf_op jit(solution)/shard_map/ppermute | solution.py:371
  82.8 15.4 %collective-permute-start.16 = (bf16[2,2,264,128]{3,2,1,0:T(8,128)(2,1)S(1)}, bf16[2,2,264,128]{3,2,1,0:T(8,128)(2,1)S(1)}, u32[]{:S(2)}, u32[]{:S(2)}) collective-permute-start(bf16[2,2,264,128]{3,2,1,0:T(8,128)(2,1)S(1)} %get-tuple-element.88), channel_id=1, source_target_pairs={{0,192},{2,194},{4,196},{6,198},{8,200},{10,202},{12,204},{14,206}... | collective-permute-start | bytes 811016 | tf_op jit(solution)/shard_map/ppermute | solution.py:360
  86.9 14.1 %collective-permute-start.17 = (bf16[2,2,264,128]{3,2,1,0:T(8,128)(2,1)S(1)}, bf16[2,2,264,128]{3,2,1,0:T(8,128)(2,1)S(1)}, u32[]{:S(2)}, u32[]{:S(2)}) collective-permute-start(bf16[2,2,264,128]{3,2,1,0:T(8,128)(2,1)S(1)} %add_convert_fusion.2), channel_id=1, source_target_pairs={{0,64},{2,66},{4,68},{6,70},{8,72},{10,74},{12,76},{14,78},{16,80}... | collective-permute-start | bytes 811016 | tf_op jit(solution)/shard_map/ppermute | solution.py:360
  87.2 13.9 %collective-permute-start.21 = (bf16[4,2,128,128]{3,2,1,0:T(8,128)(2,1)S(1)}, bf16[4,2,128,128]{3,2,1,0:T(8,128)(2,1)S(1)}, u32[]{:S(2)}, u32[]{:S(2)}) collective-permute-start(bf16[4,2,128,128]{3,2,1,0:T(8,128)(2,1)S(1)} %get-tuple-element.95), channel_id=1, source_target_pairs={{2,4},{4,2},{6,8},{8,6},{10,12},{12,10},{14,16},{16,14},{18,20},{2... | collective-permute-start | bytes 786440 | tf_op jit(solution)/shard_map/ppermute | solution.py:367
  101.2 22.5 %collective-permute-start.22 = (bf16[4,2,256,128]{3,2,1,0:T(8,128)(2,1)S(1)}, bf16[4,2,256,128]{3,2,1,0:T(8,128)(2,1)S(1)}, u32[]{:S(2)}, u32[]{:S(2)}) collective-permute-start(bf16[4,2,256,128]{3,2,1,0:T(8,128)(2,1)S(1)} %add_convert_fusion), channel_id=1, source_target_pairs={{0,4},{2,6},{4,0},{6,2},{8,12},{10,14},{12,8},{14,10},{16,20},{18,... | collective-permute-start | bytes 1572872 | tf_op jit(solution)/shard_map/ppermute | solution.py:360
  104.0 19.7 %collective-permute-start.23 = (bf16[4,2,256,128]{3,2,1,0:T(8,128)(2,1)S(1)}, bf16[4,2,256,128]{3,2,1,0:T(8,128)(2,1)S(1)}, u32[]{:S(2)}, u32[]{:S(2)}) collective-permute-start(bf16[4,2,256,128]{3,2,1,0:T(8,128)(2,1)S(1)} %get-tuple-element.104), channel_id=1, source_target_pairs={{0,16},{2,18},{4,20},{6,22},{8,24},{10,26},{12,28},{14,30},{16,0},... | collective-permute-start | bytes 1572872 | tf_op jit(solution)/shard_map/ppermute | solution.py:360
  107.7 14.8 %collective-permute-start.24 = (bf16[2,2,264,128]{3,2,1,0:T(8,128)(2,1)S(1)}, bf16[2,2,264,128]{3,2,1,0:T(8,128)(2,1)S(1)}, u32[]{:S(2)}, u32[]{:S(2)}) collective-permute-start(bf16[2,2,264,128]{3,2,1,0:T(8,128)(2,1)S(1)} %get-tuple-element.108), channel_id=1, source_target_pairs={{0,32},{2,34},{4,36},{6,38},{8,40},{10,42},{12,44},{14,46},{16,48}... | collective-permute-start | bytes 811016 | tf_op jit(solution)/shard_map/ppermute | solution.py:360
  110.2 13.5 %collective-permute-start.25 = (bf16[2,2,264,128]{3,2,1,0:T(8,128)(2,1)S(1)}, bf16[2,2,264,128]{3,2,1,0:T(8,128)(2,1)S(1)}, u32[]{:S(2)}, u32[]{:S(2)}) collective-permute-start(bf16[2,2,264,128]{3,2,1,0:T(8,128)(2,1)S(1)} %add_convert_fusion.1), channel_id=1, source_target_pairs={{0,64},{2,66},{4,68},{6,70},{8,72},{10,74},{12,76},{14,78},{16,80}... | collective-permute-start | bytes 811016 | tf_op jit(solution)/shard_map/ppermute | solution.py:360
  (1 other events, 0.7 us)
